TPU v7x, 128 devices: a whole 4x4x4 slice. The times are simulated.
128 devices in a mesh: gy: 32 (over z, y, core), var: 4 (over x).
Axes of the slice: x: 4, y: 4, z: 4, core: 2. Of those that a mesh axis runs over, the one named last changes fastest.
Arguments:
- field: float32 [32, 32, 1024, 128], P('var', None, 'gy')
- factor_x: float32 [32, 16], replicated, may hold values from -1 to 1
- factor_y: float32 [1024, 64], P('gy'), may hold values from -0.1875 to 0.1875
- factor_z: float32 [128, 64], replicated, may hold values from -0.5 to 0.5
- factor_v: float32 [32, 16], replicated, may hold values from -1 to 1
Outputs:
- proj_z: float32 [128, 128], replicated
- proj_v: float32 [32, 32], replicated
- core_rms: float32 [], replicated
All inputs are finite; a program needn't handle non-finite values.
Results may differ from a plain program's by a relative error of at most 0.0003.
Values sent between devices are 32-bit elements; how exact they have to be, the bound alone decides.
No kernel may reach another device: no remote copies, remote signals or barrier semaphores. Data moves between devices by JAX's collectives and lax.ppermute only.
A program may use at most 192 MiB of HBM per device.

v0:
```python
import jax
import jax.numpy as jnp
from jax import lax
from jax.sharding import PartitionSpec as P

precise = lax.Precision.HIGHEST


def orth(mat):
    gram = jnp.dot(mat.T, mat, precision=precise)
    lower = jnp.linalg.cholesky(gram)
    return jax.scipy.linalg.solve_triangular(lower, mat.T, lower=True).T


def total_core(local_part):
    return lax.psum(local_part, ("gy", "var"))


def per_device(field, factor_x, factor_y, factor_z, factor_v):
    var_rows = field.shape[0]
    var_start = lax.axis_index("var") * var_rows
    local_v = lax.dynamic_slice_in_dim(factor_v, var_start, var_rows, 0)
    along_x = jnp.einsum("vxyz,xa->vayz", field, factor_x, precision=precise)
    partial_value = jnp.einsum("vayz,yb->vabz", along_x, factor_y, precision=precise)
    wide_z = jnp.einsum("vabz,vc->cabz", partial_value, local_v, precision=precise)
    fibres = lax.psum_scatter(wide_z, ("gy", "var"), scatter_dimension=3, tiled=True)
    z_count = fibres.shape[3]
    z_start = lax.axis_index(("gy", "var")) * z_count
    local_z = lax.dynamic_slice_in_dim(factor_z, z_start, z_count, 0)
    small_core = total_core(jnp.einsum("cabz,zr->cabr", fibres, local_z, precision=precise))
    rows_z = jnp.einsum("cabz,cabr->zr", fibres, small_core, precision=precise)
    raw_z = lax.all_gather(rows_z, ("gy", "var"), axis=0, tiled=True)
    new_z = orth(raw_z)
    proj_z = jnp.dot(new_z, new_z.T, precision=precise)
    wide_v = jnp.einsum("vabz,zr->vabr", partial_value, new_z, precision=precise)
    flat_v = wide_v.reshape(var_rows, -1)
    summed_v = lax.psum(flat_v, "gy")
    every_v = lax.all_gather(summed_v, "var", axis=0, tiled=True)
    gram_v = jnp.dot(every_v, every_v.T, precision=precise)
    new_v = orth(jnp.dot(gram_v, factor_v, precision=precise))
    proj_v = jnp.dot(new_v, new_v.T, precision=precise)
    core = jnp.dot(new_v.T, every_v, precision=precise)
    core_rms = jnp.sqrt(jnp.mean(core * core))
    return (proj_z, proj_v, core_rms)


def solution(mesh):
    in_specs = (P("var", None, "gy", None), P(), P("gy", None), P(), P())
    out_specs = (P(), P(), P())
    return jax.shard_map(
        per_device, mesh=mesh, in_specs=in_specs, out_specs=out_specs, check_vma=False
    )
```

profile of v0, /device:TPU:1, one launch (start us, length us, event | category | flops | bytes accessed | tf_op | source)
XLA Modules:
  0.0 1346.6 jit_solution(12369558590492828368)
XLA Ops:
  7.2 0.0 copy-start
  7.2 0.0 copy-start.4
  7.2 0.0 reduce-scatter.2.cloned.1.call-start
  7.2 6.9 fusion.5
  14.1 0.0 copy-done.4
  14.1 4.1 convolution_bitcast_fusion
  18.2 0.0 copy-start.1
  18.2 2.0 copy-done.1
  20.2 0.0 copy-start.3
  20.2 5.2 copy.21
  25.4 0.0 copy-done.3
  25.4 122.6 %fusion.25 = f32[16,131072]{0,1} fusion(f32[8,131072]{1,0:T(8,128)} %bitcast.65, f32[32,16]{0,1:T(8,128)S(1)} %copy-done.3, s32[]{:T(128)S(6)} %select_n.14), kind=kOutput, calls=%fused_computation.35 | convolution fusion | flops 201326592 | bytes 71305216
  148.0 42.6 %copy.22 = f32[16,16,64,128]{2,1,0,3:T(8,128)} copy(f32[16,16,64,128]{0,3,2,1:T(8,128)} %bitcast.7) | data formatting | bytes 16777216 | tf_op jit(solution)/shard_map/vabz,vc->cabz/dot_general | solution.py:25
  190.7 0.0 reduce-scatter.2.cloned.1.call-update
  190.7 0.0 all-reduce.4.cloned.1.call-start
  190.8 0.0 copy-done
  190.8 0.2 dynamic-slice_reduce_fusion
  190.9 668.2 %reduce-scatter.2.cloned.1.call-done = f32[16,16,64,1]{2,1,0,3:T(8,128)} async-done(((f32[16,16,64,128]{2,1,0,3:T(8,128)}), f32[16,16,64,1]{2,1,0,3:T(8,128)}) %reduce-scatter.2.cloned.1.call-update) | async-done | bytes 65552 | tf_op jit(solution)/shard_map/reduce_scatter | solution.py:26
  859.1 5.5 broadcast_multiply_fusion
  864.6 0.0 copy-start.2
  864.6 0.0 all-reduce.4.cloned.1.call-update
  864.6 0.0 all-reduce.6.cloned.1.call-start
  864.7 165.4 %all-reduce.4.cloned.1.call-done = f32[16,16,64,64]{3,2,1,0:T(8,128)} async-done(((f32[16,16,64,64]{3,2,1,0:T(8,128)}), f32[16,16,64,64]{3,2,1,0:T(8,128)}) %all-reduce.4.cloned.1.call-update) | async-done | bytes 4194320 | tf_op jit(solution)/shard_map/psum | solution.py:16
  1030.1 0.0 copy-done.2
  1030.1 6.6 fusion.9
  1036.8 0.3 dynamic-update-slice.6
  1037.0 64.0 %all-reduce = f32[8192]{0:T(1024)S(1)} all-reduce(f32[8192]{0:T(1024)S(1)} %dynamic-update-slice.6), channel_id=2, replica_groups=mesh['gy'=32,'var'=4] {'gy','var'}, use_global_device_ids=true, to_apply=%add | all-reduce | flops 8192 | bytes 65536
  1101.1 0.1 reshape.39
  1101.2 0.3 fusion.28
  1101.4 0.1 copy.23
  1101.5 5.8 cholesky.29
  1107.4 0.6 compare_reduce_fusion.1
  1108.0 0.7 fusion.13
  1108.7 4.9 custom-call.14
  1113.6 0.3 fusion.16
  1113.9 6.6 fusion.14
  1120.5 4.7 reshape.38
  1125.2 0.0 all-reduce.6.cloned.1.call-update
  1125.2 0.0 all-gather.3.cloned.1.call-start
  1125.3 104.6 %all-reduce.6.cloned.1.call-done = f32[8,65536]{1,0:T(8,128)} async-done(((f32[8,65536]{1,0:T(8,128)}), f32[8,65536]{1,0:T(8,128)}) %all-reduce.6.cloned.1.call-update) | async-done | bytes 2097168 | tf_op jit(solution)/shard_map/psum | solution.py:37
  1229.9 0.0 all-gather.3.cloned.1.call-update
  1229.9 0.9 fusion.29
  1230.8 83.4 %all-gather.3.cloned.1.call-done = f32[32,65536]{1,0:T(8,128)} async-done(((f32[8,65536]{1,0:T(8,128)}), f32[32,65536]{1,0:T(8,128)}) %all-gather.3.cloned.1.call-update) | async-done | bytes 8388624 | tf_op jit(solution)/shard_map/all_gather | solution.py:38
  1314.2 10.7 fusion.30
  1324.9 0.1 fusion.31
  1325.0 0.1 fusion.32
  1325.2 0.1 copy.24
  1325.2 1.5 cholesky.61
  1326.7 0.6 compare_reduce_fusion
  1327.4 0.6 fusion.20
  1328.0 1.2 custom-call.15
  1329.3 0.2 fusion.22
  1329.5 0.8 fusion.33
  1330.3 7.5 fusion.8
  (5 shorter events, 0.1 us)
Async XLA Ops:
  7.2 183.6 %copy-start = (f32[128,64]{0,1:T(8,128)S(1)}, f32[128,64]{0,1:T(8,128)}, u32[]{:S(2)}) copy-start(f32[128,64]{0,1:T(8,128)} %param.8) | copy-start | bytes 98308
  7.2 6.9 copy-start.4
  7.2 851.9 %reduce-scatter.2.cloned.1.call-start = ((), (), s32[]{:S(2)}) async-start(), calls=%async_computation.1 | async-start | bytes 16908288 | tf_op jit(solution)/shard_map/reduce_scatter | solution.py:26
  18.2 2.0 copy-start.1
  20.2 5.3 copy-start.3
  190.7 839.4 %all-reduce.4.cloned.1.call-start = ((), (), s32[]{:S(2)}) async-start(), calls=%async_computation.2 | async-start | bytes 16777216 | tf_op jit(solution)/shard_map/psum | solution.py:16
  864.6 165.5 %copy-start.2 = (f32[16,16,64,1]{2,1,0,3:T(8,128)S(1)}, f32[16,16,64,1]{2,1,0,3:T(8,128)}, u32[]{:S(2)}) copy-start(f32[16,16,64,1]{2,1,0,3:T(8,128)} %reduce-scatter.2.cloned.1.call-done) | copy-start | bytes 196612
  864.6 365.3 %all-reduce.6.cloned.1.call-start = ((), (), s32[]{:S(2)}) async-start(), calls=%async_computation.3 | async-start | bytes 4194304 | tf_op jit(solution)/shard_map/psum | solution.py:37
  1125.2 189.0 %all-gather.3.cloned.1.call-start = ((), (), s32[]{:S(2)}) async-start(), calls=%async_computation.4 | async-start | bytes 10485760 | tf_op jit(solution)/shard_map/all_gather | solution.py:38
Sparse Core Ops, SparseCore 0:
  190.8 668.2 reduce-scatter.1
  864.7 165.3 all-reduce.3
  1125.3 104.5 all-reduce.5
  1231.5 82.6 all-gather.2
where the time goes:
time: 1350 us
  waiting for transfers between devices  1020 us (76%)
  matrix products  168 us (12%)
  blocking collectives  64 us (5%)
  local copies, waits for them, and re-layouts  55.3 us (4%)
  other arithmetic  21.6 us (2%)
  between operations  16.2 us (1%)
    reduce_scatter x1, waiting for transfers between devices, per_device(): lax.psum_scatter(wide_z, ('gy', 'var'), scatter_dimension=3, tiled=True)  668 us
    psum x1, waiting for transfers between devices, total_core(): return lax.psum(local_part, ('gy', 'var'))  165 us
    unnamed x1, matrix products  123 us
    psum x1, waiting for transfers between devices, per_device(): summed_v = lax.psum(flat_v, 'gy')  105 us
    all_gather x1, waiting for transfers between devices, per_device(): every_v = lax.all_gather(summed_v, 'var', axis=0, tiled=True)  83.4 us
    unnamed x1, blocking collectives  64 us
    dot_general x1, local copies, waits for them, and re-layouts, per_device(): jnp.einsum('vabz,vc->cabz', partial_value, local_v, precision=precise)  42.6 us
  transfers between devices with their start and end apart: 4, of which 4 were waited for; matrix products, arithmetic and copies ran while one was open for 0% of the time, Pallas kernels for 0%

commit v1 on v0

v1 whole, which is shorter than its diff:
```python
import jax
import jax.numpy as jnp
from jax import lax
from jax.sharding import Mesh, PartitionSpec as P

precise = lax.Precision.HIGHEST


def orth(mat):
    gram = jnp.dot(mat.T, mat, precision=precise)
    lower = jnp.linalg.cholesky(gram)
    return jax.scipy.linalg.solve_triangular(lower, mat.T, lower=True).T


def shift(value, axis, step):
    return lax.ppermute(value, axis, [(i, (i + step) % 4) for i in range(4)])


def from_all(value, axes, count):
    copies = jnp.broadcast_to(value[None], (count,) + value.shape)
    return lax.all_to_all(copies, axes, 0, 0, tiled=True)


def per_device(field, factor_x, factor_y, factor_z, factor_v):
    core = lax.axis_index("c")
    swap = [(0, 1), (1, 0)]
    other_y = lax.ppermute(factor_y, "c", swap)
    along_x = jnp.einsum("vxyz,xa->avyz", field, factor_x, precision=precise)
    keep = lax.dynamic_slice_in_dim(along_x, core * 8, 8, 0)
    send = lax.dynamic_slice_in_dim(along_x, (1 - core) * 8, 8, 0)
    got = lax.ppermute(send, "c", swap)
    both = jnp.concatenate([keep, got], axis=2)
    both_y = jnp.concatenate([factor_y, other_y], axis=0)
    part = jnp.einsum("avyz,yb->avbz", both, both_y, precision=precise)
    part = part.reshape(8, 8, 8, 8, 128).transpose(0, 2, 1, 3, 4).reshape(64, 8, 8, 128)
    parts = lax.all_to_all(part, ("z", "y", "x"), 0, 0, tiled=True)
    block = parts.reshape(16, 4, 8, 8, 128).sum(0).reshape(32, 8, 128)

    wide_z = jnp.einsum("vbz,vc->cbz", block, factor_v, precision=precise).reshape(128, 128)
    small_core = jnp.dot(wide_z, factor_z, precision=precise)
    raw = jnp.dot(small_core.T, wide_z, precision=precise)
    raw = raw + lax.ppermute(raw, "c", swap)
    raw = from_all(raw, ("z", "y"), 16).sum(0)
    raw = raw + shift(raw, "x", 1) + (shift(raw, "x", 2) + shift(raw, "x", 3))
    new_z = orth(raw.T)
    proj_z = jnp.dot(new_z, new_z.T, precision=precise)

    wide_v = jnp.einsum("vbz,zr->bvr", block, new_z, precision=precise)
    gram_v = jnp.einsum("bvr,bwr->vw", wide_v, wide_v, precision=precise)
    gram_v = from_all(gram_v.reshape(8, 128), ("z", "y", "c", "x"), 128).sum(0).reshape(32, 32)
    new_v = orth(jnp.dot(gram_v, factor_v, precision=precise))
    proj_v = jnp.dot(new_v, new_v.T, precision=precise)
    total = jnp.sum(new_v * jnp.dot(gram_v, new_v, precision=precise))
    core_rms = jnp.sqrt(total / (16 * 16 * 64 * 64))
    return (proj_z, proj_v, core_rms)


def solution(mesh):
    fine = Mesh(mesh.devices.reshape(4, 4, 2, 4), ("z", "y", "c", "x"))
    rows = ("z", "y", "c")
    in_specs = (P("x", None, rows, None), P(), P(rows, None), P(), P())
    out_specs = (P(), P(), P())
    return jax.shard_map(
        per_device, mesh=fine, in_specs=in_specs, out_specs=out_specs, check_vma=False
    )
```

time: 1350 us -> 123 us (0.09)
  waiting for transfers between devices: 1020 us -> 16.8 us
  matrix products: 168 us -> 13.6 us
  local copies, waits for them, and re-layouts: 55.3 us -> 2.25 us
  starting transfers between devices: 0.16 us -> 16.6 us
  between operations: 16.2 us -> 2.65 us
    reduce_scatter x1 -> x0, waiting for transfers between devices: 668 us -> none  [per_device(): lax.psum_scatter(wide_z, ('gy', 'var'), scatter_dimension=3, tiled=True)]
    psum x2 -> x0, waiting for transfers between devices: 270 us -> none  [the longest x1 165 us: total_core(): return lax.psum(local_part, ('gy', 'var'))]
    unnamed x1 -> x0, matrix products: 123 us -> none
    all_gather x1 -> x0, waiting for transfers between devices: 83.4 us -> none  [per_device(): every_v = lax.all_gather(summed_v, 'var', axis=0, tiled=True)]
    unnamed x1 -> x0, blocking collectives: 64 us -> none
    all_to_all x0 -> x2, blocking collectives: none -> 53.6 us  [the longest x1 40 us: per_device(): parts = lax.all_to_all(part, ('z', 'y', 'x'), 0, 0, tiled=True)]
    dot_general x1 -> x0, local copies, waits for them, and re-layouts: 42.6 us -> none  [per_device(): jnp.einsum('vabz,vc->cabz', partial_value, local_v, precision=precise)]
    dot_general x6 -> x8, matrix products: 42.3 us -> 11 us  [the longest x1 6.86 us: per_device(): along_x = jnp.einsum('vxyz,xa->avyz', field, factor_x, precision=precise)]
  transfers between devices with their start and end apart: 4 -> 7, of which waited for: 4 -> 6; matrix products, arithmetic and copies ran while one was open for 0% -> 1% of each run, Pallas kernels for 0% -> 0%
where the time goes in v1:
time: 123 us; the launch traced here: 122 us
  blocking collectives  53.6 us (44%)
  waiting for transfers between devices  16.8 us (14%)
  starting transfers between devices  16.6 us (13%)
  other arithmetic  16.6 us (13%)
  matrix products  13.6 us (11%)
  between operations  2.65 us (2%)
  local copies, waits for them, and re-layouts  2.25 us (2%)
    all_to_all x1, blocking collectives, per_device(): parts = lax.all_to_all(part, ('z', 'y', 'x'), 0, 0, tiled=True)  40 us
    all_to_all x1, blocking collectives, from_all(): return lax.all_to_all(copies, axes, 0, 0, tiled=True)  13.6 us
    all_to_all x1, waiting for transfers between devices, from_all(): return lax.all_to_all(copies, axes, 0, 0, tiled=True)  13.1 us
    another operation x6, other arithmetic, orth(): lower = jnp.linalg.cholesky(gram)  8.67 us
    all_to_all x1, starting transfers between devices, from_all(): return lax.all_to_all(copies, axes, 0, 0, tiled=True)  8.6 us
    another operation x4, other arithmetic, orth(): return jax.scipy.linalg.solve_triangular(lower, mat.T, lower=True).T  7.42 us
    dot_general x1, matrix products, per_device(): along_x = jnp.einsum('vxyz,xa->avyz', field, factor_x, precision=precise)  6.86 us
    ppermute x3, starting transfers between devices, shift(): return lax.ppermute(value, axis, [(i, (i + step) % 4) for i in range(4)])  3.85 us
  transfers between devices with their start and end apart: 7, of which 6 were waited for; matrix products, arithmetic and copies ran while one was open for 1% of the time, Pallas kernels for 0%

profile of v1, /device:TPU:1, one launch (start us, length us, event | category | flops | bytes accessed | tf_op | source)
XLA Modules:
  0.0 122.1 jit_solution(7966943732230657149)
XLA Ops:
  0.6 0.0 copy-start
  0.7 6.9 %fusion = f32[16,8,32,128]{3,0,2,1:T(8,128)S(1)} fusion(f32[8,32,32,128]{3,2,1,0:T(8,128)} %param.5, f32[32,16]{0,1:T(8,128)} %param.6), kind=kOutput, calls=%fused_computation | convolution fusion | flops 201326592 | bytes 6293504 | tf_op jit(solution)/shard_map/vxyz,xa->avyz/dot_general | solution.py:28
  7.5 0.0 copy-start.2
  7.5 0.1 constant_dynamic-slice_fusion.1
  7.7 1.5 %collective-permute-start.1 = (f32[8,8,32,128]{3,0,2,1:T(8,128)S(1)}, f32[8,8,32,128]{3,0,2,1:T(8,128)S(1)}, u32[]{:S(2)}, u32[]{:S(2)}) collective-permute-start(f32[8,8,32,128]{3,0,2,1:T(8,128)S(1)} %get-tuple-element.4), channel_id=1, source_target_pairs={{0,4},{4,0},{1,5},{5,1},{2,6},{6,2},{3,7},{7,3},{8,12},{12,8},{9,1... | collective-permute-start | bytes 3145736 | tf_op jit(solution)/shard_map/ppermute | solution.py:31
  9.2 0.0 copy-done.2
  9.2 0.1 copy.33
  9.3 0.5 collective-permute-start
  9.8 1.7 %collective-permute-done.1 = f32[8,8,32,128]{3,0,2,1:T(8,128)S(1)} collective-permute-done((f32[8,8,32,128]{3,0,2,1:T(8,128)S(1)}, f32[8,8,32,128]{3,0,2,1:T(8,128)S(1)}, u32[]{:S(2)}, u32[]{:S(2)}) %collective-permute-start.1) | collective-permute-done | bytes 1048608 | tf_op jit(solution)/shard_map/ppermute | solution.py:31
  11.5 0.1 pad_maximum_fusion
  11.6 0.0 collective-permute-done
  11.6 2.2 %fusion.4 = f32[8,8,8,8,128]{4,3,2,1,0:T(8,128)S(1)} fusion(f32[8,8,64,128]{3,0,2,1:T(8,128)S(1)} %pad_maximum_fusion, f32[32,64]{0,1:T(8,128)S(1)} %collective-permute-done, f32[32,64]{0,1:T(8,128)S(1)} %copy.33), kind=kOutput, calls=%fused_computation.5 | convolution fusion | flops 402657280 | bytes 4210688 | tf_op jit(solution)/shard_map/avyz,yb->avbz/dot_general | solution.py:34
  13.8 0.3 copy.36
  14.1 40.0 %all_to_all.15 = f32[64,8,8,128]{3,2,1,0:T(8,128)S(1)} all-to-all(f32[64,8,8,128]{3,2,1,0:T(8,128)S(1)} %bitcast.74), channel_id=1, replica_groups=mesh['z'=4,'y'=4,'c'=2,'x'=4] {'z','y','x'}, dimensions={0} | all-to-all | bytes 4194304 | tf_op jit(solution)/shard_map/all_to_all | solution.py:36
  54.1 0.0 copy-start.1
  54.1 0.1 reduce_sum.36
  54.2 0.6 copy-done.1
  54.8 0.2 convolution_bitcast_fusion.1
  55.0 0.0 copy-done
  55.0 0.2 fusion.12
  55.3 0.2 fusion.10
  55.5 2.2 %collective-permute-start.2 = (f32[64,128]{1,0:T(8,128)S(1)}, f32[64,128]{1,0:T(8,128)S(1)}, u32[]{:S(2)}, u32[]{:S(2)}) collective-permute-start(f32[64,128]{1,0:T(8,128)S(1)} %fusion.10), channel_id=1, source_target_pairs={{0,4},{4,0},{1,5},{5,1},{2,6},{6,2},{3,7},{7,3},{8,12},{12,8},{9,1... | collective-permute-start | bytes 98312 | tf_op jit(solution)/shard_map/ppermute | solution.py:42
  57.6 0.9 collective-permute-done.2
  58.5 13.6 %all_to_all.16 = f32[16,64,128]{2,1,0:T(8,128)S(1)} all-to-all(f32[16,64,128]{2,1,0:T(8,128)S(1)} %broadcast_in_dim.9), channel_id=1, replica_groups=mesh['z'=4,'y'=4,'c'=2,'x'=4] {'z','y'}, dimensions={0} | all-to-all | bytes 1048576 | tf_op jit(solution)/shard_map/all_to_all | solution.py:21
  72.2 0.2 collective-permute-start.3
  72.4 2.1 %collective-permute-start.4 = (f32[64,128]{1,0:T(8,128)S(1)}, f32[64,128]{1,0:T(8,128)S(1)}, u32[]{:S(2)}, u32[]{:S(2)}) collective-permute-start(f32[64,128]{1,0:T(8,128)S(1)} %reduce_sum.37), channel_id=1, source_target_pairs={{0,2},{1,3},{2,0},{3,1},{4,6},{5,7},{6,4},{7,5},{8,10},{9,11},{10,... | collective-permute-start | bytes 98312 | tf_op jit(solution)/shard_map/ppermute | solution.py:16
  74.5 1.6 %collective-permute-start.5 = (f32[64,128]{1,0:T(8,128)S(1)}, f32[64,128]{1,0:T(8,128)S(1)}, u32[]{:S(2)}, u32[]{:S(2)}) collective-permute-start(f32[64,128]{1,0:T(8,128)S(1)} %reduce_sum.37), channel_id=1, source_target_pairs={{0,3},{1,0},{2,1},{3,2},{4,7},{5,4},{6,5},{7,6},{8,11},{9,8},{10,9... | collective-permute-start | bytes 98312 | tf_op jit(solution)/shard_map/ppermute | solution.py:16
  76.1 0.2 collective-permute-done.3
  76.2 0.4 collective-permute-done.4
  76.7 0.6 collective-permute-done.5
  77.3 0.2 fusion.30
  77.4 0.1 copy.39
  77.5 5.8 %cholesky.29 = f32[64,64]{1,0:T(8,128)S(1)} custom-call(f32[64,64]{1,0:T(8,128)S(1)} %fusion.22), custom_call_target="Cholesky" | custom-call | tf_op jit(solution)/shard_map/jit(cholesky)/cholesky | solution.py:11
  83.4 0.6 compare_reduce_fusion.1
  84.1 0.7 fusion.16
  84.7 4.9 %custom-call.14 = f32[1,64,64]{1,2,0:T(8,128)S(1)} custom-call(f32[1,64,64]{2,1,0:T(8,128)S(1)} %fusion.16), custom_call_target="InvertDiagBlocksLowerTriangular" | custom-call | tf_op jit(solution)/shard_map/jit(_solve_triangular)/triangular_solve | solution.py:12
  89.6 0.3 fusion.20
  89.9 0.3 convolution_bitcast_fusion
  90.2 0.2 convolution_bitcast_fusion.2
  90.4 0.1 broadcast_in_dim.18
  90.5 0.8 broadcast_in_dim.19
  91.3 8.6 %all-to-all-start.2 = ((f32[128,8,128]{2,1,0:T(8,128)}), f32[128,8,128]{2,1,0:T(8,128)S(1)}, u32[]{:S(2)}, u32[]{:S(2)}) async-start(f32[128,8,128]{2,1,0:T(8,128)} %broadcast_in_dim.19), calls=%async_computation.2 | async-start | bytes 1048576 | tf_op jit(solution)/shard_map/all_to_all | solution.py:21
  99.9 0.9 fusion.31
  100.8 13.1 %all-to-all-done.2 = f32[128,8,128]{2,1,0:T(8,128)S(1)} async-done(((f32[128,8,128]{2,1,0:T(8,128)}), f32[128,8,128]{2,1,0:T(8,128)S(1)}, u32[]{:S(2)}, u32[]{:S(2)}) %all-to-all-start.2) | async-done | bytes 524320 | tf_op jit(solution)/shard_map/all_to_all | solution.py:21
  113.9 0.1 reduce_sum.38
  114.0 0.1 reshape.50
  114.1 0.1 fusion.32
  114.2 0.1 fusion.33
  114.4 0.1 copy.41
  114.5 1.5 %cholesky.61 = f32[16,16]{1,0:T(8,128)S(1)} custom-call(f32[16,16]{1,0:T(8,128)S(1)} %fusion.27), custom_call_target="Cholesky" | custom-call | tf_op jit(solution)/shard_map/jit(cholesky)/cholesky | solution.py:11
  116.0 0.6 compare_reduce_fusion
  116.6 0.6 fusion.23
  117.3 1.2 %custom-call.15 = f32[1,16,16]{1,2,0:T(8,128)S(1)} custom-call(f32[1,16,16]{2,1,0:T(8,128)S(1)} %fusion.23), custom_call_target="InvertDiagBlocksLowerTriangular" | custom-call | tf_op jit(solution)/shard_map/jit(_solve_triangular)/triangular_solve | solution.py:12
  118.5 0.2 fusion.25
  118.7 0.8 fusion.7
  119.5 0.8 fusion.34
  (8 shorter events, 0.2 us)
Async XLA Ops:
  0.6 54.4 %copy-start = (f32[128,64]{0,1:T(8,128)S(1)}, f32[128,64]{0,1:T(8,128)}, u32[]{:S(2)}) copy-start(f32[128,64]{0,1:T(8,128)} %param.8) | copy-start | bytes 98308
  7.5 1.7 %copy-start.2 = (f32[32,64]{1,0:T(8,128)S(1)}, f32[32,64]{1,0:T(8,128)}, u32[]{:S(2)}) copy-start(f32[32,64]{1,0:T(8,128)} %param.7) | copy-start | bytes 24580
  7.7 3.8 %collective-permute-start.1 = (f32[8,8,32,128]{3,0,2,1:T(8,128)S(1)}, f32[8,8,32,128]{3,0,2,1:T(8,128)S(1)}, u32[]{:S(2)}, u32[]{:S(2)}) collective-permute-start(f32[8,8,32,128]{3,0,2,1:T(8,128)S(1)} %get-tuple-element.4), channel_id=1, source_target_pairs={{0,4},{4,0},{1,5},{5,1},{2,6},{6,2},{3,7},{7,3},{8,12},{12,8},{9,1... | collective-permute-start | bytes 3145736 | tf_op jit(solution)/shard_map/ppermute | solution.py:31
  9.3 2.4 %collective-permute-start = (f32[32,64]{0,1:T(8,128)S(1)}, f32[32,64]{0,1:T(8,128)S(1)}, u32[]{:S(2)}, u32[]{:S(2)}) collective-permute-start(f32[32,64]{0,1:T(8,128)S(1)} %copy.33), channel_id=1, source_target_pairs={{0,4},{4,0},{1,5},{5,1},{2,6},{6,2},{3,7},{7,3},{8,12},{12,8},{9,1... | collective-permute-start | bytes 24584 | tf_op jit(solution)/shard_map/ppermute | solution.py:27
  54.1 0.7 copy-start.1
  55.5 3.0 %collective-permute-start.2 = (f32[64,128]{1,0:T(8,128)S(1)}, f32[64,128]{1,0:T(8,128)S(1)}, u32[]{:S(2)}, u32[]{:S(2)}) collective-permute-start(f32[64,128]{1,0:T(8,128)S(1)} %fusion.10), channel_id=1, source_target_pairs={{0,4},{4,0},{1,5},{5,1},{2,6},{6,2},{3,7},{7,3},{8,12},{12,8},{9,1... | collective-permute-start | bytes 98312 | tf_op jit(solution)/shard_map/ppermute | solution.py:42
  72.2 4.0 %collective-permute-start.3 = (f32[64,128]{1,0:T(8,128)S(1)}, f32[64,128]{1,0:T(8,128)S(1)}, u32[]{:S(2)}, u32[]{:S(2)}) collective-permute-start(f32[64,128]{1,0:T(8,128)S(1)} %reduce_sum.37), channel_id=1, source_target_pairs={{0,1},{1,2},{2,3},{3,0},{4,5},{5,6},{6,7},{7,4},{8,9},{9,10},{10,1... | collective-permute-start | bytes 98312 | tf_op jit(solution)/shard_map/ppermute | solution.py:16
  72.4 4.3 %collective-permute-start.4 = (f32[64,128]{1,0:T(8,128)S(1)}, f32[64,128]{1,0:T(8,128)S(1)}, u32[]{:S(2)}, u32[]{:S(2)}) collective-permute-start(f32[64,128]{1,0:T(8,128)S(1)} %reduce_sum.37), channel_id=1, source_target_pairs={{0,2},{1,3},{2,0},{3,1},{4,6},{5,7},{6,4},{7,5},{8,10},{9,11},{10,... | collective-permute-start | bytes 98312 | tf_op jit(solution)/shard_map/ppermute | solution.py:16
  74.5 2.8 %collective-permute-start.5 = (f32[64,128]{1,0:T(8,128)S(1)}, f32[64,128]{1,0:T(8,128)S(1)}, u32[]{:S(2)}, u32[]{:S(2)}) collective-permute-start(f32[64,128]{1,0:T(8,128)S(1)} %reduce_sum.37), channel_id=1, source_target_pairs={{0,3},{1,0},{2,1},{3,2},{4,7},{5,4},{6,5},{7,6},{8,11},{9,8},{10,9... | collective-permute-start | bytes 98312 | tf_op jit(solution)/shard_map/ppermute | solution.py:16
  91.3 22.6 %all-to-all-start.2 = ((f32[128,8,128]{2,1,0:T(8,128)}), f32[128,8,128]{2,1,0:T(8,128)S(1)}, u32[]{:S(2)}, u32[]{:S(2)}) async-start(f32[128,8,128]{2,1,0:T(8,128)} %broadcast_in_dim.19), calls=%async_computation.2 | async-start | bytes 1048576 | tf_op jit(solution)/shard_map/all_to_all | solution.py:21

commit v2 on v1

--- a/solution.py
+++ b/solution.py
@@ -10,10 +10,6 @@
     gram = jnp.dot(mat.T, mat, precision=precise)
     lower = jnp.linalg.cholesky(gram)
     return jax.scipy.linalg.solve_triangular(lower, mat.T, lower=True).T
-
-
-def shift(value, axis, step):
-    return lax.ppermute(value, axis, [(i, (i + step) % 4) for i in range(4)])
 
 
 def from_all(value, axes, count):
@@ -32,22 +28,21 @@
     both = jnp.concatenate([keep, got], axis=2)
     both_y = jnp.concatenate([factor_y, other_y], axis=0)
     part = jnp.einsum("avyz,yb->avbz", both, both_y, precision=precise)
-    part = part.reshape(8, 8, 8, 8, 128).transpose(0, 2, 1, 3, 4).reshape(64, 8, 8, 128)
-    parts = lax.all_to_all(part, ("z", "y", "x"), 0, 0, tiled=True)
-    block = parts.reshape(16, 4, 8, 8, 128).sum(0).reshape(32, 8, 128)
+    part = part.reshape(8, 8, 2, 32, 128).transpose(0, 2, 1, 3, 4).reshape(16, 8, 32, 128)
+    parts = lax.all_to_all(part, ("z", "y"), 0, 0, tiled=True)
+    block = from_all(parts.sum(0), "x", 4).reshape(32, 32, 128)
 
-    wide_z = jnp.einsum("vbz,vc->cbz", block, factor_v, precision=precise).reshape(128, 128)
+    wide_z = jnp.einsum("vbz,vc->cbz", block, factor_v, precision=precise).reshape(512, 128)
     small_core = jnp.dot(wide_z, factor_z, precision=precise)
     raw = jnp.dot(small_core.T, wide_z, precision=precise)
     raw = raw + lax.ppermute(raw, "c", swap)
     raw = from_all(raw, ("z", "y"), 16).sum(0)
-    raw = raw + shift(raw, "x", 1) + (shift(raw, "x", 2) + shift(raw, "x", 3))
     new_z = orth(raw.T)
     proj_z = jnp.dot(new_z, new_z.T, precision=precise)
 
     wide_v = jnp.einsum("vbz,zr->bvr", block, new_z, precision=precise)
     gram_v = jnp.einsum("bvr,bwr->vw", wide_v, wide_v, precision=precise)
-    gram_v = from_all(gram_v.reshape(8, 128), ("z", "y", "c", "x"), 128).sum(0).reshape(32, 32)
+    gram_v = from_all(gram_v.reshape(8, 128), ("z", "y", "c"), 32).sum(0).reshape(32, 32)
     new_v = orth(jnp.dot(gram_v, factor_v, precision=precise))
     proj_v = jnp.dot(new_v, new_v.T, precision=precise)
     total = jnp.sum(new_v * jnp.dot(gram_v, new_v, precision=precise))

time: 123 us -> 116 us (0.943)
  waiting for transfers between devices: 16.8 us -> 9.37 us
  blocking collectives: 53.6 us -> 60.2 us
  starting transfers between devices: 16.6 us -> 10.6 us
    all_to_all x1 -> x2, blocking collectives: 13.6 us -> 25 us  [from_all(): return lax.all_to_all(copies, axes, 0, 0, tiled=True)]
    all_to_all x1, waiting for transfers between devices: 13.1 us -> 6.82 us  [from_all(): return lax.all_to_all(copies, axes, 0, 0, tiled=True)]
    all_to_all x1, blocking collectives: 40 us -> 35.2 us  [per_device(): parts = lax.all_to_all(part, ('z', 'y'), 0, 0, tiled=True)]
    ppermute x3 -> x0, starting transfers between devices: 3.85 us -> none  [shift(): return lax.ppermute(value, axis, [(i, (i + step) % 4) for i in range(4)])]
    all_to_all x1, starting transfers between devices: 8.6 us -> 5.25 us  [from_all(): return lax.all_to_all(copies, axes, 0, 0, tiled=True)]
  transfers between devices with their start and end apart: 7 -> 4, of which waited for: 6 -> 3; matrix products, arithmetic and copies ran while one was open for 1% -> 1% of each run, Pallas kernels for 0% -> 0%
where the time goes in v2:
time: 116 us
  blocking collectives  60.2 us (52%)
  other arithmetic  16.7 us (14%)
  matrix products  14.7 us (13%)
  starting transfers between devices  10.6 us (9%)
  waiting for transfers between devices  9.37 us (8%)
  between operations  2.67 us (2%)
  local copies, waits for them, and re-layouts  1.67 us (1%)
    all_to_all x1, blocking collectives, per_device(): parts = lax.all_to_all(part, ('z', 'y'), 0, 0, tiled=True)  35.2 us
    all_to_all x2, blocking collectives, from_all(): return lax.all_to_all(copies, axes, 0, 0, tiled=True)  25 us
    another operation x6, other arithmetic, orth(): lower = jnp.linalg.cholesky(gram)  8.67 us
    another operation x4, other arithmetic, orth(): return jax.scipy.linalg.solve_triangular(lower, mat.T, lower=True).T  7.42 us
    dot_general x1, matrix products, per_device(): along_x = jnp.einsum('vxyz,xa->avyz', field, factor_x, precision=precise)  6.86 us
    all_to_all x1, waiting for transfers between devices, from_all(): return lax.all_to_all(copies, axes, 0, 0, tiled=True)  6.82 us
    all_to_all x1, starting transfers between devices, from_all(): return lax.all_to_all(copies, axes, 0, 0, tiled=True)  5.25 us
    ppermute x1, starting transfers between devices, per_device(): raw = raw + lax.ppermute(raw, 'c', swap)  3.36 us
  transfers between devices with their start and end apart: 4, of which 3 were waited for; matrix products, arithmetic and copies ran while one was open for 1% of the time, Pallas kernels for 0%

profile of v2, /device:TPU:1, one launch (start us, length us, event | category | flops | bytes accessed | tf_op | source)
XLA Modules:
  0.0 115.9 jit_solution(8389964954610906997)
XLA Ops:
  0.6 0.0 copy-start
  0.7 6.9 %fusion = f32[16,8,32,128]{3,0,2,1:T(8,128)S(1)} fusion(f32[8,32,32,128]{3,2,1,0:T(8,128)} %param.5, f32[32,16]{0,1:T(8,128)} %param.6), kind=kOutput, calls=%fused_computation | convolution fusion | flops 201326592 | bytes 6293504 | tf_op jit(solution)/shard_map/vxyz,xa->avyz/dot_general | solution.py:24
  7.5 0.0 copy-start.2
  7.5 0.1 constant_dynamic-slice_fusion.1
  7.7 1.5 %collective-permute-start.1 = (f32[8,8,32,128]{3,0,2,1:T(8,128)S(1)}, f32[8,8,32,128]{3,0,2,1:T(8,128)S(1)}, u32[]{:S(2)}, u32[]{:S(2)}) collective-permute-start(f32[8,8,32,128]{3,0,2,1:T(8,128)S(1)} %get-tuple-element.6), channel_id=1, source_target_pairs={{0,4},{4,0},{1,5},{5,1},{2,6},{6,2},{3,7},{7,3},{8,12},{12,8},{9,1... | collective-permute-start | bytes 3145736 | tf_op jit(solution)/shard_map/ppermute | solution.py:27
  9.2 0.0 copy-done.2
  9.2 0.1 copy.31
  9.3 0.5 collective-permute-start
  9.8 1.7 %collective-permute-done.1 = f32[8,8,32,128]{3,0,2,1:T(8,128)S(1)} collective-permute-done((f32[8,8,32,128]{3,0,2,1:T(8,128)S(1)}, f32[8,8,32,128]{3,0,2,1:T(8,128)S(1)}, u32[]{:S(2)}, u32[]{:S(2)}) %collective-permute-start.1) | collective-permute-done | bytes 1048608 | tf_op jit(solution)/shard_map/ppermute | solution.py:27
  11.5 0.1 pad_maximum_fusion
  11.6 0.0 collective-permute-done
  11.6 2.2 %fusion.4 = f32[8,8,64,128]{3,2,1,0:T(8,128)S(1)} fusion(f32[8,8,64,128]{3,0,2,1:T(8,128)S(1)} %pad_maximum_fusion, f32[32,64]{0,1:T(8,128)S(1)} %collective-permute-done, f32[32,64]{0,1:T(8,128)S(1)} %copy.31), kind=kOutput, calls=%fused_computation.6 | convolution fusion | flops 402657280 | bytes 4210688 | tf_op jit(solution)/shard_map/avyz,yb->avbz/dot_general | solution.py:30
  13.8 0.2 fusion.26
  14.1 0.2 pad_maximum_fusion.1
  14.3 35.2 %all_to_all.20 = f32[16,8,32,128]{3,2,1,0:T(8,128)S(1)} all-to-all(f32[16,8,32,128]{3,2,1,0:T(8,128)S(1)} %bitcast.71), channel_id=1, replica_groups=mesh['z'=4,'y'=4,'c'=2,'x'=4] {'z','y'}, dimensions={0} | all-to-all | bytes 4194304 | tf_op jit(solution)/shard_map/all_to_all | solution.py:32
  49.5 0.0 copy-start.1
  49.5 0.2 reduce_sum.36
  49.6 0.1 copy.34
  49.8 11.0 %all_to_all.21 = f32[4,8,32,128]{3,1,2,0:T(8,128)S(1)} all-to-all(f32[4,8,32,128]{3,1,2,0:T(8,128)S(1)} %broadcast_in_dim.11), channel_id=1, replica_groups=mesh['z'=4,'y'=4,'c'=2,'x'=4] {'x'}, dimensions={0} | all-to-all | bytes 1048576 | tf_op jit(solution)/shard_map/all_to_all | solution.py:17
  60.7 0.0 copy-done.1
  60.7 0.4 convolution_bitcast_fusion.1
  61.1 0.1 copy.36
  61.2 0.0 copy-done
  61.2 0.4 fusion.27
  61.7 0.3 fusion.28
  61.9 3.4 %collective-permute-start.2 = (f32[64,128]{1,0:T(8,128)S(1)}, f32[64,128]{1,0:T(8,128)S(1)}, u32[]{:S(2)}, u32[]{:S(2)}) collective-permute-start(f32[64,128]{1,0:T(8,128)S(1)} %fusion.28), channel_id=1, source_target_pairs={{0,4},{4,0},{1,5},{5,1},{2,6},{6,2},{3,7},{7,3},{8,12},{12,8},{9,1... | collective-permute-start | bytes 98312 | tf_op jit(solution)/shard_map/ppermute | solution.py:38
  65.3 0.9 collective-permute-done.2
  66.2 14.0 %all_to_all.22 = f32[16,64,128]{2,1,0:T(8,128)S(1)} all-to-all(f32[16,64,128]{2,1,0:T(8,128)S(1)} %broadcast_in_dim.12), channel_id=1, replica_groups=mesh['z'=4,'y'=4,'c'=2,'x'=4] {'z','y'}, dimensions={0} | all-to-all | bytes 1048576 | tf_op jit(solution)/shard_map/all_to_all | solution.py:17
  80.3 0.2 fusion.29
  80.5 0.1 copy.37
  80.6 5.8 %cholesky.29 = f32[64,64]{1,0:T(8,128)S(1)} custom-call(f32[64,64]{1,0:T(8,128)S(1)} %fusion.18), custom_call_target="Cholesky" | custom-call | tf_op jit(solution)/shard_map/jit(cholesky)/cholesky | solution.py:11
  86.4 0.6 compare_reduce_fusion.1
  87.1 0.7 fusion.12
  87.7 4.9 %custom-call.14 = f32[1,64,64]{1,2,0:T(8,128)S(1)} custom-call(f32[1,64,64]{2,1,0:T(8,128)S(1)} %fusion.12), custom_call_target="InvertDiagBlocksLowerTriangular" | custom-call | tf_op jit(solution)/shard_map/jit(_solve_triangular)/triangular_solve | solution.py:12
  92.6 0.3 fusion.16
  92.9 0.6 convolution_bitcast_fusion
  93.5 0.6 convolution_bitcast_fusion.2
  94.0 0.1 broadcast_in_dim.13
  94.1 0.7 broadcast_in_dim.26
  94.8 5.2 %all-to-all-start.3 = ((f32[32,8,128]{2,1,0:T(8,128)}), f32[32,8,128]{2,1,0:T(8,128)S(1)}, u32[]{:S(2)}, u32[]{:S(2)}) async-start(f32[32,8,128]{2,1,0:T(8,128)} %broadcast_in_dim.26), calls=%async_computation.3 | async-start | bytes 262144 | tf_op jit(solution)/shard_map/all_to_all | solution.py:17
  100.0 0.9 fusion.30
  100.9 6.8 %all-to-all-done.3 = f32[32,8,128]{2,1,0:T(8,128)S(1)} async-done(((f32[32,8,128]{2,1,0:T(8,128)}), f32[32,8,128]{2,1,0:T(8,128)S(1)}, u32[]{:S(2)}, u32[]{:S(2)}) %all-to-all-start.3) | async-done | bytes 131104 | tf_op jit(solution)/shard_map/all_to_all | solution.py:17
  107.8 0.1 reshape.44
  107.9 0.1 fusion.31
  108.0 0.1 fusion.32
  108.2 0.1 copy.38
  108.2 1.5 %cholesky.61 = f32[16,16]{1,0:T(8,128)S(1)} custom-call(f32[16,16]{1,0:T(8,128)S(1)} %fusion.23), custom_call_target="Cholesky" | custom-call | tf_op jit(solution)/shard_map/jit(cholesky)/cholesky | solution.py:11
  109.7 0.6 compare_reduce_fusion
  110.4 0.6 fusion.19
  111.0 1.2 %custom-call.15 = f32[1,16,16]{1,2,0:T(8,128)S(1)} custom-call(f32[1,16,16]{2,1,0:T(8,128)S(1)} %fusion.19), custom_call_target="InvertDiagBlocksLowerTriangular" | custom-call | tf_op jit(solution)/shard_map/jit(_solve_triangular)/triangular_solve | solution.py:12
  112.3 0.2 fusion.21
  112.5 0.8 fusion.7
  113.2 0.8 fusion.33
  (9 shorter events, 0.2 us)
Async XLA Ops:
  0.6 60.6 %copy-start = (f32[128,64]{0,1:T(8,128)S(1)}, f32[128,64]{0,1:T(8,128)}, u32[]{:S(2)}) copy-start(f32[128,64]{0,1:T(8,128)} %param.8) | copy-start | bytes 98308
  7.5 1.7 %copy-start.2 = (f32[32,64]{1,0:T(8,128)S(1)}, f32[32,64]{1,0:T(8,128)}, u32[]{:S(2)}) copy-start(f32[32,64]{1,0:T(8,128)} %param.7) | copy-start | bytes 24580
  7.7 3.8 %collective-permute-start.1 = (f32[8,8,32,128]{3,0,2,1:T(8,128)S(1)}, f32[8,8,32,128]{3,0,2,1:T(8,128)S(1)}, u32[]{:S(2)}, u32[]{:S(2)}) collective-permute-start(f32[8,8,32,128]{3,0,2,1:T(8,128)S(1)} %get-tuple-element.6), channel_id=1, source_target_pairs={{0,4},{4,0},{1,5},{5,1},{2,6},{6,2},{3,7},{7,3},{8,12},{12,8},{9,1... | collective-permute-start | bytes 3145736 | tf_op jit(solution)/shard_map/ppermute | solution.py:27
  9.3 2.4 %collective-permute-start = (f32[32,64]{0,1:T(8,128)S(1)}, f32[32,64]{0,1:T(8,128)S(1)}, u32[]{:S(2)}, u32[]{:S(2)}) collective-permute-start(f32[32,64]{0,1:T(8,128)S(1)} %copy.31), channel_id=1, source_target_pairs={{0,4},{4,0},{1,5},{5,1},{2,6},{6,2},{3,7},{7,3},{8,12},{12,8},{9,1... | collective-permute-start | bytes 24584 | tf_op jit(solution)/shard_map/ppermute | solution.py:23
  49.5 11.3 %copy-start.1 = (f32[32,16]{0,1:T(8,128)S(1)}, f32[32,16]{0,1:T(8,128)}, u32[]{:S(2)}) copy-start(f32[32,16]{0,1:T(8,128)} %param.9) | copy-start | bytes 6148
  61.9 4.2 %collective-permute-start.2 = (f32[64,128]{1,0:T(8,128)S(1)}, f32[64,128]{1,0:T(8,128)S(1)}, u32[]{:S(2)}, u32[]{:S(2)}) collective-permute-start(f32[64,128]{1,0:T(8,128)S(1)} %fusion.28), channel_id=1, source_target_pairs={{0,4},{4,0},{1,5},{5,1},{2,6},{6,2},{3,7},{7,3},{8,12},{12,8},{9,1... | collective-permute-start | bytes 98312 | tf_op jit(solution)/shard_map/ppermute | solution.py:38
  94.8 13.0 %all-to-all-start.3 = ((f32[32,8,128]{2,1,0:T(8,128)}), f32[32,8,128]{2,1,0:T(8,128)S(1)}, u32[]{:S(2)}, u32[]{:S(2)}) async-start(f32[32,8,128]{2,1,0:T(8,128)} %broadcast_in_dim.26), calls=%async_computation.3 | async-start | bytes 262144 | tf_op jit(solution)/shard_map/all_to_all | solution.py:17

commit v3 on v2

v3 whole, which is shorter than its diff:
```python
import jax
import jax.numpy as jnp
from jax import lax
from jax.experimental import pallas as pl
from jax.experimental.pallas import tpu as pltpu
from jax.sharding import Mesh, PartitionSpec as P

precise = lax.Precision.HIGHEST
swap = [(0, 1), (1, 0)]


def from_all(value, axes, count):
    copies = jnp.broadcast_to(value[None], (count,) + value.shape)
    return lax.all_to_all(copies, axes, 0, 0, tiled=True)


def product(left, right, contract):
    return lax.dot_general(
        left, right, (contract, ((), ())), precision=precise,
        preferred_element_type=jnp.float32,
    )


def orth_rows(rows):
    count, width = rows.shape
    gram = product(rows, rows, ((1,), (1,)))
    tiles = count // 8
    left = [gram[8 * t:8 * t + 8, :] for t in range(tiles)]
    right = [rows[8 * t:8 * t + 8, :] for t in range(tiles)]
    sub_left = lax.broadcasted_iota(jnp.int32, (8, count), 0)
    sub_right = lax.broadcasted_iota(jnp.int32, (8, width), 0)
    done = []
    for p in range(tiles):
        cols = [
            {t: jnp.broadcast_to(left[t][:, 8 * p + j:8 * p + j + 1], (8, width)) for t in range(p, tiles)}
            for j in range(8)
        ]
        scale = jnp.zeros((8, width), jnp.float32)
        for k in range(8):
            pivot = cols[k][p][k:k + 1, :]
            inverse = 1.0 / pivot
            scale = jnp.where(sub_right == k, lax.rsqrt(pivot), scale)
            row_left = left[p][k:k + 1, :] * inverse[:, :count]
            row_right = right[p][k:k + 1, :] * inverse
            row_cols = [cols[j][p][k:k + 1, :] * inverse for j in range(8)]
            for t in range(p, tiles):
                factor = cols[k][t]
                if t == p:
                    factor = jnp.where(sub_right > k, factor, 0.0)
                left[t] = left[t] - factor[:, :count] * row_left
                right[t] = right[t] - factor * row_right
                for j in range(k + 1, 8):
                    cols[j][t] = cols[j][t] - factor * row_cols[j]
        done.append(right[p] * scale)
    return jnp.concatenate(done, axis=0)


def z_kernel(raws_ref, block_ref, proj_ref, grams_ref):
    raw = raws_ref[0]
    for i in range(1, 16):
        raw = raw + raws_ref[i]
    basis = orth_rows(raw)
    proj_ref[...] = product(basis, basis, ((0,), (0,)))
    none = jnp.zeros((64, 128), jnp.float32)
    pair = jnp.concatenate(
        [jnp.concatenate([basis, none], axis=1), jnp.concatenate([none, basis], axis=1)], axis=0
    )
    block = block_ref[...].reshape(4, 16, 2, 8, 128)
    gram = jnp.zeros((32, 32), jnp.float32)
    joined = jnp.concatenate(
        [
            jnp.concatenate([block[:, b, 0].reshape(32, 128), block[:, b, 1].reshape(32, 128)], axis=1)
            for b in range(16)
        ],
        axis=0,
    )
    wide = product(joined, pair, ((1,), (1,)))
    flat = jnp.concatenate([wide[32 * b:32 * b + 32] for b in range(16)], axis=1)
    gram = product(flat, flat, ((1,), (1,)))
    packed = jnp.concatenate([gram[8 * i:8 * i + 8] for i in range(4)], axis=1)
    for i in range(32):
        grams_ref[i] = packed


def v_kernel(grams_ref, factor_ref, proj_ref, rms_ref):
    total = grams_ref[0]
    for i in range(1, 32):
        total = total + grams_ref[i]
    gram = jnp.concatenate([total[:, 32 * i:32 * i + 32] for i in range(4)], axis=0)
    raw = product(factor_ref[...], gram, ((0,), (1,)))
    basis = orth_rows(raw)
    proj_ref[...] = product(basis, basis, ((0,), (0,)))
    energy = jnp.sum(basis * product(basis, gram, ((1,), (0,))), axis=(0, 1), keepdims=True)
    rms_ref[...] = jnp.sqrt(energy / (16 * 16 * 64 * 64))


def per_device(field, factor_x, factor_y, factor_z, factor_v):
    core = lax.axis_index("c")
    other_y = lax.ppermute(factor_y, "c", swap)
    along_x = jnp.einsum("vxyz,xa->avyz", field, factor_x, precision=precise)
    keep = lax.dynamic_slice_in_dim(along_x, core * 8, 8, 0)
    send = lax.dynamic_slice_in_dim(along_x, (1 - core) * 8, 8, 0)
    got = lax.ppermute(send, "c", swap)
    both = jnp.concatenate([keep, got], axis=2)
    both_y = jnp.concatenate([factor_y, other_y], axis=0)
    part = jnp.einsum("avyz,yb->avbz", both, both_y, precision=precise)
    part = part.reshape(8, 8, 2, 32, 128).transpose(0, 2, 3, 1, 4).reshape(16, 32, 8, 128)
    parts = lax.all_to_all(part, ("z", "y"), 0, 0, tiled=True)
    block = from_all(parts.sum(0), "x", 4)

    wide_z = jnp.einsum("xbvz,xvc->bcz", block, factor_v.reshape(4, 8, 16), precision=precise).reshape(512, 128)
    small_core = jnp.dot(wide_z, factor_z, precision=precise)
    raw = jnp.dot(small_core.T, wide_z, precision=precise)
    raw = raw + lax.ppermute(raw, "c", swap)
    raws = from_all(raw, ("z", "y"), 16)
    proj_z, grams = pl.pallas_call(
        z_kernel,
        out_shape=(
            jax.ShapeDtypeStruct((128, 128), jnp.float32),
            jax.ShapeDtypeStruct((32, 8, 128), jnp.float32),
        ),
    )(raws, block)
    grams = lax.all_to_all(grams, ("z", "y", "c"), 0, 0, tiled=True)
    proj_v, core_rms = pl.pallas_call(
        v_kernel,
        out_shape=(
            jax.ShapeDtypeStruct((32, 32), jnp.float32),
            jax.ShapeDtypeStruct((1, 1), jnp.float32),
        ),
    )(grams, factor_v)
    return (proj_z, proj_v, core_rms[0, 0])


def solution(mesh):
    fine = Mesh(mesh.devices.reshape(4, 4, 2, 4), ("z", "y", "c", "x"))
    rows = ("z", "y", "c")
    in_specs = (P("x", None, rows, None), P(), P(rows, None), P(), P())
    out_specs = (P(), P(), P())
    return jax.shard_map(
        per_device, mesh=fine, in_specs=in_specs, out_specs=out_specs, check_vma=False
    )
```

time: 116 us -> 104 us (0.90)
  other arithmetic: 16.7 us -> 0.26 us
  Pallas kernels: 0 us -> 7.49 us
  matrix products: 14.7 us -> 10.4 us
  blocking collectives: 60.2 us -> 63 us
  between operations: 2.67 us -> 0.75 us
  starting transfers between devices: 10.6 us -> 9.37 us
  local copies, waits for them, and re-layouts: 1.67 us -> 2.84 us
    another operation x10 -> x0, other arithmetic: 16.1 us -> none  [the longest x6 8.67 us: orth(): lower = jnp.linalg.cholesky(gram)]
    all_to_all x0 -> x1, blocking collectives: none -> 13.7 us  [per_device(): grams = lax.all_to_all(grams, ('z', 'y', 'c'), 0, 0, tiled=True)]
    all_to_all x2 -> x1, blocking collectives: 25 us -> 14.1 us  [from_all(): return lax.all_to_all(copies, axes, 0, 0, tiled=True)]
    pallas_call x0 -> x2, Pallas kernels: none -> 7.49 us  [the longest x1 4.97 us: per_device(): pl.pallas_call(z_kernel, out_shape=(jax.ShapeDtypeStruct((128, 128), jnp....]
    dot_general x9 -> x1, matrix products: 4.48 us -> 0.41 us  [per_device(): jnp.einsum('xbvz,xvc->bcz', block, factor_v.reshape(4, 8, 16), precision=...]
    reshape x1, local copies, waits for them, and re-layouts: 0.07 us -> 1.64 us  [per_device(): part.reshape(8, 8, 2, 32, 128).transpose(0, 2, 3, 1, 4)]
    all_to_all x1, starting transfers between devices: 5.25 us -> 3.99 us  [from_all(): return lax.all_to_all(copies, axes, 0, 0, tiled=True)]
  transfers between devices with their start and end apart: 4 -> 4, of which waited for: 3 -> 3; matrix products, arithmetic and copies ran while one was open for 1% -> 0% of each run, Pallas kernels for 0% -> 0%
where the time goes in v3:
time: 104 us
  blocking collectives  63 us (61%)
  matrix products  10.4 us (10%)
  waiting for transfers between devices  9.63 us (9%)
  starting transfers between devices  9.37 us (9%)
  Pallas kernels  7.49 us (7%)
  local copies, waits for them, and re-layouts  2.84 us (3%)
    all_to_all x1, blocking collectives, per_device(): parts = lax.all_to_all(part, ('z', 'y'), 0, 0, tiled=True)  35.2 us
    all_to_all x1, blocking collectives, from_all(): return lax.all_to_all(copies, axes, 0, 0, tiled=True)  14.1 us
    all_to_all x1, blocking collectives, per_device(): grams = lax.all_to_all(grams, ('z', 'y', 'c'), 0, 0, tiled=True)  13.7 us
    all_to_all x1, waiting for transfers between devices, from_all(): return lax.all_to_all(copies, axes, 0, 0, tiled=True)  7.07 us
    dot_general x1, matrix products, per_device(): along_x = jnp.einsum('vxyz,xa->avyz', field, factor_x, precision=precise)  6.86 us
    pallas_call x1, Pallas kernels, per_device(): pl.pallas_call(z_kernel, out_shape=(jax.ShapeDtypeStruct((128, 128), jnp....  4.97 us
    all_to_all x1, starting transfers between devices, from_all(): return lax.all_to_all(copies, axes, 0, 0, tiled=True)  3.99 us
    ppermute x1, starting transfers between devices, per_device(): raw = raw + lax.ppermute(raw, 'c', swap)  3.36 us
  transfers between devices with their start and end apart: 4, of which 3 were waited for; matrix products, arithmetic and copies ran while one was open for 0% of the time, Pallas kernels for 0%

profile of v3, /device:TPU:1, one launch (start us, length us, event | category | flops | bytes accessed | tf_op | source)
XLA Modules:
  0.0 103.8 jit_solution(765276623945837280)
XLA Ops:
  0.6 0.0 copy-start
  0.7 6.9 %fusion = f32[16,8,32,128]{3,0,2,1:T(8,128)S(1)} fusion(f32[8,32,32,128]{3,2,1,0:T(8,128)} %param.5, f32[32,16]{0,1:T(8,128)} %param.6), kind=kOutput, calls=%fused_computation | convolution fusion | flops 201326592 | bytes 6293504 | tf_op jit(solution)/shard_map/vxyz,xa->avyz/dot_general | solution.py:100
  7.5 0.0 copy-start.3
  7.5 0.1 constant_dynamic-slice_fusion.1
  7.7 1.5 %collective-permute-start.1 = (f32[8,8,32,128]{3,0,2,1:T(8,128)S(1)}, f32[8,8,32,128]{3,0,2,1:T(8,128)S(1)}, u32[]{:S(2)}, u32[]{:S(2)}) collective-permute-start(f32[8,8,32,128]{3,0,2,1:T(8,128)S(1)} %get-tuple-element.12), channel_id=1, source_target_pairs={{0,4},{4,0},{1,5},{5,1},{2,6},{6,2},{3,7},{7,3},{8,12},{12,8},{9,1... | collective-permute-start | bytes 3145736 | tf_op jit(solution)/shard_map/ppermute | solution.py:103
  9.2 0.0 copy-done.3
  9.2 0.1 copy.16
  9.3 0.5 collective-permute-start
  9.8 1.7 %collective-permute-done.1 = f32[8,8,32,128]{3,0,2,1:T(8,128)S(1)} collective-permute-done((f32[8,8,32,128]{3,0,2,1:T(8,128)S(1)}, f32[8,8,32,128]{3,0,2,1:T(8,128)S(1)}, u32[]{:S(2)}, u32[]{:S(2)}) %collective-permute-start.1) | collective-permute-done | bytes 1048608 | tf_op jit(solution)/shard_map/ppermute | solution.py:103
  11.5 0.1 pad_maximum_fusion
  11.6 0.0 collective-permute-done
  11.6 2.2 %fusion.2 = f32[64,8,8,128]{3,0,2,1:T(8,128)S(1)} fusion(f32[8,8,64,128]{3,0,2,1:T(8,128)S(1)} %pad_maximum_fusion, f32[32,64]{0,1:T(8,128)S(1)} %collective-permute-done, f32[32,64]{0,1:T(8,128)S(1)} %copy.16), kind=kOutput, calls=%fused_computation.3 | convolution fusion | flops 402657280 | bytes 4210688 | tf_op jit(solution)/shard_map/avyz,yb->avbz/dot_general | solution.py:106
  13.8 1.6 %copy.19 = f32[8,8,2,32,128]{4,1,3,2,0:T(8,128)S(1)} copy(f32[8,8,2,32,128]{4,3,2,1,0:T(8,128)S(1)} %bitcast.34) | data formatting | bytes 4194304 | tf_op jit(solution)/shard_map/reshape | solution.py:107
  15.5 35.2 %all_to_all.20 = f32[16,32,8,128]{3,2,1,0:T(8,128)S(1)} all-to-all(f32[16,32,8,128]{3,2,1,0:T(8,128)S(1)} %bitcast.35), channel_id=1, replica_groups=mesh['z'=4,'y'=4,'c'=2,'x'=4] {'z','y'}, dimensions={0} | all-to-all | bytes 4194304 | tf_op jit(solution)/shard_map/all_to_all | solution.py:108
  50.7 0.0 copy-start.4
  50.7 0.1 reduce_sum.9
  50.8 0.8 broadcast_in_dim.4
  51.7 4.0 %all-to-all-start.1 = ((f32[4,32,8,128]{3,2,1,0:T(8,128)}), f32[4,32,8,128]{3,2,1,0:T(8,128)S(1)}, u32[]{:S(2)}, u32[]{:S(2)}) async-start(f32[4,32,8,128]{3,2,1,0:T(8,128)} %broadcast_in_dim.4), calls=%async_computation.1 | async-start | bytes 1048576 | tf_op jit(solution)/shard_map/all_to_all | solution.py:14
  55.7 0.0 copy-done.4
  55.7 0.1 copy.20.factor_ref
  55.7 0.0 copy-start.2
  55.7 7.1 %all-to-all-done.1.block_ref = f32[4,32,8,128]{3,2,1,0:T(8,128)S(1)} async-done(((f32[4,32,8,128]{3,2,1,0:T(8,128)}), f32[4,32,8,128]{3,2,1,0:T(8,128)S(1)}, u32[]{:S(2)}, u32[]{:S(2)}) %all-to-all-start.1) | async-done | bytes 524320 | tf_op jit(solution)/shard_map/all_to_all | solution.py:14
  62.8 0.0 copy-start.1
  62.8 0.4 fusion.6
  63.2 0.0 copy-done
  63.2 0.4 fusion.10
  63.6 0.6 fusion.11
  64.2 3.4 %collective-permute-start.2 = (f32[64,128]{1,0:T(8,128)S(1)}, f32[64,128]{1,0:T(8,128)S(1)}, u32[]{:S(2)}, u32[]{:S(2)}) collective-permute-start(f32[64,128]{1,0:T(8,128)S(1)} %fusion.11), channel_id=1, source_target_pairs={{0,4},{4,0},{1,5},{5,1},{2,6},{6,2},{3,7},{7,3},{8,12},{12,8},{9,1... | collective-permute-start | bytes 98312 | tf_op jit(solution)/shard_map/ppermute | solution.py:114
  67.6 0.9 collective-permute-done.2
  68.5 14.1 %all_to_all.21.raws_ref = f32[16,64,128]{2,1,0:T(8,128)} all-to-all(f32[16,64,128]{2,1,0:T(8,128)S(1)} %broadcast_in_dim.5), channel_id=1, replica_groups=mesh['z'=4,'y'=4,'c'=2,'x'=4] {'z','y'}, dimensions={0} | all-to-all | bytes 1048576 | tf_op jit(solution)/shard_map/all_to_all | solution.py:14
  82.6 0.0 copy-done.1
  82.6 5.0 %shard_map.76 = (f32[128,128]{1,0:T(8,128)}, f32[32,8,128]{2,1,0:T(8,128)}) custom-call(f32[16,64,128]{2,1,0:T(8,128)} %all_to_all.21.raws_ref, f32[4,32,8,128]{3,2,1,0:T(8,128)} %copy-done.1), custom_call_target="tpu_custom_call" | custom-call | tf_op jit(solution)/shard_map/pallas_call | solution.py:116
  87.6 0.0 copy-done.2
  87.6 13.7 %all_to_all.22.grams_ref = f32[32,8,128]{2,1,0:T(8,128)} all-to-all(f32[32,8,128]{2,1,0:T(8,128)} %get-tuple-element.8), channel_id=1, replica_groups=mesh['z'=4,'y'=4,'c'=2,'x'=4] {'z','y','c'}, dimensions={0} | all-to-all | bytes 262144 | tf_op jit(solution)/shard_map/all_to_all | solution.py:123
  101.3 2.5 %shard_map.77 = (f32[32,32]{1,0:T(8,128)}, f32[1,1]{1,0:T(1,128)}) custom-call(f32[32,8,128]{2,1,0:T(8,128)} %all_to_all.22.grams_ref, f32[32,16]{1,0:T(8,128)} %copy-done.2), custom_call_target="tpu_custom_call" | custom-call | tf_op jit(solution)/shard_map/pallas_call | solution.py:124
  (2 shorter events, 0.1 us)
Async XLA Ops:
  0.6 62.6 %copy-start = (f32[128,64]{0,1:T(8,128)S(1)}, f32[128,64]{0,1:T(8,128)}, u32[]{:S(2)}) copy-start(f32[128,64]{0,1:T(8,128)} %param.8) | copy-start | bytes 98308
  7.5 1.7 %copy-start.3 = (f32[32,64]{1,0:T(8,128)S(1)}, f32[32,64]{1,0:T(8,128)}, u32[]{:S(2)}) copy-start(f32[32,64]{1,0:T(8,128)} %param.7) | copy-start | bytes 24580
  7.7 3.8 %collective-permute-start.1 = (f32[8,8,32,128]{3,0,2,1:T(8,128)S(1)}, f32[8,8,32,128]{3,0,2,1:T(8,128)S(1)}, u32[]{:S(2)}, u32[]{:S(2)}) collective-permute-start(f32[8,8,32,128]{3,0,2,1:T(8,128)S(1)} %get-tuple-element.12), channel_id=1, source_target_pairs={{0,4},{4,0},{1,5},{5,1},{2,6},{6,2},{3,7},{7,3},{8,12},{12,8},{9,1... | collective-permute-start | bytes 3145736 | tf_op jit(solution)/shard_map/ppermute | solution.py:103
  9.3 2.4 %collective-permute-start = (f32[32,64]{0,1:T(8,128)S(1)}, f32[32,64]{0,1:T(8,128)S(1)}, u32[]{:S(2)}, u32[]{:S(2)}) collective-permute-start(f32[32,64]{0,1:T(8,128)S(1)} %copy.16), channel_id=1, source_target_pairs={{0,4},{4,0},{1,5},{5,1},{2,6},{6,2},{3,7},{7,3},{8,12},{12,8},{9,1... | collective-permute-start | bytes 24584 | tf_op jit(solution)/shard_map/ppermute | solution.py:99
  50.7 4.9 %copy-start.4 = (f32[32,16]{0,1:T(8,128)S(1)}, f32[32,16]{0,1:T(8,128)}, u32[]{:S(2)}) copy-start(f32[32,16]{0,1:T(8,128)} %param.9) | copy-start | bytes 6148
  51.7 11.1 %all-to-all-start.1 = ((f32[4,32,8,128]{3,2,1,0:T(8,128)}), f32[4,32,8,128]{3,2,1,0:T(8,128)S(1)}, u32[]{:S(2)}, u32[]{:S(2)}) async-start(f32[4,32,8,128]{3,2,1,0:T(8,128)} %broadcast_in_dim.4), calls=%async_computation.1 | async-start | bytes 1048576 | tf_op jit(solution)/shard_map/all_to_all | solution.py:14
  55.7 31.9 %copy-start.2 = (f32[32,16]{1,0:T(8,128)}, f32[32,16]{1,0:T(8,128)S(1)}, u32[]{:S(2)}) copy-start(f32[32,16]{1,0:T(8,128)S(1)} %copy.20.factor_ref) | copy-start | bytes 6148
  62.8 19.8 %copy-start.1 = (f32[4,32,8,128]{3,2,1,0:T(8,128)}, f32[4,32,8,128]{3,2,1,0:T(8,128)S(1)}, u32[]{:S(2)}) copy-start(f32[4,32,8,128]{3,2,1,0:T(8,128)S(1)} %all-to-all-done.1.block_ref) | copy-start | bytes 1572868
  64.2 4.2 %collective-permute-start.2 = (f32[64,128]{1,0:T(8,128)S(1)}, f32[64,128]{1,0:T(8,128)S(1)}, u32[]{:S(2)}, u32[]{:S(2)}) collective-permute-start(f32[64,128]{1,0:T(8,128)S(1)} %fusion.11), channel_id=1, source_target_pairs={{0,4},{4,0},{1,5},{5,1},{2,6},{6,2},{3,7},{7,3},{8,12},{12,8},{9,1... | collective-permute-start | bytes 98312 | tf_op jit(solution)/shard_map/ppermute | solution.py:114

commit v4 on v3

--- a/solution.py
+++ b/solution.py
@@ -19,6 +19,82 @@
         left, right, (contract, ((), ())), precision=precise,
         preferred_element_type=jnp.float32,
     )
+
+
+def halves(value):
+    high = value.astype(jnp.bfloat16)
+    low = (value - high.astype(jnp.float32)).astype(jnp.bfloat16)
+    return high, low
+
+
+def dot16(left, right):
+    return lax.dot_general(
+        left, right, (((1,), (0,)), ((), ())), preferred_element_type=jnp.float32
+    )
+
+
+def spread(factor, turn):
+    pick = lax.broadcasted_iota(jnp.int32, (128, 16), 0) // 8 + turn
+    pick = jnp.where(pick >= 16, pick - 16, pick)
+    pick = (pick == lax.broadcasted_iota(jnp.int32, (128, 16), 1)).astype(jnp.float32)
+    wide = lax.broadcasted_iota(jnp.int32, (32, 256), 1) // 8
+    wide = (wide == lax.broadcasted_iota(jnp.int32, (32, 256), 0)).astype(jnp.float32)
+    full = product(product(pick, factor, ((1,), (0,))), wide, ((1,), (0,)))
+    row = lax.broadcasted_iota(jnp.int32, (128, 256), 0)
+    col = lax.broadcasted_iota(jnp.int32, (128, 256), 1)
+    return jnp.where((row & 7) == (col & 7), full, 0.0)
+
+
+def x_kernel(core_ref, factor_ref, factor_y_ref, field_ref, keep_ref, send_ref, both_ref):
+    step = pl.program_id(0)
+
+    @pl.when(step == 0)
+    def _():
+        high, low = halves(spread(factor_ref[...], core_ref[0] * 8))
+        both_ref[0:128, :] = high
+        both_ref[128:256, :] = low
+        send_ref[64, :, 0:64] = factor_y_ref[...]
+        send_ref[64, :, 64:128] = factor_y_ref[...]
+
+    count = field_ref.shape[0]
+    for v in range(count):
+        tile = jnp.concatenate(
+            [field_ref[v, :, 8 * t:8 * t + 8, :].reshape(256, 128) for t in range(4)], axis=1
+        )
+        high, low = halves(tile)
+        first = dot16(both_ref[...], high)
+        total = first[:128] + (first[128:] + dot16(both_ref[0:128, :], low))
+        for t in range(4):
+            cut = total[:, 128 * t:128 * t + 128].reshape(16, 8, 128)
+            keep_ref[:, step * count + v, 8 * t:8 * t + 8, :] = cut[:8]
+            for a in range(8):
+                send_ref[8 * a + step * count + v, 8 * t:8 * t + 8, :] = cut[8 + a]
+
+
+def y_kernel(mine_ref, keep_ref, got_ref, part_ref):
+    high, low = halves(jnp.concatenate([mine_ref[...], got_ref[64, :, 0:64]], axis=0).T)
+    left = jnp.concatenate([high, low, high], axis=1)
+    for a in range(8):
+        tile = jnp.concatenate(
+            [jnp.concatenate([keep_ref[a, v], got_ref[8 * a + v]], axis=0) for v in range(8)], axis=1
+        )
+        high, low = halves(tile)
+        total = dot16(left, jnp.concatenate([high, high, low], axis=0))
+        for v in range(8):
+            cut = total[:, 128 * v:128 * v + 128]
+            part_ref[2 * a, v] = cut[:32]
+            part_ref[2 * a + 1, v] = cut[32:]
+
+
+def raw_kernel(block_ref, factor_v_ref, factor_z_ref, raw_ref):
+    left = spread(factor_v_ref[...], 0)
+    tile = jnp.concatenate(
+        [block_ref[:, :, 8 * t:8 * t + 8, :].reshape(256, 128) for t in range(4)], axis=1
+    )
+    wide = product(left, tile, ((1,), (0,)))
+    wide = jnp.concatenate([wide[:, 128 * t:128 * t + 128] for t in range(4)], axis=0)
+    small = product(wide, factor_z_ref[...], ((1,), (1,)))
+    raw_ref[...] = product(small, wide, ((0,), (0,)))
 
 
 def orth_rows(rows):
@@ -65,18 +141,17 @@
     pair = jnp.concatenate(
         [jnp.concatenate([basis, none], axis=1), jnp.concatenate([none, basis], axis=1)], axis=0
     )
-    block = block_ref[...].reshape(4, 16, 2, 8, 128)
-    gram = jnp.zeros((32, 32), jnp.float32)
-    joined = jnp.concatenate(
-        [
-            jnp.concatenate([block[:, b, 0].reshape(32, 128), block[:, b, 1].reshape(32, 128)], axis=1)
-            for b in range(16)
-        ],
-        axis=0,
-    )
-    wide = product(joined, pair, ((1,), (1,)))
-    flat = jnp.concatenate([wide[32 * b:32 * b + 32] for b in range(16)], axis=1)
-    gram = product(flat, flat, ((1,), (1,)))
+    tiles = [block_ref[:, :, 8 * t:8 * t + 8, :].reshape(256, 128) for t in range(4)]
+    wide = jnp.concatenate(
+        [product(jnp.concatenate(tiles[t:t + 2], axis=1), pair, ((1,), (1,))) for t in (0, 2)], axis=1
+    )
+    outer = product(wide, wide, ((1,), (1,)))
+    row = lax.broadcasted_iota(jnp.int32, (256, 256), 0)
+    col = lax.broadcasted_iota(jnp.int32, (256, 256), 1)
+    outer = jnp.where((row & 7) == (col & 7), outer, 0.0).reshape(32, 8, 256).sum(axis=1)
+    fold = lax.broadcasted_iota(jnp.int32, (256, 32), 0) // 8
+    fold = (fold == lax.broadcasted_iota(jnp.int32, (256, 32), 1)).astype(jnp.float32)
+    gram = product(outer, fold, ((1,), (0,)))
     packed = jnp.concatenate([gram[8 * i:8 * i + 8] for i in range(4)], axis=1)
     for i in range(32):
         grams_ref[i] = packed
@@ -87,47 +162,88 @@
     for i in range(1, 32):
         total = total + grams_ref[i]
     gram = jnp.concatenate([total[:, 32 * i:32 * i + 32] for i in range(4)], axis=0)
-    raw = product(factor_ref[...], gram, ((0,), (1,)))
+    raw = product(factor_ref[...], gram, ((1,), (0,)))
     basis = orth_rows(raw)
     proj_ref[...] = product(basis, basis, ((0,), (0,)))
     energy = jnp.sum(basis * product(basis, gram, ((1,), (0,))), axis=(0, 1), keepdims=True)
     rms_ref[...] = jnp.sqrt(energy / (16 * 16 * 64 * 64))
 
 
+def in_vmem(*shape):
+    return pltpu.VMEM(shape, jnp.float32)
+
+
+def fast(value):
+    return pltpu.with_memory_space_constraint(value, pltpu.VMEM)
+
+
+def slow(value):
+    return pltpu.with_memory_space_constraint(value, pltpu.HBM)
+
+
+def room(mib):
+    return pltpu.CompilerParams(vmem_limit_bytes=mib << 20)
+
+
+def whole():
+    return pl.BlockSpec(memory_space=pltpu.VMEM)
+
+
 def per_device(field, factor_x, factor_y, factor_z, factor_v):
-    core = lax.axis_index("c")
-    other_y = lax.ppermute(factor_y, "c", swap)
-    along_x = jnp.einsum("vxyz,xa->avyz", field, factor_x, precision=precise)
-    keep = lax.dynamic_slice_in_dim(along_x, core * 8, 8, 0)
-    send = lax.dynamic_slice_in_dim(along_x, (1 - core) * 8, 8, 0)
+    core = lax.axis_index("c").astype(jnp.int32).reshape(1)
+    step = 2
+    keep, send = pl.pallas_call(
+        x_kernel,
+        grid=(8 // step,),
+        in_specs=[
+            pl.BlockSpec(memory_space=pltpu.SMEM),
+            whole(),
+            whole(),
+            pl.BlockSpec((step, 32, 32, 128), lambda i: (i, 0, 0, 0)),
+        ],
+        out_specs=(whole(), whole()),
+        out_shape=(in_vmem(8, 8, 32, 128), in_vmem(65, 32, 128)),
+        scratch_shapes=[pltpu.VMEM((256, 256), jnp.bfloat16)],
+        compiler_params=room(12),
+    )(core, slow(factor_x.T), slow(factor_y), slow(field))
     got = lax.ppermute(send, "c", swap)
-    both = jnp.concatenate([keep, got], axis=2)
-    both_y = jnp.concatenate([factor_y, other_y], axis=0)
-    part = jnp.einsum("avyz,yb->avbz", both, both_y, precision=precise)
-    part = part.reshape(8, 8, 2, 32, 128).transpose(0, 2, 3, 1, 4).reshape(16, 32, 8, 128)
+    part = pl.pallas_call(
+        y_kernel,
+        in_specs=[whole()] * 3,
+        out_specs=whole(),
+        out_shape=in_vmem(16, 8, 32, 128),
+        compiler_params=room(12),
+    )(factor_y, fast(keep), fast(got))
     parts = lax.all_to_all(part, ("z", "y"), 0, 0, tiled=True)
     block = from_all(parts.sum(0), "x", 4)
 
-    wide_z = jnp.einsum("xbvz,xvc->bcz", block, factor_v.reshape(4, 8, 16), precision=precise).reshape(512, 128)
-    small_core = jnp.dot(wide_z, factor_z, precision=precise)
-    raw = jnp.dot(small_core.T, wide_z, precision=precise)
+    raw = pl.pallas_call(
+        raw_kernel,
+        in_specs=[whole()] * 3,
+        out_specs=whole(),
+        out_shape=in_vmem(64, 128),
+        compiler_params=room(12),
+    )(fast(block), factor_v.T, factor_z.T)
     raw = raw + lax.ppermute(raw, "c", swap)
     raws = from_all(raw, ("z", "y"), 16)
     proj_z, grams = pl.pallas_call(
         z_kernel,
-        out_shape=(
-            jax.ShapeDtypeStruct((128, 128), jnp.float32),
-            jax.ShapeDtypeStruct((32, 8, 128), jnp.float32),
-        ),
-    )(raws, block)
+        in_specs=[whole()] * 2,
+        out_specs=(whole(), whole()),
+        out_shape=(jax.ShapeDtypeStruct((128, 128), jnp.float32), in_vmem(32, 8, 128)),
+        compiler_params=room(12),
+    )(fast(raws), fast(block))
     grams = lax.all_to_all(grams, ("z", "y", "c"), 0, 0, tiled=True)
     proj_v, core_rms = pl.pallas_call(
         v_kernel,
+        in_specs=[whole()] * 2,
+        out_specs=(whole(), whole()),
         out_shape=(
             jax.ShapeDtypeStruct((32, 32), jnp.float32),
             jax.ShapeDtypeStruct((1, 1), jnp.float32),
         ),
-    )(grams, factor_v)
+        compiler_params=room(12),
+    )(fast(grams), factor_v.T)
     return (proj_z, proj_v, core_rms[0, 0])
 
 

time: 104 us -> 93.6 us (0.90)
  matrix products: 10.4 us -> 0 us
  blocking collectives: 63 us -> 72.6 us
  waiting for transfers between devices: 9.63 us -> 3.17 us
  starting transfers between devices: 9.37 us -> 4.86 us
  Pallas kernels: 7.49 us -> 11.7 us
  local copies, waits for them, and re-layouts: 2.84 us -> 0.11 us
    all_to_all x1 -> x2, blocking collectives: 14.1 us -> 25 us  [from_all(): return lax.all_to_all(copies, axes, 0, 0, tiled=True)]
    dot_general x5 -> x0, matrix products: 10.4 us -> none  [the longest x1 6.86 us: per_device(): along_x = jnp.einsum('vxyz,xa->avyz', field, factor_x, precision=precise)]
    all_to_all x1 -> x0, waiting for transfers between devices: 7.07 us -> none  [from_all(): return lax.all_to_all(copies, axes, 0, 0, tiled=True)]
    pallas_call x2 -> x5, Pallas kernels: 7.49 us -> 11.7 us  [the longest x1 4.33 us: per_device(): pl.pallas_call(x_kernel, grid=(8 // step,), in_specs=[pl.BlockSpec(memory...]
    all_to_all x1 -> x0, starting transfers between devices: 3.99 us -> none  [from_all(): return lax.all_to_all(copies, axes, 0, 0, tiled=True)]
    reshape x1 -> x0, local copies, waits for them, and re-layouts: 1.64 us -> none  [per_device(): part.reshape(8, 8, 2, 32, 128).transpose(0, 2, 3, 1, 4)]
    all_to_all x1, blocking collectives: 13.7 us -> 12.4 us  [per_device(): grams = lax.all_to_all(grams, ('z', 'y', 'c'), 0, 0, tiled=True)]
  transfers between devices with their start and end apart: 4 -> 2, of which waited for: 3 -> 2; matrix products, arithmetic and copies ran while one was open for 0% -> 0% of each run, Pallas kernels for 0% -> 0%
where the time goes in v4:
time: 93.6 us; the launch traced here: 93.2 us
  blocking collectives  72.6 us (78%)
  Pallas kernels  11.7 us (12%)
  starting transfers between devices  4.86 us (5%)
  waiting for transfers between devices  3.17 us (3%)
    all_to_all x1, blocking collectives, per_device(): parts = lax.all_to_all(part, ('z', 'y'), 0, 0, tiled=True)  35.2 us
    all_to_all x2, blocking collectives, from_all(): return lax.all_to_all(copies, axes, 0, 0, tiled=True)  25 us
    all_to_all x1, blocking collectives, per_device(): grams = lax.all_to_all(grams, ('z', 'y', 'c'), 0, 0, tiled=True)  12.4 us
    pallas_call x1, Pallas kernels, per_device(): pl.pallas_call(x_kernel, grid=(8 // step,), in_specs=[pl.BlockSpec(memory...  4.33 us
    ppermute x1, starting transfers between devices, per_device(): raw = raw + lax.ppermute(raw, 'c', swap)  3.35 us
    pallas_call x1, Pallas kernels, per_device(): pl.pallas_call(z_kernel, in_specs=[whole()] * 2, out_specs=(whole(), whol...  3.29 us
    ppermute x1, waiting for transfers between devices, per_device(): got = lax.ppermute(send, 'c', swap)  2.31 us
  transfers between devices with their start and end apart: 2, of which 2 were waited for; matrix products, arithmetic and copies ran while one was open for 0% of the time, Pallas kernels for 0%

profile of v4, /device:TPU:1, one launch (start us, length us, event | category | flops | bytes accessed | tf_op | source)
XLA Modules:
  0.0 93.2 jit_solution(7221024028086734636)
XLA Ops:
  0.6 0.0 copy-start
  0.6 4.3 %shard_map.76 = (f32[8,8,32,128]{3,2,1,0:T(8,128)S(1)}, f32[65,32,128]{2,1,0:T(8,128)S(1)}) custom-call(s32[1]{0:T(128)} %bitcast.core_ref, f32[16,32]{1,0:T(8,128)} %bitcast.8, f32[32,64]{1,0:T(8,128)} %mine_ref.1, f32[8,32,32,128]{3,2,1,0:T(8,128)} %field_ref.1), custom_call_target="tpu_custom_call" | custom-call | tf_op jit(solution)/shard_map/pallas_call | solution.py:195
  5.0 1.5 %collective-permute-start = (f32[65,32,128]{2,1,0:T(8,128)S(1)}, f32[65,32,128]{2,1,0:T(8,128)S(1)}, u32[]{:S(2)}, u32[]{:S(2)}) collective-permute-start(f32[65,32,128]{2,1,0:T(8,128)S(1)} %get-tuple-element.10), channel_id=1, source_target_pairs={{0,4},{4,0},{1,5},{5,1},{2,6},{6,2},{3,7},{7,3},{8,12},{12,8},{9,1... | collective-permute-start | bytes 3194888 | tf_op jit(solution)/shard_map/ppermute | solution.py:209
  6.5 2.3 %collective-permute-done.got_ref = f32[65,32,128]{2,1,0:T(8,128)S(1)} collective-permute-done((f32[65,32,128]{2,1,0:T(8,128)S(1)}, f32[65,32,128]{2,1,0:T(8,128)S(1)}, u32[]{:S(2)}, u32[]{:S(2)}) %collective-permute-start) | collective-permute-done | bytes 1064992 | tf_op jit(solution)/shard_map/ppermute | solution.py:209
  8.8 0.0 copy-done
  8.8 0.8 shard_map.77
  9.6 35.2 %all_to_all.20 = f32[16,8,32,128]{3,2,1,0:T(8,128)S(1)} all-to-all(f32[16,8,32,128]{3,2,1,0:T(8,128)S(1)} %shard_map.77), channel_id=1, replica_groups=mesh['z'=4,'y'=4,'c'=2,'x'=4] {'z','y'}, dimensions={0} | all-to-all | bytes 4194304 | tf_op jit(solution)/shard_map/all_to_all | solution.py:217
  44.8 0.0 copy-start.1
  44.9 0.0 copy-start.2
  44.9 0.2 reduce_sum.9
  45.0 0.1 broadcast_in_dim.4
  45.1 11.0 %all_to_all.21.block_ref = f32[4,8,32,128]{3,2,1,0:T(8,128)S(1)} all-to-all(f32[4,8,32,128]{3,2,1,0:T(8,128)S(1)} %broadcast_in_dim.4), channel_id=1, replica_groups=mesh['z'=4,'y'=4,'c'=2,'x'=4] {'x'}, dimensions={0} | all-to-all | bytes 1048576 | tf_op jit(solution)/shard_map/all_to_all | solution.py:14
  56.1 0.0 copy-done.1
  56.1 0.0 copy-done.2
  56.1 1.7 %shard_map.78 = f32[64,128]{1,0:T(8,128)S(1)} custom-call(f32[4,8,32,128]{3,2,1,0:T(8,128)S(1)} %all_to_all.21.block_ref, f32[16,32]{1,0:T(8,128)S(1)} %bitcast.5, f32[64,128]{1,0:T(8,128)S(1)} %bitcast.7), custom_call_target="tpu_custom_call" | custom-call | tf_op jit(solution)/shard_map/pallas_call | solution.py:220
  57.8 3.4 %collective-permute-start.1 = (f32[64,128]{1,0:T(8,128)S(1)}, f32[64,128]{1,0:T(8,128)S(1)}, u32[]{:S(2)}, u32[]{:S(2)}) collective-permute-start(f32[64,128]{1,0:T(8,128)S(1)} %shard_map.78), channel_id=1, source_target_pairs={{0,4},{4,0},{1,5},{5,1},{2,6},{6,2},{3,7},{7,3},{8,12},{12,8},{9,1... | collective-permute-start | bytes 98312 | tf_op jit(solution)/shard_map/ppermute | solution.py:227
  61.1 0.9 collective-permute-done.1
  62.0 14.0 %all_to_all.22.raws_ref = f32[16,64,128]{2,1,0:T(8,128)S(1)} all-to-all(f32[16,64,128]{2,1,0:T(8,128)S(1)} %broadcast_in_dim.5), channel_id=1, replica_groups=mesh['z'=4,'y'=4,'c'=2,'x'=4] {'z','y'}, dimensions={0} | all-to-all | bytes 1048576 | tf_op jit(solution)/shard_map/all_to_all | solution.py:14
  76.0 3.3 %shard_map.79 = (f32[128,128]{1,0:T(8,128)}, f32[32,8,128]{2,1,0:T(8,128)S(1)}) custom-call(f32[16,64,128]{2,1,0:T(8,128)S(1)} %all_to_all.22.raws_ref, f32[4,8,32,128]{3,2,1,0:T(8,128)S(1)} %all_to_all.21.block_ref), custom_call_target="tpu_custom_call" | custom-call | tf_op jit(solution)/shard_map/pallas_call | solution.py:229
  79.3 12.4 %all_to_all.23.grams_ref = f32[32,8,128]{2,1,0:T(8,128)S(1)} all-to-all(f32[32,8,128]{2,1,0:T(8,128)S(1)} %get-tuple-element.12), channel_id=1, replica_groups=mesh['z'=4,'y'=4,'c'=2,'x'=4] {'z','y','c'}, dimensions={0} | all-to-all | bytes 262144 | tf_op jit(solution)/shard_map/all_to_all | solution.py:236
  91.7 1.5 %shard_map.80 = (f32[32,32]{1,0:T(8,128)}, f32[1,1]{1,0:T(1,128)}) custom-call(f32[32,8,128]{2,1,0:T(8,128)S(1)} %all_to_all.23.grams_ref, f32[16,32]{1,0:T(8,128)S(1)} %bitcast.6), custom_call_target="tpu_custom_call" | custom-call | tf_op jit(solution)/shard_map/pallas_call | solution.py:237
  (2 shorter events, 0.1 us)
Async XLA Ops:
  0.6 8.2 %copy-start = (f32[32,64]{1,0:T(8,128)S(1)}, f32[32,64]{1,0:T(8,128)}, u32[]{:S(2)}) copy-start(f32[32,64]{1,0:T(8,128)} %mine_ref.1) | copy-start | bytes 24580
  5.0 3.8 %collective-permute-start = (f32[65,32,128]{2,1,0:T(8,128)S(1)}, f32[65,32,128]{2,1,0:T(8,128)S(1)}, u32[]{:S(2)}, u32[]{:S(2)}) collective-permute-start(f32[65,32,128]{2,1,0:T(8,128)S(1)} %get-tuple-element.10), channel_id=1, source_target_pairs={{0,4},{4,0},{1,5},{5,1},{2,6},{6,2},{3,7},{7,3},{8,12},{12,8},{9,1... | collective-permute-start | bytes 3194888 | tf_op jit(solution)/shard_map/ppermute | solution.py:209
  44.8 11.2 %copy-start.1 = (f32[32,16]{0,1:T(8,128)S(1)}, f32[32,16]{0,1:T(8,128)}, u32[]{:S(2)}) copy-start(f32[32,16]{0,1:T(8,128)} %param.9) | copy-start | bytes 6148
  44.9 11.2 %copy-start.2 = (f32[128,64]{0,1:T(8,128)S(1)}, f32[128,64]{0,1:T(8,128)}, u32[]{:S(2)}) copy-start(f32[128,64]{0,1:T(8,128)} %param.8) | copy-start | bytes 98308
  57.8 4.2 %collective-permute-start.1 = (f32[64,128]{1,0:T(8,128)S(1)}, f32[64,128]{1,0:T(8,128)S(1)}, u32[]{:S(2)}, u32[]{:S(2)}) collective-permute-start(f32[64,128]{1,0:T(8,128)S(1)} %shard_map.78), channel_id=1, source_target_pairs={{0,4},{4,0},{1,5},{5,1},{2,6},{6,2},{3,7},{7,3},{8,12},{12,8},{9,1... | collective-permute-start | bytes 98312 | tf_op jit(solution)/shard_map/ppermute | solution.py:227

commit v5 on v4

--- a/solution.py
+++ b/solution.py
@@ -12,6 +12,11 @@
 def from_all(value, axes, count):
     copies = jnp.broadcast_to(value[None], (count,) + value.shape)
     return lax.all_to_all(copies, axes, 0, 0, tiled=True)
+
+
+def gather_sum(slots, axis):
+    got = [lax.ppermute(slots[k], axis, [(i, (i + k) % 4) for i in range(4)]) for k in (1, 3, 2)]
+    return (slots[0] + got[0]) + (got[1] + got[2])
 
 
 def product(left, right, contract):
@@ -71,7 +76,8 @@
                 send_ref[8 * a + step * count + v, 8 * t:8 * t + 8, :] = cut[8 + a]
 
 
-def y_kernel(mine_ref, keep_ref, got_ref, part_ref):
+def y_kernel(mine_ref, keep_ref, got_ref, y_first_ref, z_first_ref):
+    my_y, my_z = lax.axis_index("y"), lax.axis_index("z")
     high, low = halves(jnp.concatenate([mine_ref[...], got_ref[64, :, 0:64]], axis=0).T)
     left = jnp.concatenate([high, low, high], axis=1)
     for a in range(8):
@@ -80,10 +86,12 @@
         )
         high, low = halves(tile)
         total = dot16(left, jnp.concatenate([high, high, low], axis=0))
-        for v in range(8):
-            cut = total[:, 128 * v:128 * v + 128]
-            part_ref[2 * a, v] = cut[:32]
-            part_ref[2 * a + 1, v] = cut[32:]
+        for half in range(2):
+            to_z, to_y = divmod(2 * a + half, 4)
+            dz, dy = (to_z - my_z + 4) % 4, (to_y - my_y + 4) % 4
+            for v in range(4):
+                y_first_ref[dy, dz, v] = total[32 * half:32 * half + 32, 128 * v:128 * v + 128]
+                z_first_ref[dz, dy, v] = total[32 * half:32 * half + 32, 128 * v + 512:128 * v + 640]
 
 
 def raw_kernel(block_ref, factor_v_ref, factor_z_ref, raw_ref):
@@ -207,15 +215,16 @@
         compiler_params=room(12),
     )(core, slow(factor_x.T), slow(factor_y), slow(field))
     got = lax.ppermute(send, "c", swap)
-    part = pl.pallas_call(
+    y_first, z_first = pl.pallas_call(
         y_kernel,
         in_specs=[whole()] * 3,
-        out_specs=whole(),
-        out_shape=in_vmem(16, 8, 32, 128),
+        out_specs=(whole(), whole()),
+        out_shape=(in_vmem(4, 4, 4, 32, 128), in_vmem(4, 4, 4, 32, 128)),
         compiler_params=room(12),
     )(factor_y, fast(keep), fast(got))
-    parts = lax.all_to_all(part, ("z", "y"), 0, 0, tiled=True)
-    block = from_all(parts.sum(0), "x", 4)
+    y_done, z_done = gather_sum(y_first, "y"), gather_sum(z_first, "z")
+    block = jnp.concatenate([gather_sum(y_done, "z"), gather_sum(z_done, "y")], axis=0)
+    block = from_all(block, "x", 4)
 
     raw = pl.pallas_call(
         raw_kernel,

time: 93.6 us -> 88 us (0.940)
  blocking collectives: 72.6 us -> 36.7 us
  starting transfers between devices: 4.86 us -> 26.1 us
  waiting for transfers between devices: 3.17 us -> 12 us
    all_to_all x1 -> x0, blocking collectives: 35.2 us -> none  [per_device(): parts = lax.all_to_all(part, ('z', 'y'), 0, 0, tiled=True)]
    ppermute x0 -> x12, starting transfers between devices: none -> 19.9 us  [gather_sum(): lax.ppermute(slots[k], axis, [(i, (i + k) % 4) for i in range(4)])]
    ppermute x0 -> x12, waiting for transfers between devices: none -> 8.83 us  [gather_sum(): lax.ppermute(slots[k], axis, [(i, (i + k) % 4) for i in range(4)])]
    ppermute x1, starting transfers between devices: 3.35 us -> 4.61 us  [per_device(): raw = raw + lax.ppermute(raw, 'c', swap)]
  transfers between devices with their start and end apart: 2 -> 14, of which waited for: 2 -> 8; matrix products, arithmetic and copies ran while one was open for 0% -> 0% of each run, Pallas kernels for 0% -> 0%
where the time goes in v5:
time: 88 us; the launch traced here: 87.7 us
  blocking collectives  36.7 us (42%)
  starting transfers between devices  26.1 us (30%)
  waiting for transfers between devices  12 us (14%)
  Pallas kernels  11.7 us (13%)
    all_to_all x2, blocking collectives, from_all(): return lax.all_to_all(copies, axes, 0, 0, tiled=True)  24.3 us
    ppermute x12, starting transfers between devices, gather_sum(): lax.ppermute(slots[k], axis, [(i, (i + k) % 4) for i in range(4)])  19.9 us
    all_to_all x1, blocking collectives, per_device(): grams = lax.all_to_all(grams, ('z', 'y', 'c'), 0, 0, tiled=True)  12.4 us
    ppermute x12, waiting for transfers between devices, gather_sum(): lax.ppermute(slots[k], axis, [(i, (i + k) % 4) for i in range(4)])  8.83 us
    ppermute x1, starting transfers between devices, per_device(): raw = raw + lax.ppermute(raw, 'c', swap)  4.61 us
    pallas_call x1, Pallas kernels, per_device(): pl.pallas_call(x_kernel, grid=(8 // step,), in_specs=[pl.BlockSpec(memory...  4.33 us
    pallas_call x1, Pallas kernels, per_device(): pl.pallas_call(z_kernel, in_specs=[whole()] * 2, out_specs=(whole(), whol...  3.29 us
    ppermute x1, waiting for transfers between devices, per_device(): got = lax.ppermute(send, 'c', swap)  2.31 us
  transfers between devices with their start and end apart: 14, of which 8 were waited for; matrix products, arithmetic and copies ran while one was open for 0% of the time, Pallas kernels for 0%

profile of v5, /device:TPU:1, one launch (start us, length us, event | category | flops | bytes accessed | tf_op | source)
XLA Modules:
  0.0 87.7 jit_solution(15362115258567239537)
XLA Ops:
  0.6 0.0 copy-start
  0.6 4.3 %shard_map.76 = (f32[8,8,32,128]{3,2,1,0:T(8,128)S(1)}, f32[65,32,128]{2,1,0:T(8,128)S(1)}) custom-call(s32[1]{0:T(128)} %bitcast.core_ref, f32[16,32]{1,0:T(8,128)} %bitcast.52, f32[32,64]{1,0:T(8,128)} %mine_ref.1, f32[8,32,32,128]{3,2,1,0:T(8,128)} %field_ref.1), custom_call_target="tpu_custom_call" | custom-call | tf_op jit(solution)/shard_map/pallas_call | solution.py:203
  5.0 1.5 %collective-permute-start = (f32[65,32,128]{2,1,0:T(8,128)S(1)}, f32[65,32,128]{2,1,0:T(8,128)S(1)}, u32[]{:S(2)}, u32[]{:S(2)}) collective-permute-start(f32[65,32,128]{2,1,0:T(8,128)S(1)} %get-tuple-element.12), channel_id=1, source_target_pairs={{0,4},{4,0},{1,5},{5,1},{2,6},{6,2},{3,7},{7,3},{8,12},{12,8},{9,1... | collective-permute-start | bytes 3194888 | tf_op jit(solution)/shard_map/ppermute | solution.py:217
  6.5 2.3 %collective-permute-done.got_ref = f32[65,32,128]{2,1,0:T(8,128)S(1)} collective-permute-done((f32[65,32,128]{2,1,0:T(8,128)S(1)}, f32[65,32,128]{2,1,0:T(8,128)S(1)}, u32[]{:S(2)}, u32[]{:S(2)}) %collective-permute-start) | collective-permute-done | bytes 1064992 | tf_op jit(solution)/shard_map/ppermute | solution.py:217
  8.8 0.0 copy-done
  8.8 0.8 shard_map.77
  9.6 0.1 slice_bitcast_fusion.3
  9.7 3.1 %collective-permute-start.3 = (f32[4,4,32,128]{3,2,1,0:T(8,128)S(1)}, f32[4,4,32,128]{3,2,1,0:T(8,128)S(1)}, u32[]{:S(2)}, u32[]{:S(2)}) collective-permute-start(f32[4,4,32,128]{3,2,1,0:T(8,128)S(1)} %get-tuple-element.19), channel_id=1, source_target_pairs={{0,16},{8,24},{16,0},{24,8},{1,17},{9,25},{17,1},{25,9},{2,18},{10... | collective-permute-start | bytes 786440 | tf_op jit(solution)/shard_map/ppermute | solution.py:18
  12.8 0.8 collective-permute-start.2
  13.6 0.7 collective-permute-start.1
  14.3 0.1 slice_bitcast_fusion
  14.3 3.7 %collective-permute-start.9 = (f32[4,4,32,128]{3,2,1,0:T(8,128)S(1)}, f32[4,4,32,128]{3,2,1,0:T(8,128)S(1)}, u32[]{:S(2)}, u32[]{:S(2)}) collective-permute-start(f32[4,4,32,128]{3,2,1,0:T(8,128)S(1)} %get-tuple-element.22), channel_id=1, source_target_pairs={{0,64},{32,96},{64,0},{96,32},{1,65},{33,97},{65,1},{97,33},{2,66}... | collective-permute-start | bytes 786440 | tf_op jit(solution)/shard_map/ppermute | solution.py:18
  18.0 0.4 collective-permute-start.8
  18.4 0.5 collective-permute-done.3
  18.9 1.6 %collective-permute-start.7 = (f32[4,4,32,128]{3,2,1,0:T(8,128)S(1)}, f32[4,4,32,128]{3,2,1,0:T(8,128)S(1)}, u32[]{:S(2)}, u32[]{:S(2)}) collective-permute-start(f32[4,4,32,128]{3,2,1,0:T(8,128)S(1)} %get-tuple-element.24), channel_id=1, source_target_pairs={{0,32},{32,64},{64,96},{96,0},{1,33},{33,65},{65,97},{97,1},{2,34}... | collective-permute-start | bytes 786440 | tf_op jit(solution)/shard_map/ppermute | solution.py:18
  20.5 4.4 %collective-permute-done.2 = f32[4,4,32,128]{3,2,1,0:T(8,128)S(1)} collective-permute-done((f32[4,4,32,128]{3,2,1,0:T(8,128)S(1)}, f32[4,4,32,128]{3,2,1,0:T(8,128)S(1)}, u32[]{:S(2)}, u32[]{:S(2)}) %collective-permute-start.2) | collective-permute-done | bytes 262176 | tf_op jit(solution)/shard_map/ppermute | solution.py:18
  24.9 0.3 collective-permute-done.1
  25.2 0.1 fusion.1
  25.3 3.7 %collective-permute-start.6 = (f32[4,32,128]{2,1,0:T(8,128)S(1)}, f32[4,32,128]{2,1,0:T(8,128)S(1)}, u32[]{:S(2)}, u32[]{:S(2)}) collective-permute-start(f32[4,32,128]{2,1,0:T(8,128)S(1)} %get-tuple-element.25), channel_id=1, source_target_pairs={{0,64},{32,96},{64,0},{96,32},{1,65},{33,97},{65,1},{97,33},{2,66}... | collective-permute-start | bytes 196616 | tf_op jit(solution)/shard_map/ppermute | solution.py:18
  29.0 0.4 collective-permute-start.5
  29.4 0.0 collective-permute-done.9
  29.5 1.0 %collective-permute-start.4 = (f32[4,32,128]{2,1,0:T(8,128)S(1)}, f32[4,32,128]{2,1,0:T(8,128)S(1)}, u32[]{:S(2)}, u32[]{:S(2)}) collective-permute-start(f32[4,32,128]{2,1,0:T(8,128)S(1)} %get-tuple-element.27), channel_id=1, source_target_pairs={{0,32},{32,64},{64,96},{96,0},{1,33},{33,65},{65,97},{97,1},{2,34}... | collective-permute-start | bytes 196616 | tf_op jit(solution)/shard_map/ppermute | solution.py:18
  30.5 0.0 collective-permute-done.8
  30.5 0.0 collective-permute-done.7
  30.5 0.1 fusion
  30.6 3.0 %collective-permute-start.12 = (f32[4,32,128]{2,1,0:T(8,128)S(1)}, f32[4,32,128]{2,1,0:T(8,128)S(1)}, u32[]{:S(2)}, u32[]{:S(2)}) collective-permute-start(f32[4,32,128]{2,1,0:T(8,128)S(1)} %get-tuple-element.28), channel_id=1, source_target_pairs={{0,16},{8,24},{16,0},{24,8},{1,17},{9,25},{17,1},{25,9},{2,18},{10... | collective-permute-start | bytes 196616 | tf_op jit(solution)/shard_map/ppermute | solution.py:18
  33.6 0.8 collective-permute-start.11
  34.4 0.0 collective-permute-done.6
  34.4 0.7 collective-permute-start.10
  35.1 0.0 collective-permute-done.5
  35.1 0.0 collective-permute-done.4
  35.1 0.2 collective-permute-done.12
  35.3 1.4 %collective-permute-done.11 = f32[4,32,128]{2,1,0:T(8,128)S(1)} collective-permute-done((f32[4,32,128]{2,1,0:T(8,128)S(1)}, f32[4,32,128]{2,1,0:T(8,128)S(1)}, u32[]{:S(2)}, u32[]{:S(2)}) %collective-permute-start.11) | collective-permute-done | bytes 65568 | tf_op jit(solution)/shard_map/ppermute | solution.py:18
  36.7 2.1 %collective-permute-done.10 = f32[4,32,128]{2,1,0:T(8,128)S(1)} collective-permute-done((f32[4,32,128]{2,1,0:T(8,128)S(1)}, f32[4,32,128]{2,1,0:T(8,128)S(1)}, u32[]{:S(2)}, u32[]{:S(2)}) %collective-permute-start.10) | collective-permute-done | bytes 65568 | tf_op jit(solution)/shard_map/ppermute | solution.py:18
  38.8 0.0 copy-start.1
  38.8 0.0 copy-start.2
  38.9 0.1 broadcast_in_dim.4
  38.9 10.7 %all_to_all.15.block_ref = f32[4,8,32,128]{3,2,1,0:T(8,128)S(1)} all-to-all(f32[4,8,32,128]{3,2,1,0:T(8,128)S(1)} %broadcast_in_dim.4), channel_id=1, replica_groups=mesh['z'=4,'y'=4,'c'=2,'x'=4] {'x'}, dimensions={0} | all-to-all | bytes 1048576 | tf_op jit(solution)/shard_map/all_to_all | solution.py:14
  49.7 0.0 copy-done.1
  49.7 0.0 copy-done.2
  49.7 1.7 %shard_map.78 = f32[64,128]{1,0:T(8,128)S(1)} custom-call(f32[4,8,32,128]{3,2,1,0:T(8,128)S(1)} %all_to_all.15.block_ref, f32[16,32]{1,0:T(8,128)S(1)} %bitcast.49, f32[64,128]{1,0:T(8,128)S(1)} %bitcast.51), custom_call_target="tpu_custom_call" | custom-call | tf_op jit(solution)/shard_map/pallas_call | solution.py:229
  51.4 4.6 %collective-permute-start.13 = (f32[64,128]{1,0:T(8,128)S(1)}, f32[64,128]{1,0:T(8,128)S(1)}, u32[]{:S(2)}, u32[]{:S(2)}) collective-permute-start(f32[64,128]{1,0:T(8,128)S(1)} %shard_map.78), channel_id=1, source_target_pairs={{0,4},{4,0},{1,5},{5,1},{2,6},{6,2},{3,7},{7,3},{8,12},{12,8},{9,1... | collective-permute-start | bytes 98312 | tf_op jit(solution)/shard_map/ppermute | solution.py:236
  56.0 0.9 collective-permute-done.13
  56.9 13.6 %all_to_all.16.raws_ref = f32[16,64,128]{2,1,0:T(8,128)S(1)} all-to-all(f32[16,64,128]{2,1,0:T(8,128)S(1)} %broadcast_in_dim.5), channel_id=1, replica_groups=mesh['z'=4,'y'=4,'c'=2,'x'=4] {'z','y'}, dimensions={0} | all-to-all | bytes 1048576 | tf_op jit(solution)/shard_map/all_to_all | solution.py:14
  70.5 3.3 %shard_map.79 = (f32[128,128]{1,0:T(8,128)}, f32[32,8,128]{2,1,0:T(8,128)S(1)}) custom-call(f32[16,64,128]{2,1,0:T(8,128)S(1)} %all_to_all.16.raws_ref, f32[4,8,32,128]{3,2,1,0:T(8,128)S(1)} %all_to_all.15.block_ref), custom_call_target="tpu_custom_call" | custom-call | tf_op jit(solution)/shard_map/pallas_call | solution.py:238
  73.8 12.4 %all_to_all.17.grams_ref = f32[32,8,128]{2,1,0:T(8,128)S(1)} all-to-all(f32[32,8,128]{2,1,0:T(8,128)S(1)} %get-tuple-element.16), channel_id=1, replica_groups=mesh['z'=4,'y'=4,'c'=2,'x'=4] {'z','y','c'}, dimensions={0} | all-to-all | bytes 262144 | tf_op jit(solution)/shard_map/all_to_all | solution.py:245
  86.2 1.5 %shard_map.80 = (f32[32,32]{1,0:T(8,128)}, f32[1,1]{1,0:T(1,128)}) custom-call(f32[32,8,128]{2,1,0:T(8,128)S(1)} %all_to_all.17.grams_ref, f32[16,32]{1,0:T(8,128)S(1)} %bitcast.50), custom_call_target="tpu_custom_call" | custom-call | tf_op jit(solution)/shard_map/pallas_call | solution.py:246
  (7 shorter events, 0.1 us)
Async XLA Ops:
  0.6 8.2 %copy-start = (f32[32,64]{1,0:T(8,128)S(1)}, f32[32,64]{1,0:T(8,128)}, u32[]{:S(2)}) copy-start(f32[32,64]{1,0:T(8,128)} %mine_ref.1) | copy-start | bytes 24580
  5.0 3.8 %collective-permute-start = (f32[65,32,128]{2,1,0:T(8,128)S(1)}, f32[65,32,128]{2,1,0:T(8,128)S(1)}, u32[]{:S(2)}, u32[]{:S(2)}) collective-permute-start(f32[65,32,128]{2,1,0:T(8,128)S(1)} %get-tuple-element.12), channel_id=1, source_target_pairs={{0,4},{4,0},{1,5},{5,1},{2,6},{6,2},{3,7},{7,3},{8,12},{12,8},{9,1... | collective-permute-start | bytes 3194888 | tf_op jit(solution)/shard_map/ppermute | solution.py:217
  9.7 9.2 %collective-permute-start.3 = (f32[4,4,32,128]{3,2,1,0:T(8,128)S(1)}, f32[4,4,32,128]{3,2,1,0:T(8,128)S(1)}, u32[]{:S(2)}, u32[]{:S(2)}) collective-permute-start(f32[4,4,32,128]{3,2,1,0:T(8,128)S(1)} %get-tuple-element.19), channel_id=1, source_target_pairs={{0,16},{8,24},{16,0},{24,8},{1,17},{9,25},{17,1},{25,9},{2,18},{10... | collective-permute-start | bytes 786440 | tf_op jit(solution)/shard_map/ppermute | solution.py:18
  12.8 12.1 %collective-permute-start.2 = (f32[4,4,32,128]{3,2,1,0:T(8,128)S(1)}, f32[4,4,32,128]{3,2,1,0:T(8,128)S(1)}, u32[]{:S(2)}, u32[]{:S(2)}) collective-permute-start(f32[4,4,32,128]{3,2,1,0:T(8,128)S(1)} %get-tuple-element.20), channel_id=1, source_target_pairs={{0,24},{8,0},{16,8},{24,16},{1,25},{9,1},{17,9},{25,17},{2,26},{10... | collective-permute-start | bytes 786440 | tf_op jit(solution)/shard_map/ppermute | solution.py:18
  13.6 11.6 %collective-permute-start.1 = (f32[4,4,32,128]{3,2,1,0:T(8,128)S(1)}, f32[4,4,32,128]{3,2,1,0:T(8,128)S(1)}, u32[]{:S(2)}, u32[]{:S(2)}) collective-permute-start(f32[4,4,32,128]{3,2,1,0:T(8,128)S(1)} %get-tuple-element.21), channel_id=1, source_target_pairs={{0,8},{8,16},{16,24},{24,0},{1,9},{9,17},{17,25},{25,1},{2,10},{10... | collective-permute-start | bytes 786440 | tf_op jit(solution)/shard_map/ppermute | solution.py:18
  14.3 15.1 %collective-permute-start.9 = (f32[4,4,32,128]{3,2,1,0:T(8,128)S(1)}, f32[4,4,32,128]{3,2,1,0:T(8,128)S(1)}, u32[]{:S(2)}, u32[]{:S(2)}) collective-permute-start(f32[4,4,32,128]{3,2,1,0:T(8,128)S(1)} %get-tuple-element.22), channel_id=1, source_target_pairs={{0,64},{32,96},{64,0},{96,32},{1,65},{33,97},{65,1},{97,33},{2,66}... | collective-permute-start | bytes 786440 | tf_op jit(solution)/shard_map/ppermute | solution.py:18
  18.0 12.5 %collective-permute-start.8 = (f32[4,4,32,128]{3,2,1,0:T(8,128)S(1)}, f32[4,4,32,128]{3,2,1,0:T(8,128)S(1)}, u32[]{:S(2)}, u32[]{:S(2)}) collective-permute-start(f32[4,4,32,128]{3,2,1,0:T(8,128)S(1)} %get-tuple-element.23), channel_id=1, source_target_pairs={{0,96},{32,0},{64,32},{96,64},{1,97},{33,1},{65,33},{97,65},{2,98}... | collective-permute-start | bytes 786440 | tf_op jit(solution)/shard_map/ppermute | solution.py:18
  18.9 11.6 %collective-permute-start.7 = (f32[4,4,32,128]{3,2,1,0:T(8,128)S(1)}, f32[4,4,32,128]{3,2,1,0:T(8,128)S(1)}, u32[]{:S(2)}, u32[]{:S(2)}) collective-permute-start(f32[4,4,32,128]{3,2,1,0:T(8,128)S(1)} %get-tuple-element.24), channel_id=1, source_target_pairs={{0,32},{32,64},{64,96},{96,0},{1,33},{33,65},{65,97},{97,1},{2,34}... | collective-permute-start | bytes 786440 | tf_op jit(solution)/shard_map/ppermute | solution.py:18
  25.3 9.1 %collective-permute-start.6 = (f32[4,32,128]{2,1,0:T(8,128)S(1)}, f32[4,32,128]{2,1,0:T(8,128)S(1)}, u32[]{:S(2)}, u32[]{:S(2)}) collective-permute-start(f32[4,32,128]{2,1,0:T(8,128)S(1)} %get-tuple-element.25), channel_id=1, source_target_pairs={{0,64},{32,96},{64,0},{96,32},{1,65},{33,97},{65,1},{97,33},{2,66}... | collective-permute-start | bytes 196616 | tf_op jit(solution)/shard_map/ppermute | solution.py:18
  29.0 6.1 %collective-permute-start.5 = (f32[4,32,128]{2,1,0:T(8,128)S(1)}, f32[4,32,128]{2,1,0:T(8,128)S(1)}, u32[]{:S(2)}, u32[]{:S(2)}) collective-permute-start(f32[4,32,128]{2,1,0:T(8,128)S(1)} %get-tuple-element.26), channel_id=1, source_target_pairs={{0,96},{32,0},{64,32},{96,64},{1,97},{33,1},{65,33},{97,65},{2,98}... | collective-permute-start | bytes 196616 | tf_op jit(solution)/shard_map/ppermute | solution.py:18
  29.5 5.6 %collective-permute-start.4 = (f32[4,32,128]{2,1,0:T(8,128)S(1)}, f32[4,32,128]{2,1,0:T(8,128)S(1)}, u32[]{:S(2)}, u32[]{:S(2)}) collective-permute-start(f32[4,32,128]{2,1,0:T(8,128)S(1)} %get-tuple-element.27), channel_id=1, source_target_pairs={{0,32},{32,64},{64,96},{96,0},{1,33},{33,65},{65,97},{97,1},{2,34}... | collective-permute-start | bytes 196616 | tf_op jit(solution)/shard_map/ppermute | solution.py:18
  30.6 4.7 %collective-permute-start.12 = (f32[4,32,128]{2,1,0:T(8,128)S(1)}, f32[4,32,128]{2,1,0:T(8,128)S(1)}, u32[]{:S(2)}, u32[]{:S(2)}) collective-permute-start(f32[4,32,128]{2,1,0:T(8,128)S(1)} %get-tuple-element.28), channel_id=1, source_target_pairs={{0,16},{8,24},{16,0},{24,8},{1,17},{9,25},{17,1},{25,9},{2,18},{10... | collective-permute-start | bytes 196616 | tf_op jit(solution)/shard_map/ppermute | solution.py:18
  33.6 3.1 %collective-permute-start.11 = (f32[4,32,128]{2,1,0:T(8,128)S(1)}, f32[4,32,128]{2,1,0:T(8,128)S(1)}, u32[]{:S(2)}, u32[]{:S(2)}) collective-permute-start(f32[4,32,128]{2,1,0:T(8,128)S(1)} %get-tuple-element.29), channel_id=1, source_target_pairs={{0,24},{8,0},{16,8},{24,16},{1,25},{9,1},{17,9},{25,17},{2,26},{10... | collective-permute-start | bytes 196616 | tf_op jit(solution)/shard_map/ppermute | solution.py:18
  34.4 4.4 %collective-permute-start.10 = (f32[4,32,128]{2,1,0:T(8,128)S(1)}, f32[4,32,128]{2,1,0:T(8,128)S(1)}, u32[]{:S(2)}, u32[]{:S(2)}) collective-permute-start(f32[4,32,128]{2,1,0:T(8,128)S(1)} %get-tuple-element.30), channel_id=1, source_target_pairs={{0,8},{8,16},{16,24},{24,0},{1,9},{9,17},{17,25},{25,1},{2,10},{10... | collective-permute-start | bytes 196616 | tf_op jit(solution)/shard_map/ppermute | solution.py:18
  38.8 10.9 %copy-start.1 = (f32[32,16]{0,1:T(8,128)S(1)}, f32[32,16]{0,1:T(8,128)}, u32[]{:S(2)}) copy-start(f32[32,16]{0,1:T(8,128)} %param.9) | copy-start | bytes 6148
  38.8 10.8 %copy-start.2 = (f32[128,64]{0,1:T(8,128)S(1)}, f32[128,64]{0,1:T(8,128)}, u32[]{:S(2)}) copy-start(f32[128,64]{0,1:T(8,128)} %param.8) | copy-start | bytes 98308
  51.4 5.5 %collective-permute-start.13 = (f32[64,128]{1,0:T(8,128)S(1)}, f32[64,128]{1,0:T(8,128)S(1)}, u32[]{:S(2)}, u32[]{:S(2)}) collective-permute-start(f32[64,128]{1,0:T(8,128)S(1)} %shard_map.78), channel_id=1, source_target_pairs={{0,4},{4,0},{1,5},{5,1},{2,6},{6,2},{3,7},{7,3},{8,12},{12,8},{9,1... | collective-permute-start | bytes 98312 | tf_op jit(solution)/shard_map/ppermute | solution.py:236

commit v6 on v4

--- a/solution.py
+++ b/solution.py
@@ -12,6 +12,22 @@
 def from_all(value, axes, count):
     copies = jnp.broadcast_to(value[None], (count,) + value.shape)
     return lax.all_to_all(copies, axes, 0, 0, tiled=True)
+
+
+def hops(step, first):
+    pairs = []
+    for z in range(4):
+        for y in range(4):
+            for c in range(2):
+                along_y = (c == 0) == first
+                to_z, to_y = (z, (y + step) % 4) if along_y else ((z + step) % 4, y)
+                pairs.append((8 * z + 2 * y + c, 8 * to_z + 2 * to_y + c))
+    return pairs
+
+
+def gather_sum(slots, first):
+    got = [lax.ppermute(slots[k], ("z", "y", "c"), hops(k, first)) for k in (2, 1, 3)]
+    return (slots[0] + got[0]) + (got[1] + got[2])
 
 
 def product(left, right, contract):
@@ -71,7 +87,8 @@
                 send_ref[8 * a + step * count + v, 8 * t:8 * t + 8, :] = cut[8 + a]
 
 
-def y_kernel(mine_ref, keep_ref, got_ref, part_ref):
+def y_kernel(mine_ref, keep_ref, got_ref, slots_ref):
+    my_y, my_z, core = lax.axis_index("y"), lax.axis_index("z"), lax.axis_index("c")
     high, low = halves(jnp.concatenate([mine_ref[...], got_ref[64, :, 0:64]], axis=0).T)
     left = jnp.concatenate([high, low, high], axis=1)
     for a in range(8):
@@ -80,14 +97,24 @@
         )
         high, low = halves(tile)
         total = dot16(left, jnp.concatenate([high, high, low], axis=0))
-        for v in range(8):
-            cut = total[:, 128 * v:128 * v + 128]
-            part_ref[2 * a, v] = cut[:32]
-            part_ref[2 * a + 1, v] = cut[32:]
-
-
-def raw_kernel(block_ref, factor_v_ref, factor_z_ref, raw_ref):
-    left = spread(factor_v_ref[...], 0)
+        for half in range(2):
+            to_z, to_y = divmod(2 * a + half, 4)
+            dz, dy = (to_z - my_z + 4) % 4, (to_y - my_y + 4) % 4
+            first = dy + core * (dz - dy)
+            second = dz + core * (dy - dz)
+            for v in range(8):
+                slots_ref[first, second, v] = total[32 * half:32 * half + 32, 128 * v:128 * v + 128]
+
+
+def spread_kernel(factor_ref, spread_ref):
+    spread_ref[...] = spread(factor_ref[...], 0)
+
+
+def raw_kernel(mine_ref, one_ref, two_ref, three_ref, spread_ref, factor_z_ref, raw_ref, block_ref):
+    my_x = lax.axis_index("x")
+    for back, ref in enumerate((mine_ref, one_ref, two_ref, three_ref)):
+        block_ref[(my_x - back + 4) % 4] = ref[...]
+    left = spread_ref[...]
     tile = jnp.concatenate(
         [block_ref[:, :, 8 * t:8 * t + 8, :].reshape(256, 128) for t in range(4)], axis=1
     )
@@ -207,23 +234,32 @@
         compiler_params=room(12),
     )(core, slow(factor_x.T), slow(factor_y), slow(field))
     got = lax.ppermute(send, "c", swap)
-    part = pl.pallas_call(
+    late_v, keep = lax.optimization_barrier((factor_v.T, keep))
+    wide_v = pl.pallas_call(
+        spread_kernel,
+        in_specs=[whole()],
+        out_specs=whole(),
+        out_shape=in_vmem(128, 256),
+        compiler_params=room(4),
+    )(late_v)
+    slots = pl.pallas_call(
         y_kernel,
         in_specs=[whole()] * 3,
         out_specs=whole(),
-        out_shape=in_vmem(16, 8, 32, 128),
+        out_shape=in_vmem(4, 4, 8, 32, 128),
         compiler_params=room(12),
     )(factor_y, fast(keep), fast(got))
-    parts = lax.all_to_all(part, ("z", "y"), 0, 0, tiled=True)
-    block = from_all(parts.sum(0), "x", 4)
-
-    raw = pl.pallas_call(
+    mine = gather_sum(gather_sum(slots, True), False)
+    one, two, three = [
+        lax.ppermute(mine, "x", [(i, (i + k) % 4) for i in range(4)]) for k in (1, 2, 3)
+    ]
+    raw, block = pl.pallas_call(
         raw_kernel,
-        in_specs=[whole()] * 3,
-        out_specs=whole(),
-        out_shape=in_vmem(64, 128),
-        compiler_params=room(12),
-    )(fast(block), factor_v.T, factor_z.T)
+        in_specs=[whole()] * 6,
+        out_specs=(whole(), whole()),
+        out_shape=(in_vmem(64, 128), in_vmem(4, 8, 32, 128)),
+        compiler_params=room(12),
+    )(fast(mine), fast(one), fast(two), fast(three), fast(wide_v), factor_z.T)
     raw = raw + lax.ppermute(raw, "c", swap)
     raws = from_all(raw, ("z", "y"), 16)
     proj_z, grams = pl.pallas_call(

time: 93.6 us -> 83.3 us (0.89)
  blocking collectives: 72.6 us -> 29.3 us
  starting transfers between devices: 4.86 us -> 22.5 us
  waiting for transfers between devices: 3.17 us -> 18.4 us
    all_to_all x1 -> x0, blocking collectives: 35.2 us -> none  [per_device(): parts = lax.all_to_all(part, ('z', 'y'), 0, 0, tiled=True)]
    ppermute x0 -> x9, starting transfers between devices: none -> 16.9 us  [the longest x6 12 us: gather_sum(): lax.ppermute(slots[k], ('z', 'y', 'c'), hops(k, first))]
    ppermute x0 -> x9, waiting for transfers between devices: none -> 15.2 us  [the longest x6 12.7 us: gather_sum(): lax.ppermute(slots[k], ('z', 'y', 'c'), hops(k, first))]
    all_to_all x2 -> x1, blocking collectives: 25 us -> 16.9 us  [from_all(): return lax.all_to_all(copies, axes, 0, 0, tiled=True)]
  transfers between devices with their start and end apart: 2 -> 11, of which waited for: 2 -> 9; matrix products, arithmetic and copies ran while one was open for 0% -> 0% of each run, Pallas kernels for 0% -> 1%
where the time goes in v6:
time: 83.3 us; the launch traced here: 83.1 us
  blocking collectives  29.3 us (35%)
  starting transfers between devices  22.5 us (27%)
  waiting for transfers between devices  18.4 us (22%)
  Pallas kernels  11.7 us (14%)
    all_to_all x1, blocking collectives, from_all(): return lax.all_to_all(copies, axes, 0, 0, tiled=True)  16.9 us
    ppermute x6, waiting for transfers between devices, gather_sum(): lax.ppermute(slots[k], ('z', 'y', 'c'), hops(k, first))  12.7 us
    all_to_all x1, blocking collectives, per_device(): grams = lax.all_to_all(grams, ('z', 'y', 'c'), 0, 0, tiled=True)  12.4 us
    ppermute x6, starting transfers between devices, gather_sum(): lax.ppermute(slots[k], ('z', 'y', 'c'), hops(k, first))  12 us
    ppermute x3, starting transfers between devices, per_device(): lax.ppermute(mine, 'x', [(i, (i + k) % 4) for i in range(4)])  4.89 us
    pallas_call x1, Pallas kernels, per_device(): pl.pallas_call(x_kernel, grid=(8 // step,), in_specs=[pl.BlockSpec(memory...  4.33 us
    ppermute x1, starting transfers between devices, per_device(): raw = raw + lax.ppermute(raw, 'c', swap)  4.11 us
    pallas_call x1, Pallas kernels, per_device(): pl.pallas_call(z_kernel, in_specs=[whole()] * 2, out_specs=(whole(), whol...  3.29 us
  transfers between devices with their start and end apart: 11, of which 9 were waited for; matrix products, arithmetic and copies ran while one was open for 0% of the time, Pallas kernels for 1%

profile of v6, /device:TPU:1, one launch (start us, length us, event | category | flops | bytes accessed | tf_op | source)
XLA Modules:
  0.0 83.1 jit_solution(17526112546166243866)
XLA Ops:
  0.6 0.0 copy-start
  0.6 4.3 %shard_map.76 = (f32[8,8,32,128]{3,2,1,0:T(8,128)S(1)}, f32[65,32,128]{2,1,0:T(8,128)S(1)}) custom-call(s32[1]{0:T(128)} %bitcast.1.core_ref, f32[16,32]{1,0:T(8,128)} %bitcast.32, f32[32,64]{1,0:T(8,128)} %mine_ref.1, f32[8,32,32,128]{3,2,1,0:T(8,128)} %field_ref.1), custom_call_target="tpu_custom_call" | custom-call | tf_op jit(solution)/shard_map/pallas_call | solution.py:222
  5.0 1.5 %collective-permute-start = (f32[65,32,128]{2,1,0:T(8,128)S(1)}, f32[65,32,128]{2,1,0:T(8,128)S(1)}, u32[]{:S(2)}, u32[]{:S(2)}) collective-permute-start(f32[65,32,128]{2,1,0:T(8,128)S(1)} %get-tuple-element.15), channel_id=1, source_target_pairs={{0,4},{4,0},{1,5},{5,1},{2,6},{6,2},{3,7},{7,3},{8,12},{12,8},{9,1... | collective-permute-start | bytes 3194888 | tf_op jit(solution)/shard_map/ppermute | solution.py:236
  6.5 2.3 %collective-permute-done.got_ref = f32[65,32,128]{2,1,0:T(8,128)S(1)} collective-permute-done((f32[65,32,128]{2,1,0:T(8,128)S(1)}, f32[65,32,128]{2,1,0:T(8,128)S(1)}, u32[]{:S(2)}, u32[]{:S(2)}) %collective-permute-start) | collective-permute-done | bytes 1064992 | tf_op jit(solution)/shard_map/ppermute | solution.py:236
  8.8 0.0 copy-done
  8.8 0.8 shard_map.77
  9.6 0.1 slice_bitcast_fusion
  9.8 0.0 copy-start.1
  9.8 3.8 %collective-permute-start.1 = (f32[4,8,32,128]{3,2,1,0:T(8,128)S(1)}, f32[4,8,32,128]{3,2,1,0:T(8,128)S(1)}, u32[]{:S(2)}, u32[]{:S(2)}) collective-permute-start(f32[4,8,32,128]{3,2,1,0:T(8,128)S(1)} %get-tuple-element.25), channel_id=1, source_target_pairs={{0,16},{4,68},{8,24},{12,76},{16,0},{20,84},{24,8},{28,92},{32,48}... | collective-permute-start | bytes 1572872 | tf_op jit(solution)/shard_map/ppermute | solution.py:29
  13.5 0.7 collective-permute-start.2
  14.3 0.0 copy-start.2
  14.3 1.9 %collective-permute-start.3 = (f32[4,8,32,128]{3,2,1,0:T(8,128)S(1)}, f32[4,8,32,128]{3,2,1,0:T(8,128)S(1)}, u32[]{:S(2)}, u32[]{:S(2)}) collective-permute-start(f32[4,8,32,128]{3,2,1,0:T(8,128)S(1)} %get-tuple-element.23), channel_id=1, source_target_pairs={{0,24},{4,100},{8,0},{12,108},{16,8},{20,116},{24,16},{28,124},{32... | collective-permute-start | bytes 1572872 | tf_op jit(solution)/shard_map/ppermute | solution.py:29
  16.2 4.2 %collective-permute-done.1 = f32[4,8,32,128]{3,2,1,0:T(8,128)S(1)} collective-permute-done((f32[4,8,32,128]{3,2,1,0:T(8,128)S(1)}, f32[4,8,32,128]{3,2,1,0:T(8,128)S(1)}, u32[]{:S(2)}, u32[]{:S(2)}) %collective-permute-start.1) | collective-permute-done | bytes 524320 | tf_op jit(solution)/shard_map/ppermute | solution.py:29
  20.4 5.6 %collective-permute-done.2 = f32[4,8,32,128]{3,2,1,0:T(8,128)S(1)} collective-permute-done((f32[4,8,32,128]{3,2,1,0:T(8,128)S(1)}, f32[4,8,32,128]{3,2,1,0:T(8,128)S(1)}, u32[]{:S(2)}, u32[]{:S(2)}) %collective-permute-start.2) | collective-permute-done | bytes 524320 | tf_op jit(solution)/shard_map/ppermute | solution.py:29
  26.0 0.6 collective-permute-done.3
  26.6 0.2 fusion.1
  26.9 2.9 %collective-permute-start.4 = (f32[8,32,128]{2,1,0:T(8,128)S(1)}, f32[8,32,128]{2,1,0:T(8,128)S(1)}, u32[]{:S(2)}, u32[]{:S(2)}) collective-permute-start(f32[8,32,128]{2,1,0:T(8,128)S(1)} %get-tuple-element.28), channel_id=1, source_target_pairs={{0,64},{4,20},{8,72},{12,28},{16,80},{20,4},{24,88},{28,12},{32,96... | collective-permute-start | bytes 393224 | tf_op jit(solution)/shard_map/ppermute | solution.py:29
  29.8 0.4 collective-permute-start.5
  30.2 2.3 %collective-permute-start.6 = (f32[8,32,128]{2,1,0:T(8,128)S(1)}, f32[8,32,128]{2,1,0:T(8,128)S(1)}, u32[]{:S(2)}, u32[]{:S(2)}) collective-permute-start(f32[8,32,128]{2,1,0:T(8,128)S(1)} %get-tuple-element.26), channel_id=1, source_target_pairs={{0,96},{4,28},{8,104},{12,4},{16,112},{20,12},{24,120},{28,20},{32... | collective-permute-start | bytes 393224 | tf_op jit(solution)/shard_map/ppermute | solution.py:29
  32.4 0.1 collective-permute-done.4
  32.6 2.2 %collective-permute-done.5 = f32[8,32,128]{2,1,0:T(8,128)S(1)} collective-permute-done((f32[8,32,128]{2,1,0:T(8,128)S(1)}, f32[8,32,128]{2,1,0:T(8,128)S(1)}, u32[]{:S(2)}, u32[]{:S(2)}) %collective-permute-start.5) | collective-permute-done | bytes 131104 | tf_op jit(solution)/shard_map/ppermute | solution.py:29
  34.8 0.0 collective-permute-done.6
  34.8 1.3 %collective-permute-start.7 = (f32[8,32,128]{2,1,0:T(8,128)S(1)}, f32[8,32,128]{2,1,0:T(8,128)S(1)}, u32[]{:S(2)}, u32[]{:S(2)}) collective-permute-start(f32[8,32,128]{2,1,0:T(8,128)S(1)} %fusion.3.mine_ref), channel_id=1, source_target_pairs={{0,1},{1,2},{2,3},{3,0},{4,5},{5,6},{6,7},{7,4},{8,9},{9,10},{10,1... | collective-permute-start | bytes 393224 | tf_op jit(solution)/shard_map/ppermute | solution.py:254
  36.1 2.5 %collective-permute-start.8 = (f32[8,32,128]{2,1,0:T(8,128)S(1)}, f32[8,32,128]{2,1,0:T(8,128)S(1)}, u32[]{:S(2)}, u32[]{:S(2)}) collective-permute-start(f32[8,32,128]{2,1,0:T(8,128)S(1)} %fusion.3.mine_ref), channel_id=1, source_target_pairs={{0,2},{1,3},{2,0},{3,1},{4,6},{5,7},{6,4},{7,5},{8,10},{9,11},{10,... | collective-permute-start | bytes 393224 | tf_op jit(solution)/shard_map/ppermute | solution.py:254
  38.6 1.2 %collective-permute-start.9 = (f32[8,32,128]{2,1,0:T(8,128)S(1)}, f32[8,32,128]{2,1,0:T(8,128)S(1)}, u32[]{:S(2)}, u32[]{:S(2)}) collective-permute-start(f32[8,32,128]{2,1,0:T(8,128)S(1)} %fusion.3.mine_ref), channel_id=1, source_target_pairs={{0,3},{1,0},{2,1},{3,2},{4,7},{5,4},{6,5},{7,6},{8,11},{9,8},{10,9... | collective-permute-start | bytes 393224 | tf_op jit(solution)/shard_map/ppermute | solution.py:254
  39.7 0.0 copy-done.1
  39.7 0.5 shard_map.78.spread_ref
  40.2 0.0 collective-permute-done.7.one_ref
  40.2 2.2 %collective-permute-done.8.two_ref = f32[8,32,128]{2,1,0:T(8,128)S(1)} collective-permute-done((f32[8,32,128]{2,1,0:T(8,128)S(1)}, f32[8,32,128]{2,1,0:T(8,128)S(1)}, u32[]{:S(2)}, u32[]{:S(2)}) %collective-permute-start.8) | collective-permute-done | bytes 131104 | tf_op jit(solution)/shard_map/ppermute | solution.py:254
  42.4 0.3 collective-permute-done.9.three_ref
  42.7 0.0 copy-done.2
  42.7 1.2 %shard_map.79 = (f32[64,128]{1,0:T(8,128)S(1)}, f32[4,8,32,128]{3,2,1,0:T(8,128)S(1)}) custom-call(f32[8,32,128]{2,1,0:T(8,128)S(1)} %fusion.3.mine_ref, f32[8,32,128]{2,1,0:T(8,128)S(1)} %collective-permute-done.7.one_ref, f32[8,32,128]{2,1,0:T(8,128)S(1)} %collective-permute-done.8.two_ref, f32[8,32,128]{2,1,0:T(8,128)S(1)} %collective-permute-done.9.three_ref, ...), custom_call_target="tpu_custom_call" | custom-call | tf_op jit(solution)/shard_map/pallas_call | solution.py:256
  43.9 4.1 %collective-permute-start.10 = (f32[64,128]{1,0:T(8,128)S(1)}, f32[64,128]{1,0:T(8,128)S(1)}, u32[]{:S(2)}, u32[]{:S(2)}) collective-permute-start(f32[64,128]{1,0:T(8,128)S(1)} %get-tuple-element.17), channel_id=1, source_target_pairs={{0,4},{4,0},{1,5},{5,1},{2,6},{6,2},{3,7},{7,3},{8,12},{12,8},{9,1... | collective-permute-start | bytes 98312 | tf_op jit(solution)/shard_map/ppermute | solution.py:263
  48.0 0.9 %collective-permute-done.10 = f32[64,128]{1,0:T(8,128)S(1)} collective-permute-done((f32[64,128]{1,0:T(8,128)S(1)}, f32[64,128]{1,0:T(8,128)S(1)}, u32[]{:S(2)}, u32[]{:S(2)}) %collective-permute-start.10) | collective-permute-done | bytes 32800 | tf_op jit(solution)/shard_map/ppermute | solution.py:263
  48.9 16.9 %all_to_all.10.raws_ref = f32[16,64,128]{2,1,0:T(8,128)S(1)} all-to-all(f32[16,64,128]{2,1,0:T(8,128)S(1)} %broadcast_in_dim.2), channel_id=1, replica_groups=mesh['z'=4,'y'=4,'c'=2,'x'=4] {'z','y'}, dimensions={0} | all-to-all | bytes 1048576 | tf_op jit(solution)/shard_map/all_to_all | solution.py:14
  65.9 3.3 %shard_map.80 = (f32[128,128]{1,0:T(8,128)}, f32[32,8,128]{2,1,0:T(8,128)S(1)}) custom-call(f32[16,64,128]{2,1,0:T(8,128)S(1)} %all_to_all.10.raws_ref, f32[4,8,32,128]{3,2,1,0:T(8,128)S(1)} %get-tuple-element.18.block_ref), custom_call_target="tpu_custom_call" | custom-call | tf_op jit(solution)/shard_map/pallas_call | solution.py:265
  69.2 12.4 %all_to_all.11.grams_ref = f32[32,8,128]{2,1,0:T(8,128)S(1)} all-to-all(f32[32,8,128]{2,1,0:T(8,128)S(1)} %get-tuple-element.20), channel_id=1, replica_groups=mesh['z'=4,'y'=4,'c'=2,'x'=4] {'z','y','c'}, dimensions={0} | all-to-all | bytes 262144 | tf_op jit(solution)/shard_map/all_to_all | solution.py:272
  81.5 1.5 %shard_map.81 = (f32[32,32]{1,0:T(8,128)}, f32[1,1]{1,0:T(1,128)}) custom-call(f32[32,8,128]{2,1,0:T(8,128)S(1)} %all_to_all.11.grams_ref, f32[16,32]{1,0:T(8,128)S(1)} %bitcast.30), custom_call_target="tpu_custom_call" | custom-call | tf_op jit(solution)/shard_map/pallas_call | solution.py:273
  (4 shorter events, 0.1 us)
Async XLA Ops:
  0.6 8.2 %copy-start = (f32[32,64]{1,0:T(8,128)S(1)}, f32[32,64]{1,0:T(8,128)}, u32[]{:S(2)}) copy-start(f32[32,64]{1,0:T(8,128)} %mine_ref.1) | copy-start | bytes 24580
  5.0 3.8 %collective-permute-start = (f32[65,32,128]{2,1,0:T(8,128)S(1)}, f32[65,32,128]{2,1,0:T(8,128)S(1)}, u32[]{:S(2)}, u32[]{:S(2)}) collective-permute-start(f32[65,32,128]{2,1,0:T(8,128)S(1)} %get-tuple-element.15), channel_id=1, source_target_pairs={{0,4},{4,0},{1,5},{5,1},{2,6},{6,2},{3,7},{7,3},{8,12},{12,8},{9,1... | collective-permute-start | bytes 3194888 | tf_op jit(solution)/shard_map/ppermute | solution.py:236
  9.8 30.0 %copy-start.1 = (f32[32,16]{0,1:T(8,128)S(1)}, f32[32,16]{0,1:T(8,128)}, u32[]{:S(2)}) copy-start(f32[32,16]{0,1:T(8,128)} %param.9) | copy-start | bytes 6148
  9.8 10.7 %collective-permute-start.1 = (f32[4,8,32,128]{3,2,1,0:T(8,128)S(1)}, f32[4,8,32,128]{3,2,1,0:T(8,128)S(1)}, u32[]{:S(2)}, u32[]{:S(2)}) collective-permute-start(f32[4,8,32,128]{3,2,1,0:T(8,128)S(1)} %get-tuple-element.25), channel_id=1, source_target_pairs={{0,16},{4,68},{8,24},{12,76},{16,0},{20,84},{24,8},{28,92},{32,48}... | collective-permute-start | bytes 1572872 | tf_op jit(solution)/shard_map/ppermute | solution.py:29
  13.5 12.5 %collective-permute-start.2 = (f32[4,8,32,128]{3,2,1,0:T(8,128)S(1)}, f32[4,8,32,128]{3,2,1,0:T(8,128)S(1)}, u32[]{:S(2)}, u32[]{:S(2)}) collective-permute-start(f32[4,8,32,128]{3,2,1,0:T(8,128)S(1)} %get-tuple-element.24), channel_id=1, source_target_pairs={{0,8},{4,36},{8,16},{12,44},{16,24},{20,52},{24,0},{28,60},{32,40}... | collective-permute-start | bytes 1572872 | tf_op jit(solution)/shard_map/ppermute | solution.py:29
  14.3 28.4 %copy-start.2 = (f32[128,64]{0,1:T(8,128)S(1)}, f32[128,64]{0,1:T(8,128)}, u32[]{:S(2)}) copy-start(f32[128,64]{0,1:T(8,128)} %param.8) | copy-start | bytes 98308
  14.3 12.3 %collective-permute-start.3 = (f32[4,8,32,128]{3,2,1,0:T(8,128)S(1)}, f32[4,8,32,128]{3,2,1,0:T(8,128)S(1)}, u32[]{:S(2)}, u32[]{:S(2)}) collective-permute-start(f32[4,8,32,128]{3,2,1,0:T(8,128)S(1)} %get-tuple-element.23), channel_id=1, source_target_pairs={{0,24},{4,100},{8,0},{12,108},{16,8},{20,116},{24,16},{28,124},{32... | collective-permute-start | bytes 1572872 | tf_op jit(solution)/shard_map/ppermute | solution.py:29
  26.9 5.7 %collective-permute-start.4 = (f32[8,32,128]{2,1,0:T(8,128)S(1)}, f32[8,32,128]{2,1,0:T(8,128)S(1)}, u32[]{:S(2)}, u32[]{:S(2)}) collective-permute-start(f32[8,32,128]{2,1,0:T(8,128)S(1)} %get-tuple-element.28), channel_id=1, source_target_pairs={{0,64},{4,20},{8,72},{12,28},{16,80},{20,4},{24,88},{28,12},{32,96... | collective-permute-start | bytes 393224 | tf_op jit(solution)/shard_map/ppermute | solution.py:29
  29.8 5.0 %collective-permute-start.5 = (f32[8,32,128]{2,1,0:T(8,128)S(1)}, f32[8,32,128]{2,1,0:T(8,128)S(1)}, u32[]{:S(2)}, u32[]{:S(2)}) collective-permute-start(f32[8,32,128]{2,1,0:T(8,128)S(1)} %get-tuple-element.27), channel_id=1, source_target_pairs={{0,32},{4,12},{8,40},{12,20},{16,48},{20,28},{24,56},{28,4},{32,64... | collective-permute-start | bytes 393224 | tf_op jit(solution)/shard_map/ppermute | solution.py:29
  30.2 4.6 %collective-permute-start.6 = (f32[8,32,128]{2,1,0:T(8,128)S(1)}, f32[8,32,128]{2,1,0:T(8,128)S(1)}, u32[]{:S(2)}, u32[]{:S(2)}) collective-permute-start(f32[8,32,128]{2,1,0:T(8,128)S(1)} %get-tuple-element.26), channel_id=1, source_target_pairs={{0,96},{4,28},{8,104},{12,4},{16,112},{20,12},{24,120},{28,20},{32... | collective-permute-start | bytes 393224 | tf_op jit(solution)/shard_map/ppermute | solution.py:29
  34.8 5.4 %collective-permute-start.7 = (f32[8,32,128]{2,1,0:T(8,128)S(1)}, f32[8,32,128]{2,1,0:T(8,128)S(1)}, u32[]{:S(2)}, u32[]{:S(2)}) collective-permute-start(f32[8,32,128]{2,1,0:T(8,128)S(1)} %fusion.3.mine_ref), channel_id=1, source_target_pairs={{0,1},{1,2},{2,3},{3,0},{4,5},{5,6},{6,7},{7,4},{8,9},{9,10},{10,1... | collective-permute-start | bytes 393224 | tf_op jit(solution)/shard_map/ppermute | solution.py:254
  36.1 6.3 %collective-permute-start.8 = (f32[8,32,128]{2,1,0:T(8,128)S(1)}, f32[8,32,128]{2,1,0:T(8,128)S(1)}, u32[]{:S(2)}, u32[]{:S(2)}) collective-permute-start(f32[8,32,128]{2,1,0:T(8,128)S(1)} %fusion.3.mine_ref), channel_id=1, source_target_pairs={{0,2},{1,3},{2,0},{3,1},{4,6},{5,7},{6,4},{7,5},{8,10},{9,11},{10,... | collective-permute-start | bytes 393224 | tf_op jit(solution)/shard_map/ppermute | solution.py:254
  38.6 4.1 %collective-permute-start.9 = (f32[8,32,128]{2,1,0:T(8,128)S(1)}, f32[8,32,128]{2,1,0:T(8,128)S(1)}, u32[]{:S(2)}, u32[]{:S(2)}) collective-permute-start(f32[8,32,128]{2,1,0:T(8,128)S(1)} %fusion.3.mine_ref), channel_id=1, source_target_pairs={{0,3},{1,0},{2,1},{3,2},{4,7},{5,4},{6,5},{7,6},{8,11},{9,8},{10,9... | collective-permute-start | bytes 393224 | tf_op jit(solution)/shard_map/ppermute | solution.py:254
  43.9 5.0 %collective-permute-start.10 = (f32[64,128]{1,0:T(8,128)S(1)}, f32[64,128]{1,0:T(8,128)S(1)}, u32[]{:S(2)}, u32[]{:S(2)}) collective-permute-start(f32[64,128]{1,0:T(8,128)S(1)} %get-tuple-element.17), channel_id=1, source_target_pairs={{0,4},{4,0},{1,5},{5,1},{2,6},{6,2},{3,7},{7,3},{8,12},{12,8},{9,1... | collective-permute-start | bytes 98312 | tf_op jit(solution)/shard_map/ppermute | solution.py:263

commit v7 on v6

--- a/solution.py
+++ b/solution.py
@@ -7,11 +7,6 @@
 
 precise = lax.Precision.HIGHEST
 swap = [(0, 1), (1, 0)]
-
-
-def from_all(value, axes, count):
-    copies = jnp.broadcast_to(value[None], (count,) + value.shape)
-    return lax.all_to_all(copies, axes, 0, 0, tiled=True)
 
 
 def hops(step, first):
@@ -30,6 +25,13 @@
     return (slots[0] + got[0]) + (got[1] + got[2])
 
 
+def sum_all(value, axis):
+    one, two, three = [
+        lax.ppermute(value, axis, [(i, (i + k) % 4) for i in range(4)]) for k in (1, 2, 3)
+    ]
+    return (value + two) + (one + three)
+
+
 def product(left, right, contract):
     return lax.dot_general(
         left, right, (contract, ((), ())), precision=precise,
@@ -41,6 +43,15 @@
     high = value.astype(jnp.bfloat16)
     low = (value - high.astype(jnp.float32)).astype(jnp.bfloat16)
     return high, low
+
+
+def product3(left, right, contract):
+    (left_high, left_low), (right_high, right_low) = halves(left), halves(right)
+
+    def one(a, b):
+        return lax.dot_general(a, b, (contract, ((), ())), preferred_element_type=jnp.float32)
+
+    return one(left_high, right_high) + (one(left_high, right_low) + one(left_low, right_high))
 
 
 def dot16(left, right):
@@ -118,10 +129,10 @@
     tile = jnp.concatenate(
         [block_ref[:, :, 8 * t:8 * t + 8, :].reshape(256, 128) for t in range(4)], axis=1
     )
-    wide = product(left, tile, ((1,), (0,)))
+    wide = product3(left, tile, ((1,), (0,)))
     wide = jnp.concatenate([wide[:, 128 * t:128 * t + 128] for t in range(4)], axis=0)
-    small = product(wide, factor_z_ref[...], ((1,), (1,)))
-    raw_ref[...] = product(small, wide, ((0,), (0,)))
+    small = product3(wide, factor_z_ref[...], ((1,), (1,)))
+    raw_ref[...] = product3(small, wide, ((0,), (0,)))
 
 
 def orth_rows(rows):
@@ -158,21 +169,18 @@
     return jnp.concatenate(done, axis=0)
 
 
-def z_kernel(raws_ref, block_ref, proj_ref, grams_ref):
-    raw = raws_ref[0]
-    for i in range(1, 16):
-        raw = raw + raws_ref[i]
-    basis = orth_rows(raw)
-    proj_ref[...] = product(basis, basis, ((0,), (0,)))
+def z_kernel(rows_ref, block_ref, proj_ref, grams_ref):
+    basis = orth_rows(rows_ref[...])
+    proj_ref[...] = product3(basis, basis, ((0,), (0,)))
     none = jnp.zeros((64, 128), jnp.float32)
     pair = jnp.concatenate(
         [jnp.concatenate([basis, none], axis=1), jnp.concatenate([none, basis], axis=1)], axis=0
     )
     tiles = [block_ref[:, :, 8 * t:8 * t + 8, :].reshape(256, 128) for t in range(4)]
     wide = jnp.concatenate(
-        [product(jnp.concatenate(tiles[t:t + 2], axis=1), pair, ((1,), (1,))) for t in (0, 2)], axis=1
-    )
-    outer = product(wide, wide, ((1,), (1,)))
+        [product3(jnp.concatenate(tiles[t:t + 2], axis=1), pair, ((1,), (1,))) for t in (0, 2)], axis=1
+    )
+    outer = product3(wide, wide, ((1,), (1,)))
     row = lax.broadcasted_iota(jnp.int32, (256, 256), 0)
     col = lax.broadcasted_iota(jnp.int32, (256, 256), 1)
     outer = jnp.where((row & 7) == (col & 7), outer, 0.0).reshape(32, 8, 256).sum(axis=1)
@@ -191,8 +199,8 @@
     gram = jnp.concatenate([total[:, 32 * i:32 * i + 32] for i in range(4)], axis=0)
     raw = product(factor_ref[...], gram, ((1,), (0,)))
     basis = orth_rows(raw)
-    proj_ref[...] = product(basis, basis, ((0,), (0,)))
-    energy = jnp.sum(basis * product(basis, gram, ((1,), (0,))), axis=(0, 1), keepdims=True)
+    proj_ref[...] = product3(basis, basis, ((0,), (0,)))
+    energy = jnp.sum(basis * product3(basis, gram, ((1,), (0,))), axis=(0, 1), keepdims=True)
     rms_ref[...] = jnp.sqrt(energy / (16 * 16 * 64 * 64))
 
 
@@ -261,14 +269,14 @@
         compiler_params=room(12),
     )(fast(mine), fast(one), fast(two), fast(three), fast(wide_v), factor_z.T)
     raw = raw + lax.ppermute(raw, "c", swap)
-    raws = from_all(raw, ("z", "y"), 16)
+    raw = sum_all(sum_all(raw, "y"), "z")
     proj_z, grams = pl.pallas_call(
         z_kernel,
         in_specs=[whole()] * 2,
         out_specs=(whole(), whole()),
         out_shape=(jax.ShapeDtypeStruct((128, 128), jnp.float32), in_vmem(32, 8, 128)),
         compiler_params=room(12),
-    )(fast(raws), fast(block))
+    )(fast(raw), fast(block))
     grams = lax.all_to_all(grams, ("z", "y", "c"), 0, 0, tiled=True)
     proj_v, core_rms = pl.pallas_call(
         v_kernel,

time: 83.3 us -> 81.9 us (0.983)
  blocking collectives: 29.3 us -> 16.5 us
  starting transfers between devices: 22.5 us -> 31.2 us
  waiting for transfers between devices: 18.4 us -> 22.1 us
  Pallas kernels: 11.7 us -> 10.7 us
    all_to_all x1 -> x0, blocking collectives: 16.9 us -> none  [from_all(): return lax.all_to_all(copies, axes, 0, 0, tiled=True)]
    ppermute x0 -> x6, starting transfers between devices: none -> 8.69 us  [sum_all(): lax.ppermute(value, axis, [(i, (i + k) % 4) for i in range(4)])]
    all_to_all x1, blocking collectives: 12.4 us -> 16.5 us  [per_device(): grams = lax.all_to_all(grams, ('z', 'y', 'c'), 0, 0, tiled=True)]
    ppermute x0 -> x6, waiting for transfers between devices: none -> 3.7 us  [sum_all(): lax.ppermute(value, axis, [(i, (i + k) % 4) for i in range(4)])]
  transfers between devices with their start and end apart: 11 -> 17, of which waited for: 9 -> 13; matrix products, arithmetic and copies ran while one was open for 0% -> 0% of each run, Pallas kernels for 1% -> 1%
where the time goes in v7:
time: 81.9 us; the launch traced here: 81.7 us
  starting transfers between devices  31.2 us (38%)
  waiting for transfers between devices  22.1 us (27%)
  blocking collectives  16.5 us (20%)
  Pallas kernels  10.7 us (13%)
    all_to_all x1, blocking collectives, per_device(): grams = lax.all_to_all(grams, ('z', 'y', 'c'), 0, 0, tiled=True)  16.5 us
    ppermute x6, waiting for transfers between devices, gather_sum(): lax.ppermute(slots[k], ('z', 'y', 'c'), hops(k, first))  12.7 us
    ppermute x6, starting transfers between devices, gather_sum(): lax.ppermute(slots[k], ('z', 'y', 'c'), hops(k, first))  12 us
    ppermute x6, starting transfers between devices, sum_all(): lax.ppermute(value, axis, [(i, (i + k) % 4) for i in range(4)])  8.69 us
    ppermute x3, starting transfers between devices, per_device(): lax.ppermute(mine, 'x', [(i, (i + k) % 4) for i in range(4)])  4.89 us
    pallas_call x1, Pallas kernels, per_device(): pl.pallas_call(x_kernel, grid=(8 // step,), in_specs=[pl.BlockSpec(memory...  4.33 us
    ppermute x1, starting transfers between devices, per_device(): raw = raw + lax.ppermute(raw, 'c', swap)  4.1 us
    ppermute x6, waiting for transfers between devices, sum_all(): lax.ppermute(value, axis, [(i, (i + k) % 4) for i in range(4)])  3.7 us
  transfers between devices with their start and end apart: 17, of which 13 were waited for; matrix products, arithmetic and copies ran while one was open for 0% of the time, Pallas kernels for 1%

profile of v7, /device:TPU:1, one launch (start us, length us, event | category | flops | bytes accessed | tf_op | source)
XLA Modules:
  0.0 81.7 jit_solution(17193621035184846970)
XLA Ops:
  0.6 0.0 copy-start
  0.6 4.3 %shard_map.76 = (f32[8,8,32,128]{3,2,1,0:T(8,128)S(1)}, f32[65,32,128]{2,1,0:T(8,128)S(1)}) custom-call(s32[1]{0:T(128)} %bitcast.1.core_ref, f32[16,32]{1,0:T(8,128)} %bitcast.32, f32[32,64]{1,0:T(8,128)} %mine_ref.1, f32[8,32,32,128]{3,2,1,0:T(8,128)} %field_ref.1), custom_call_target="tpu_custom_call" | custom-call | tf_op jit(solution)/shard_map/pallas_call | solution.py:230
  5.0 1.5 %collective-permute-start = (f32[65,32,128]{2,1,0:T(8,128)S(1)}, f32[65,32,128]{2,1,0:T(8,128)S(1)}, u32[]{:S(2)}, u32[]{:S(2)}) collective-permute-start(f32[65,32,128]{2,1,0:T(8,128)S(1)} %get-tuple-element.15), channel_id=1, source_target_pairs={{0,4},{4,0},{1,5},{5,1},{2,6},{6,2},{3,7},{7,3},{8,12},{12,8},{9,1... | collective-permute-start | bytes 3194888 | tf_op jit(solution)/shard_map/ppermute | solution.py:244
  6.5 2.3 %collective-permute-done.got_ref = f32[65,32,128]{2,1,0:T(8,128)S(1)} collective-permute-done((f32[65,32,128]{2,1,0:T(8,128)S(1)}, f32[65,32,128]{2,1,0:T(8,128)S(1)}, u32[]{:S(2)}, u32[]{:S(2)}) %collective-permute-start) | collective-permute-done | bytes 1064992 | tf_op jit(solution)/shard_map/ppermute | solution.py:244
  8.8 0.0 copy-done
  8.8 0.8 %shard_map.77 = f32[4,4,8,32,128]{4,3,2,1,0:T(8,128)S(1)} custom-call(f32[32,64]{1,0:T(8,128)S(1)} %copy-done, f32[8,8,32,128]{3,2,1,0:T(8,128)S(1)} %get-tuple-element.14.keep_ref, f32[65,32,128]{2,1,0:T(8,128)S(1)} %collective-permute-done.got_ref), custom_call_target="tpu_custom_call" | custom-call | tf_op jit(solution)/shard_map/pallas_call | solution.py:253
  9.6 0.1 slice_bitcast_fusion
  9.8 0.0 copy-start.1
  9.8 3.8 %collective-permute-start.1 = (f32[4,8,32,128]{3,2,1,0:T(8,128)S(1)}, f32[4,8,32,128]{3,2,1,0:T(8,128)S(1)}, u32[]{:S(2)}, u32[]{:S(2)}) collective-permute-start(f32[4,8,32,128]{3,2,1,0:T(8,128)S(1)} %get-tuple-element.25), channel_id=1, source_target_pairs={{0,16},{4,68},{8,24},{12,76},{16,0},{20,84},{24,8},{28,92},{32,48}... | collective-permute-start | bytes 1572872 | tf_op jit(solution)/shard_map/ppermute | solution.py:24
  13.5 0.7 collective-permute-start.2
  14.3 0.0 copy-start.2
  14.3 1.9 %collective-permute-start.3 = (f32[4,8,32,128]{3,2,1,0:T(8,128)S(1)}, f32[4,8,32,128]{3,2,1,0:T(8,128)S(1)}, u32[]{:S(2)}, u32[]{:S(2)}) collective-permute-start(f32[4,8,32,128]{3,2,1,0:T(8,128)S(1)} %get-tuple-element.23), channel_id=1, source_target_pairs={{0,24},{4,100},{8,0},{12,108},{16,8},{20,116},{24,16},{28,124},{32... | collective-permute-start | bytes 1572872 | tf_op jit(solution)/shard_map/ppermute | solution.py:24
  16.2 4.2 %collective-permute-done.1 = f32[4,8,32,128]{3,2,1,0:T(8,128)S(1)} collective-permute-done((f32[4,8,32,128]{3,2,1,0:T(8,128)S(1)}, f32[4,8,32,128]{3,2,1,0:T(8,128)S(1)}, u32[]{:S(2)}, u32[]{:S(2)}) %collective-permute-start.1) | collective-permute-done | bytes 524320 | tf_op jit(solution)/shard_map/ppermute | solution.py:24
  20.4 5.6 %collective-permute-done.2 = f32[4,8,32,128]{3,2,1,0:T(8,128)S(1)} collective-permute-done((f32[4,8,32,128]{3,2,1,0:T(8,128)S(1)}, f32[4,8,32,128]{3,2,1,0:T(8,128)S(1)}, u32[]{:S(2)}, u32[]{:S(2)}) %collective-permute-start.2) | collective-permute-done | bytes 524320 | tf_op jit(solution)/shard_map/ppermute | solution.py:24
  26.0 0.6 collective-permute-done.3
  26.6 0.2 fusion.1
  26.9 2.9 %collective-permute-start.4 = (f32[8,32,128]{2,1,0:T(8,128)S(1)}, f32[8,32,128]{2,1,0:T(8,128)S(1)}, u32[]{:S(2)}, u32[]{:S(2)}) collective-permute-start(f32[8,32,128]{2,1,0:T(8,128)S(1)} %get-tuple-element.28), channel_id=1, source_target_pairs={{0,64},{4,20},{8,72},{12,28},{16,80},{20,4},{24,88},{28,12},{32,96... | collective-permute-start | bytes 393224 | tf_op jit(solution)/shard_map/ppermute | solution.py:24
  29.8 0.4 collective-permute-start.5
  30.2 2.3 %collective-permute-start.6 = (f32[8,32,128]{2,1,0:T(8,128)S(1)}, f32[8,32,128]{2,1,0:T(8,128)S(1)}, u32[]{:S(2)}, u32[]{:S(2)}) collective-permute-start(f32[8,32,128]{2,1,0:T(8,128)S(1)} %get-tuple-element.26), channel_id=1, source_target_pairs={{0,96},{4,28},{8,104},{12,4},{16,112},{20,12},{24,120},{28,20},{32... | collective-permute-start | bytes 393224 | tf_op jit(solution)/shard_map/ppermute | solution.py:24
  32.4 0.1 collective-permute-done.4
  32.6 2.2 %collective-permute-done.5 = f32[8,32,128]{2,1,0:T(8,128)S(1)} collective-permute-done((f32[8,32,128]{2,1,0:T(8,128)S(1)}, f32[8,32,128]{2,1,0:T(8,128)S(1)}, u32[]{:S(2)}, u32[]{:S(2)}) %collective-permute-start.5) | collective-permute-done | bytes 131104 | tf_op jit(solution)/shard_map/ppermute | solution.py:24
  34.8 0.0 collective-permute-done.6
  34.8 1.3 %collective-permute-start.7 = (f32[8,32,128]{2,1,0:T(8,128)S(1)}, f32[8,32,128]{2,1,0:T(8,128)S(1)}, u32[]{:S(2)}, u32[]{:S(2)}) collective-permute-start(f32[8,32,128]{2,1,0:T(8,128)S(1)} %fusion.3.mine_ref), channel_id=1, source_target_pairs={{0,1},{1,2},{2,3},{3,0},{4,5},{5,6},{6,7},{7,4},{8,9},{9,10},{10,1... | collective-permute-start | bytes 393224 | tf_op jit(solution)/shard_map/ppermute | solution.py:262
  36.1 2.5 %collective-permute-start.8 = (f32[8,32,128]{2,1,0:T(8,128)S(1)}, f32[8,32,128]{2,1,0:T(8,128)S(1)}, u32[]{:S(2)}, u32[]{:S(2)}) collective-permute-start(f32[8,32,128]{2,1,0:T(8,128)S(1)} %fusion.3.mine_ref), channel_id=1, source_target_pairs={{0,2},{1,3},{2,0},{3,1},{4,6},{5,7},{6,4},{7,5},{8,10},{9,11},{10,... | collective-permute-start | bytes 393224 | tf_op jit(solution)/shard_map/ppermute | solution.py:262
  38.6 1.2 %collective-permute-start.9 = (f32[8,32,128]{2,1,0:T(8,128)S(1)}, f32[8,32,128]{2,1,0:T(8,128)S(1)}, u32[]{:S(2)}, u32[]{:S(2)}) collective-permute-start(f32[8,32,128]{2,1,0:T(8,128)S(1)} %fusion.3.mine_ref), channel_id=1, source_target_pairs={{0,3},{1,0},{2,1},{3,2},{4,7},{5,4},{6,5},{7,6},{8,11},{9,8},{10,9... | collective-permute-start | bytes 393224 | tf_op jit(solution)/shard_map/ppermute | solution.py:262
  39.7 0.0 copy-done.1
  39.7 0.5 shard_map.78.spread_ref
  40.2 0.0 collective-permute-done.7.one_ref
  40.2 2.2 %collective-permute-done.8.two_ref = f32[8,32,128]{2,1,0:T(8,128)S(1)} collective-permute-done((f32[8,32,128]{2,1,0:T(8,128)S(1)}, f32[8,32,128]{2,1,0:T(8,128)S(1)}, u32[]{:S(2)}, u32[]{:S(2)}) %collective-permute-start.8) | collective-permute-done | bytes 131104 | tf_op jit(solution)/shard_map/ppermute | solution.py:262
  42.4 0.3 collective-permute-done.9.three_ref
  42.7 0.0 copy-done.2
  42.7 0.9 %shard_map.79 = (f32[64,128]{1,0:T(8,128)S(1)}, f32[4,8,32,128]{3,2,1,0:T(8,128)S(1)}) custom-call(f32[8,32,128]{2,1,0:T(8,128)S(1)} %fusion.3.mine_ref, f32[8,32,128]{2,1,0:T(8,128)S(1)} %collective-permute-done.7.one_ref, f32[8,32,128]{2,1,0:T(8,128)S(1)} %collective-permute-done.8.two_ref, f32[8,32,128]{2,1,0:T(8,128)S(1)} %collective-permute-done.9.three_ref, ...), custom_call_target="tpu_custom_call" | custom-call | tf_op jit(solution)/shard_map/pallas_call | solution.py:264
  43.5 4.1 %collective-permute-start.10 = (f32[64,128]{1,0:T(8,128)S(1)}, f32[64,128]{1,0:T(8,128)S(1)}, u32[]{:S(2)}, u32[]{:S(2)}) collective-permute-start(f32[64,128]{1,0:T(8,128)S(1)} %get-tuple-element.17), channel_id=1, source_target_pairs={{0,4},{4,0},{1,5},{5,1},{2,6},{6,2},{3,7},{7,3},{8,12},{12,8},{9,1... | collective-permute-start | bytes 98312 | tf_op jit(solution)/shard_map/ppermute | solution.py:271
  47.6 0.9 %collective-permute-done.10 = f32[64,128]{1,0:T(8,128)S(1)} collective-permute-done((f32[64,128]{1,0:T(8,128)S(1)}, f32[64,128]{1,0:T(8,128)S(1)}, u32[]{:S(2)}, u32[]{:S(2)}) %collective-permute-start.10) | collective-permute-done | bytes 32800 | tf_op jit(solution)/shard_map/ppermute | solution.py:271
  48.5 1.8 %collective-permute-start.11 = (f32[64,128]{1,0:T(8,128)S(1)}, f32[64,128]{1,0:T(8,128)S(1)}, u32[]{:S(2)}, u32[]{:S(2)}) collective-permute-start(f32[64,128]{1,0:T(8,128)S(1)} %add.45), channel_id=1, source_target_pairs={{0,16},{8,24},{16,0},{24,8},{1,17},{9,25},{17,1},{25,9},{2,18},{10... | collective-permute-start | bytes 98312 | tf_op jit(solution)/shard_map/ppermute | solution.py:30
  50.3 1.2 %collective-permute-start.12 = (f32[64,128]{1,0:T(8,128)S(1)}, f32[64,128]{1,0:T(8,128)S(1)}, u32[]{:S(2)}, u32[]{:S(2)}) collective-permute-start(f32[64,128]{1,0:T(8,128)S(1)} %add.45), channel_id=1, source_target_pairs={{0,8},{8,16},{16,24},{24,0},{1,9},{9,17},{17,25},{25,1},{2,10},{10... | collective-permute-start | bytes 98312 | tf_op jit(solution)/shard_map/ppermute | solution.py:30
  51.4 1.5 %collective-permute-start.13 = (f32[64,128]{1,0:T(8,128)S(1)}, f32[64,128]{1,0:T(8,128)S(1)}, u32[]{:S(2)}, u32[]{:S(2)}) collective-permute-start(f32[64,128]{1,0:T(8,128)S(1)} %add.45), channel_id=1, source_target_pairs={{0,24},{8,0},{16,8},{24,16},{1,25},{9,1},{17,9},{25,17},{2,26},{10... | collective-permute-start | bytes 98312 | tf_op jit(solution)/shard_map/ppermute | solution.py:30
  52.9 0.0 collective-permute-done.11
  52.9 1.3 %collective-permute-done.12 = f32[64,128]{1,0:T(8,128)S(1)} collective-permute-done((f32[64,128]{1,0:T(8,128)S(1)}, f32[64,128]{1,0:T(8,128)S(1)}, u32[]{:S(2)}, u32[]{:S(2)}) %collective-permute-start.12) | collective-permute-done | bytes 32800 | tf_op jit(solution)/shard_map/ppermute | solution.py:30
  54.2 0.0 collective-permute-done.13
  54.3 1.6 %collective-permute-start.14 = (f32[64,128]{1,0:T(8,128)S(1)}, f32[64,128]{1,0:T(8,128)S(1)}, u32[]{:S(2)}, u32[]{:S(2)}) collective-permute-start(f32[64,128]{1,0:T(8,128)S(1)} %add_add_fusion.1), channel_id=1, source_target_pairs={{0,64},{32,96},{64,0},{96,32},{1,65},{33,97},{65,1},{97,33},{2,66}... | collective-permute-start | bytes 98312 | tf_op jit(solution)/shard_map/ppermute | solution.py:30
  55.8 2.0 %collective-permute-start.15 = (f32[64,128]{1,0:T(8,128)S(1)}, f32[64,128]{1,0:T(8,128)S(1)}, u32[]{:S(2)}, u32[]{:S(2)}) collective-permute-start(f32[64,128]{1,0:T(8,128)S(1)} %add_add_fusion.1), channel_id=1, source_target_pairs={{0,32},{32,64},{64,96},{96,0},{1,33},{33,65},{65,97},{97,1},{2,34}... | collective-permute-start | bytes 98312 | tf_op jit(solution)/shard_map/ppermute | solution.py:30
  57.9 0.7 collective-permute-start.16
  58.5 0.1 collective-permute-done.14
  58.6 1.2 %collective-permute-done.15 = f32[64,128]{1,0:T(8,128)S(1)} collective-permute-done((f32[64,128]{1,0:T(8,128)S(1)}, f32[64,128]{1,0:T(8,128)S(1)}, u32[]{:S(2)}, u32[]{:S(2)}) %collective-permute-start.15) | collective-permute-done | bytes 32800 | tf_op jit(solution)/shard_map/ppermute | solution.py:30
  59.8 1.1 %collective-permute-done.16 = f32[64,128]{1,0:T(8,128)S(1)} collective-permute-done((f32[64,128]{1,0:T(8,128)S(1)}, f32[64,128]{1,0:T(8,128)S(1)}, u32[]{:S(2)}, u32[]{:S(2)}) %collective-permute-start.16) | collective-permute-done | bytes 32800 | tf_op jit(solution)/shard_map/ppermute | solution.py:30
  60.9 2.7 %shard_map.80 = (f32[128,128]{1,0:T(8,128)}, f32[32,8,128]{2,1,0:T(8,128)S(1)}) custom-call(f32[64,128]{1,0:T(8,128)S(1)} %add_add_fusion.rows_ref, f32[4,8,32,128]{3,2,1,0:T(8,128)S(1)} %get-tuple-element.18.block_ref), custom_call_target="tpu_custom_call" | custom-call | tf_op jit(solution)/shard_map/pallas_call | solution.py:273
  63.7 16.5 %all_to_all.5.grams_ref = f32[32,8,128]{2,1,0:T(8,128)S(1)} all-to-all(f32[32,8,128]{2,1,0:T(8,128)S(1)} %get-tuple-element.20), channel_id=1, replica_groups=mesh['z'=4,'y'=4,'c'=2,'x'=4] {'z','y','c'}, dimensions={0} | all-to-all | bytes 262144 | tf_op jit(solution)/shard_map/all_to_all | solution.py:280
  80.2 1.5 %shard_map.81 = (f32[32,32]{1,0:T(8,128)}, f32[1,1]{1,0:T(1,128)}) custom-call(f32[32,8,128]{2,1,0:T(8,128)S(1)} %all_to_all.5.grams_ref, f32[16,32]{1,0:T(8,128)S(1)} %bitcast.30), custom_call_target="tpu_custom_call" | custom-call | tf_op jit(solution)/shard_map/pallas_call | solution.py:281
  (5 shorter events, 0.1 us)
Async XLA Ops:
  0.6 8.2 %copy-start = (f32[32,64]{1,0:T(8,128)S(1)}, f32[32,64]{1,0:T(8,128)}, u32[]{:S(2)}) copy-start(f32[32,64]{1,0:T(8,128)} %mine_ref.1) | copy-start | bytes 24580
  5.0 3.8 %collective-permute-start = (f32[65,32,128]{2,1,0:T(8,128)S(1)}, f32[65,32,128]{2,1,0:T(8,128)S(1)}, u32[]{:S(2)}, u32[]{:S(2)}) collective-permute-start(f32[65,32,128]{2,1,0:T(8,128)S(1)} %get-tuple-element.15), channel_id=1, source_target_pairs={{0,4},{4,0},{1,5},{5,1},{2,6},{6,2},{3,7},{7,3},{8,12},{12,8},{9,1... | collective-permute-start | bytes 3194888 | tf_op jit(solution)/shard_map/ppermute | solution.py:244
  9.8 30.0 %copy-start.1 = (f32[32,16]{0,1:T(8,128)S(1)}, f32[32,16]{0,1:T(8,128)}, u32[]{:S(2)}) copy-start(f32[32,16]{0,1:T(8,128)} %param.9) | copy-start | bytes 6148
  9.8 10.7 %collective-permute-start.1 = (f32[4,8,32,128]{3,2,1,0:T(8,128)S(1)}, f32[4,8,32,128]{3,2,1,0:T(8,128)S(1)}, u32[]{:S(2)}, u32[]{:S(2)}) collective-permute-start(f32[4,8,32,128]{3,2,1,0:T(8,128)S(1)} %get-tuple-element.25), channel_id=1, source_target_pairs={{0,16},{4,68},{8,24},{12,76},{16,0},{20,84},{24,8},{28,92},{32,48}... | collective-permute-start | bytes 1572872 | tf_op jit(solution)/shard_map/ppermute | solution.py:24
  13.5 12.5 %collective-permute-start.2 = (f32[4,8,32,128]{3,2,1,0:T(8,128)S(1)}, f32[4,8,32,128]{3,2,1,0:T(8,128)S(1)}, u32[]{:S(2)}, u32[]{:S(2)}) collective-permute-start(f32[4,8,32,128]{3,2,1,0:T(8,128)S(1)} %get-tuple-element.24), channel_id=1, source_target_pairs={{0,8},{4,36},{8,16},{12,44},{16,24},{20,52},{24,0},{28,60},{32,40}... | collective-permute-start | bytes 1572872 | tf_op jit(solution)/shard_map/ppermute | solution.py:24
  14.3 28.4 %copy-start.2 = (f32[128,64]{0,1:T(8,128)S(1)}, f32[128,64]{0,1:T(8,128)}, u32[]{:S(2)}) copy-start(f32[128,64]{0,1:T(8,128)} %param.8) | copy-start | bytes 98308
  14.3 12.3 %collective-permute-start.3 = (f32[4,8,32,128]{3,2,1,0:T(8,128)S(1)}, f32[4,8,32,128]{3,2,1,0:T(8,128)S(1)}, u32[]{:S(2)}, u32[]{:S(2)}) collective-permute-start(f32[4,8,32,128]{3,2,1,0:T(8,128)S(1)} %get-tuple-element.23), channel_id=1, source_target_pairs={{0,24},{4,100},{8,0},{12,108},{16,8},{20,116},{24,16},{28,124},{32... | collective-permute-start | bytes 1572872 | tf_op jit(solution)/shard_map/ppermute | solution.py:24
  26.9 5.7 %collective-permute-start.4 = (f32[8,32,128]{2,1,0:T(8,128)S(1)}, f32[8,32,128]{2,1,0:T(8,128)S(1)}, u32[]{:S(2)}, u32[]{:S(2)}) collective-permute-start(f32[8,32,128]{2,1,0:T(8,128)S(1)} %get-tuple-element.28), channel_id=1, source_target_pairs={{0,64},{4,20},{8,72},{12,28},{16,80},{20,4},{24,88},{28,12},{32,96... | collective-permute-start | bytes 393224 | tf_op jit(solution)/shard_map/ppermute | solution.py:24
  29.8 5.0 %collective-permute-start.5 = (f32[8,32,128]{2,1,0:T(8,128)S(1)}, f32[8,32,128]{2,1,0:T(8,128)S(1)}, u32[]{:S(2)}, u32[]{:S(2)}) collective-permute-start(f32[8,32,128]{2,1,0:T(8,128)S(1)} %get-tuple-element.27), channel_id=1, source_target_pairs={{0,32},{4,12},{8,40},{12,20},{16,48},{20,28},{24,56},{28,4},{32,64... | collective-permute-start | bytes 393224 | tf_op jit(solution)/shard_map/ppermute | solution.py:24
  30.2 4.6 %collective-permute-start.6 = (f32[8,32,128]{2,1,0:T(8,128)S(1)}, f32[8,32,128]{2,1,0:T(8,128)S(1)}, u32[]{:S(2)}, u32[]{:S(2)}) collective-permute-start(f32[8,32,128]{2,1,0:T(8,128)S(1)} %get-tuple-element.26), channel_id=1, source_target_pairs={{0,96},{4,28},{8,104},{12,4},{16,112},{20,12},{24,120},{28,20},{32... | collective-permute-start | bytes 393224 | tf_op jit(solution)/shard_map/ppermute | solution.py:24
  34.8 5.4 %collective-permute-start.7 = (f32[8,32,128]{2,1,0:T(8,128)S(1)}, f32[8,32,128]{2,1,0:T(8,128)S(1)}, u32[]{:S(2)}, u32[]{:S(2)}) collective-permute-start(f32[8,32,128]{2,1,0:T(8,128)S(1)} %fusion.3.mine_ref), channel_id=1, source_target_pairs={{0,1},{1,2},{2,3},{3,0},{4,5},{5,6},{6,7},{7,4},{8,9},{9,10},{10,1... | collective-permute-start | bytes 393224 | tf_op jit(solution)/shard_map/ppermute | solution.py:262
  36.1 6.3 %collective-permute-start.8 = (f32[8,32,128]{2,1,0:T(8,128)S(1)}, f32[8,32,128]{2,1,0:T(8,128)S(1)}, u32[]{:S(2)}, u32[]{:S(2)}) collective-permute-start(f32[8,32,128]{2,1,0:T(8,128)S(1)} %fusion.3.mine_ref), channel_id=1, source_target_pairs={{0,2},{1,3},{2,0},{3,1},{4,6},{5,7},{6,4},{7,5},{8,10},{9,11},{10,... | collective-permute-start | bytes 393224 | tf_op jit(solution)/shard_map/ppermute | solution.py:262
  38.6 4.1 %collective-permute-start.9 = (f32[8,32,128]{2,1,0:T(8,128)S(1)}, f32[8,32,128]{2,1,0:T(8,128)S(1)}, u32[]{:S(2)}, u32[]{:S(2)}) collective-permute-start(f32[8,32,128]{2,1,0:T(8,128)S(1)} %fusion.3.mine_ref), channel_id=1, source_target_pairs={{0,3},{1,0},{2,1},{3,2},{4,7},{5,4},{6,5},{7,6},{8,11},{9,8},{10,9... | collective-permute-start | bytes 393224 | tf_op jit(solution)/shard_map/ppermute | solution.py:262
  43.5 5.0 %collective-permute-start.10 = (f32[64,128]{1,0:T(8,128)S(1)}, f32[64,128]{1,0:T(8,128)S(1)}, u32[]{:S(2)}, u32[]{:S(2)}) collective-permute-start(f32[64,128]{1,0:T(8,128)S(1)} %get-tuple-element.17), channel_id=1, source_target_pairs={{0,4},{4,0},{1,5},{5,1},{2,6},{6,2},{3,7},{7,3},{8,12},{12,8},{9,1... | collective-permute-start | bytes 98312 | tf_op jit(solution)/shard_map/ppermute | solution.py:271
  48.5 4.4 %collective-permute-start.11 = (f32[64,128]{1,0:T(8,128)S(1)}, f32[64,128]{1,0:T(8,128)S(1)}, u32[]{:S(2)}, u32[]{:S(2)}) collective-permute-start(f32[64,128]{1,0:T(8,128)S(1)} %add.45), channel_id=1, source_target_pairs={{0,16},{8,24},{16,0},{24,8},{1,17},{9,25},{17,1},{25,9},{2,18},{10... | collective-permute-start | bytes 98312 | tf_op jit(solution)/shard_map/ppermute | solution.py:30
  50.3 4.0 %collective-permute-start.12 = (f32[64,128]{1,0:T(8,128)S(1)}, f32[64,128]{1,0:T(8,128)S(1)}, u32[]{:S(2)}, u32[]{:S(2)}) collective-permute-start(f32[64,128]{1,0:T(8,128)S(1)} %add.45), channel_id=1, source_target_pairs={{0,8},{8,16},{16,24},{24,0},{1,9},{9,17},{17,25},{25,1},{2,10},{10... | collective-permute-start | bytes 98312 | tf_op jit(solution)/shard_map/ppermute | solution.py:30
  51.4 2.8 %collective-permute-start.13 = (f32[64,128]{1,0:T(8,128)S(1)}, f32[64,128]{1,0:T(8,128)S(1)}, u32[]{:S(2)}, u32[]{:S(2)}) collective-permute-start(f32[64,128]{1,0:T(8,128)S(1)} %add.45), channel_id=1, source_target_pairs={{0,24},{8,0},{16,8},{24,16},{1,25},{9,1},{17,9},{25,17},{2,26},{10... | collective-permute-start | bytes 98312 | tf_op jit(solution)/shard_map/ppermute | solution.py:30
  54.3 4.3 %collective-permute-start.14 = (f32[64,128]{1,0:T(8,128)S(1)}, f32[64,128]{1,0:T(8,128)S(1)}, u32[]{:S(2)}, u32[]{:S(2)}) collective-permute-start(f32[64,128]{1,0:T(8,128)S(1)} %add_add_fusion.1), channel_id=1, source_target_pairs={{0,64},{32,96},{64,0},{96,32},{1,65},{33,97},{65,1},{97,33},{2,66}... | collective-permute-start | bytes 98312 | tf_op jit(solution)/shard_map/ppermute | solution.py:30
  55.8 4.0 %collective-permute-start.15 = (f32[64,128]{1,0:T(8,128)S(1)}, f32[64,128]{1,0:T(8,128)S(1)}, u32[]{:S(2)}, u32[]{:S(2)}) collective-permute-start(f32[64,128]{1,0:T(8,128)S(1)} %add_add_fusion.1), channel_id=1, source_target_pairs={{0,32},{32,64},{64,96},{96,0},{1,33},{33,65},{65,97},{97,1},{2,34}... | collective-permute-start | bytes 98312 | tf_op jit(solution)/shard_map/ppermute | solution.py:30
  57.9 3.1 %collective-permute-start.16 = (f32[64,128]{1,0:T(8,128)S(1)}, f32[64,128]{1,0:T(8,128)S(1)}, u32[]{:S(2)}, u32[]{:S(2)}) collective-permute-start(f32[64,128]{1,0:T(8,128)S(1)} %add_add_fusion.1), channel_id=1, source_target_pairs={{0,96},{32,0},{64,32},{96,64},{1,97},{33,1},{65,33},{97,65},{2,98}... | collective-permute-start | bytes 98312 | tf_op jit(solution)/shard_map/ppermute | solution.py:30

commit v8 on v7

--- a/solution.py
+++ b/solution.py
@@ -72,30 +72,35 @@
     return jnp.where((row & 7) == (col & 7), full, 0.0)
 
 
-def x_kernel(core_ref, factor_ref, factor_y_ref, field_ref, keep_ref, send_ref, both_ref):
-    step = pl.program_id(0)
-
-    @pl.when(step == 0)
-    def _():
-        high, low = halves(spread(factor_ref[...], core_ref[0] * 8))
-        both_ref[0:128, :] = high
-        both_ref[128:256, :] = low
-        send_ref[64, :, 0:64] = factor_y_ref[...]
-        send_ref[64, :, 64:128] = factor_y_ref[...]
-
-    count = field_ref.shape[0]
-    for v in range(count):
+def x_kernel(factor_ref, factor_y_ref, field_ref, keep_ref, send_ref, held, held_x, held_y, arrived, small):
+    copies = [
+        pltpu.make_async_copy(field_ref.at[4 * i:4 * i + 4], held.at[4 * i:4 * i + 4], arrived.at[i])
+        for i in range(2)
+    ]
+    copy_x = pltpu.make_async_copy(factor_ref, held_x, small.at[0])
+    copy_y = pltpu.make_async_copy(factor_y_ref, held_y, small.at[1])
+    for copy in [copy_x, copy_y] + copies:
+        copy.start()
+    copy_x.wait()
+    factor_high, factor_low = halves(spread(held_x[...], lax.axis_index("c") * 8))
+    both = jnp.concatenate([factor_high, factor_low], axis=0)
+    copy_y.wait()
+    send_ref[64, :, 0:64] = held_y[...]
+    send_ref[64, :, 64:128] = held_y[...]
+    for v in range(8):
+        if v % 4 == 0:
+            copies[v // 4].wait()
         tile = jnp.concatenate(
-            [field_ref[v, :, 8 * t:8 * t + 8, :].reshape(256, 128) for t in range(4)], axis=1
+            [held[v, :, 8 * t:8 * t + 8, :].reshape(256, 128) for t in range(4)], axis=1
         )
         high, low = halves(tile)
-        first = dot16(both_ref[...], high)
-        total = first[:128] + (first[128:] + dot16(both_ref[0:128, :], low))
+        first = dot16(both, high)
+        total = first[:128] + (first[128:] + dot16(factor_high, low))
         for t in range(4):
             cut = total[:, 128 * t:128 * t + 128].reshape(16, 8, 128)
-            keep_ref[:, step * count + v, 8 * t:8 * t + 8, :] = cut[:8]
+            keep_ref[:, v, 8 * t:8 * t + 8, :] = cut[:8]
             for a in range(8):
-                send_ref[8 * a + step * count + v, 8 * t:8 * t + 8, :] = cut[8 + a]
+                send_ref[8 * a + v, 8 * t:8 * t + 8, :] = cut[8 + a]
 
 
 def y_kernel(mine_ref, keep_ref, got_ref, slots_ref):
@@ -225,22 +230,20 @@
 
 
 def per_device(field, factor_x, factor_y, factor_z, factor_v):
-    core = lax.axis_index("c").astype(jnp.int32).reshape(1)
-    step = 2
     keep, send = pl.pallas_call(
         x_kernel,
-        grid=(8 // step,),
-        in_specs=[
-            pl.BlockSpec(memory_space=pltpu.SMEM),
-            whole(),
-            whole(),
-            pl.BlockSpec((step, 32, 32, 128), lambda i: (i, 0, 0, 0)),
-        ],
+        in_specs=[pl.BlockSpec(memory_space=pltpu.HBM)] * 3,
         out_specs=(whole(), whole()),
         out_shape=(in_vmem(8, 8, 32, 128), in_vmem(65, 32, 128)),
-        scratch_shapes=[pltpu.VMEM((256, 256), jnp.bfloat16)],
-        compiler_params=room(12),
-    )(core, slow(factor_x.T), slow(factor_y), slow(field))
+        scratch_shapes=[
+            in_vmem(8, 32, 32, 128),
+            in_vmem(16, 32),
+            in_vmem(32, 64),
+            pltpu.SemaphoreType.DMA((2,)),
+            pltpu.SemaphoreType.DMA((2,)),
+        ],
+        compiler_params=room(12),
+    )(slow(factor_x.T), slow(factor_y), slow(field))
     got = lax.ppermute(send, "c", swap)
     late_v, keep = lax.optimization_barrier((factor_v.T, keep))
     wide_v = pl.pallas_call(

time: 81.9 us -> 80.8 us (0.987)
  Pallas kernels: 10.7 us -> 9.66 us
    pallas_call x1, Pallas kernels: 4.33 us -> 3.25 us  [per_device(): pl.pallas_call(x_kernel, in_specs=[pl.BlockSpec(memory_space=pltpu.HBM)]...]
where the time goes in v8:
time: 80.8 us; the launch traced here: 80.6 us
  starting transfers between devices  31.2 us (39%)
  waiting for transfers between devices  22.1 us (27%)
  blocking collectives  16.5 us (20%)
  Pallas kernels  9.66 us (12%)
    all_to_all x1, blocking collectives, per_device(): grams = lax.all_to_all(grams, ('z', 'y', 'c'), 0, 0, tiled=True)  16.5 us
    ppermute x6, waiting for transfers between devices, gather_sum(): lax.ppermute(slots[k], ('z', 'y', 'c'), hops(k, first))  12.7 us
    ppermute x6, starting transfers between devices, gather_sum(): lax.ppermute(slots[k], ('z', 'y', 'c'), hops(k, first))  12 us
    ppermute x6, starting transfers between devices, sum_all(): lax.ppermute(value, axis, [(i, (i + k) % 4) for i in range(4)])  8.69 us
    ppermute x3, starting transfers between devices, per_device(): lax.ppermute(mine, 'x', [(i, (i + k) % 4) for i in range(4)])  4.88 us
    ppermute x1, starting transfers between devices, per_device(): raw = raw + lax.ppermute(raw, 'c', swap)  4.1 us
    ppermute x6, waiting for transfers between devices, sum_all(): lax.ppermute(value, axis, [(i, (i + k) % 4) for i in range(4)])  3.7 us
    pallas_call x1, Pallas kernels, per_device(): pl.pallas_call(x_kernel, in_specs=[pl.BlockSpec(memory_space=pltpu.HBM)]...  3.25 us
  transfers between devices with their start and end apart: 17, of which 13 were waited for; matrix products, arithmetic and copies ran while one was open for 0% of the time, Pallas kernels for 1%

profile of v8, /device:TPU:1, one launch (start us, length us, event | category | flops | bytes accessed | tf_op | source)
XLA Modules:
  0.0 80.6 jit_solution(7972627796137708547)
XLA Ops:
  0.6 0.0 copy-start
  0.6 3.2 %shard_map.76 = (f32[8,8,32,128]{3,2,1,0:T(8,128)S(1)}, f32[65,32,128]{2,1,0:T(8,128)S(1)}) custom-call(f32[16,32]{1,0:T(8,128)} %bitcast.31, f32[32,64]{1,0:T(8,128)} %mine_ref.1, f32[8,32,32,128]{3,2,1,0:T(8,128)} %field_ref.1), custom_call_target="tpu_custom_call" | custom-call | tf_op jit(solution)/shard_map/pallas_call | solution.py:233
  3.9 1.5 %collective-permute-start = (f32[65,32,128]{2,1,0:T(8,128)S(1)}, f32[65,32,128]{2,1,0:T(8,128)S(1)}, u32[]{:S(2)}, u32[]{:S(2)}) collective-permute-start(f32[65,32,128]{2,1,0:T(8,128)S(1)} %get-tuple-element.15), channel_id=1, source_target_pairs={{0,4},{4,0},{1,5},{5,1},{2,6},{6,2},{3,7},{7,3},{8,12},{12,8},{9,1... | collective-permute-start | bytes 3194888 | tf_op jit(solution)/shard_map/ppermute | solution.py:247
  5.4 2.3 %collective-permute-done.got_ref = f32[65,32,128]{2,1,0:T(8,128)S(1)} collective-permute-done((f32[65,32,128]{2,1,0:T(8,128)S(1)}, f32[65,32,128]{2,1,0:T(8,128)S(1)}, u32[]{:S(2)}, u32[]{:S(2)}) %collective-permute-start) | collective-permute-done | bytes 1064992 | tf_op jit(solution)/shard_map/ppermute | solution.py:247
  7.7 0.0 copy-done
  7.7 0.8 %shard_map.77 = f32[4,4,8,32,128]{4,3,2,1,0:T(8,128)S(1)} custom-call(f32[32,64]{1,0:T(8,128)S(1)} %copy-done, f32[8,8,32,128]{3,2,1,0:T(8,128)S(1)} %get-tuple-element.14.keep_ref, f32[65,32,128]{2,1,0:T(8,128)S(1)} %collective-permute-done.got_ref), custom_call_target="tpu_custom_call" | custom-call | tf_op jit(solution)/shard_map/pallas_call | solution.py:256
  8.5 0.1 slice_bitcast_fusion
  8.7 0.0 copy-start.1
  8.7 3.8 %collective-permute-start.1 = (f32[4,8,32,128]{3,2,1,0:T(8,128)S(1)}, f32[4,8,32,128]{3,2,1,0:T(8,128)S(1)}, u32[]{:S(2)}, u32[]{:S(2)}) collective-permute-start(f32[4,8,32,128]{3,2,1,0:T(8,128)S(1)} %get-tuple-element.25), channel_id=1, source_target_pairs={{0,16},{4,68},{8,24},{12,76},{16,0},{20,84},{24,8},{28,92},{32,48}... | collective-permute-start | bytes 1572872 | tf_op jit(solution)/shard_map/ppermute | solution.py:24
  12.5 0.7 collective-permute-start.2
  13.2 0.0 copy-start.2
  13.2 2.0 %collective-permute-start.3 = (f32[4,8,32,128]{3,2,1,0:T(8,128)S(1)}, f32[4,8,32,128]{3,2,1,0:T(8,128)S(1)}, u32[]{:S(2)}, u32[]{:S(2)}) collective-permute-start(f32[4,8,32,128]{3,2,1,0:T(8,128)S(1)} %get-tuple-element.23), channel_id=1, source_target_pairs={{0,24},{4,100},{8,0},{12,108},{16,8},{20,116},{24,16},{28,124},{32... | collective-permute-start | bytes 1572872 | tf_op jit(solution)/shard_map/ppermute | solution.py:24
  15.1 4.2 %collective-permute-done.1 = f32[4,8,32,128]{3,2,1,0:T(8,128)S(1)} collective-permute-done((f32[4,8,32,128]{3,2,1,0:T(8,128)S(1)}, f32[4,8,32,128]{3,2,1,0:T(8,128)S(1)}, u32[]{:S(2)}, u32[]{:S(2)}) %collective-permute-start.1) | collective-permute-done | bytes 524320 | tf_op jit(solution)/shard_map/ppermute | solution.py:24
  19.4 5.6 %collective-permute-done.2 = f32[4,8,32,128]{3,2,1,0:T(8,128)S(1)} collective-permute-done((f32[4,8,32,128]{3,2,1,0:T(8,128)S(1)}, f32[4,8,32,128]{3,2,1,0:T(8,128)S(1)}, u32[]{:S(2)}, u32[]{:S(2)}) %collective-permute-start.2) | collective-permute-done | bytes 524320 | tf_op jit(solution)/shard_map/ppermute | solution.py:24
  24.9 0.6 collective-permute-done.3
  25.5 0.2 fusion.1
  25.8 2.9 %collective-permute-start.4 = (f32[8,32,128]{2,1,0:T(8,128)S(1)}, f32[8,32,128]{2,1,0:T(8,128)S(1)}, u32[]{:S(2)}, u32[]{:S(2)}) collective-permute-start(f32[8,32,128]{2,1,0:T(8,128)S(1)} %get-tuple-element.28), channel_id=1, source_target_pairs={{0,64},{4,20},{8,72},{12,28},{16,80},{20,4},{24,88},{28,12},{32,96... | collective-permute-start | bytes 393224 | tf_op jit(solution)/shard_map/ppermute | solution.py:24
  28.7 0.4 collective-permute-start.5
  29.1 2.3 %collective-permute-start.6 = (f32[8,32,128]{2,1,0:T(8,128)S(1)}, f32[8,32,128]{2,1,0:T(8,128)S(1)}, u32[]{:S(2)}, u32[]{:S(2)}) collective-permute-start(f32[8,32,128]{2,1,0:T(8,128)S(1)} %get-tuple-element.26), channel_id=1, source_target_pairs={{0,96},{4,28},{8,104},{12,4},{16,112},{20,12},{24,120},{28,20},{32... | collective-permute-start | bytes 393224 | tf_op jit(solution)/shard_map/ppermute | solution.py:24
  31.3 0.1 collective-permute-done.4
  31.5 2.2 %collective-permute-done.5 = f32[8,32,128]{2,1,0:T(8,128)S(1)} collective-permute-done((f32[8,32,128]{2,1,0:T(8,128)S(1)}, f32[8,32,128]{2,1,0:T(8,128)S(1)}, u32[]{:S(2)}, u32[]{:S(2)}) %collective-permute-start.5) | collective-permute-done | bytes 131104 | tf_op jit(solution)/shard_map/ppermute | solution.py:24
  33.7 0.0 collective-permute-done.6
  33.7 1.3 %collective-permute-start.7 = (f32[8,32,128]{2,1,0:T(8,128)S(1)}, f32[8,32,128]{2,1,0:T(8,128)S(1)}, u32[]{:S(2)}, u32[]{:S(2)}) collective-permute-start(f32[8,32,128]{2,1,0:T(8,128)S(1)} %fusion.3.mine_ref), channel_id=1, source_target_pairs={{0,1},{1,2},{2,3},{3,0},{4,5},{5,6},{6,7},{7,4},{8,9},{9,10},{10,1... | collective-permute-start | bytes 393224 | tf_op jit(solution)/shard_map/ppermute | solution.py:265
  35.0 2.5 %collective-permute-start.8 = (f32[8,32,128]{2,1,0:T(8,128)S(1)}, f32[8,32,128]{2,1,0:T(8,128)S(1)}, u32[]{:S(2)}, u32[]{:S(2)}) collective-permute-start(f32[8,32,128]{2,1,0:T(8,128)S(1)} %fusion.3.mine_ref), channel_id=1, source_target_pairs={{0,2},{1,3},{2,0},{3,1},{4,6},{5,7},{6,4},{7,5},{8,10},{9,11},{10,... | collective-permute-start | bytes 393224 | tf_op jit(solution)/shard_map/ppermute | solution.py:265
  37.5 1.1 %collective-permute-start.9 = (f32[8,32,128]{2,1,0:T(8,128)S(1)}, f32[8,32,128]{2,1,0:T(8,128)S(1)}, u32[]{:S(2)}, u32[]{:S(2)}) collective-permute-start(f32[8,32,128]{2,1,0:T(8,128)S(1)} %fusion.3.mine_ref), channel_id=1, source_target_pairs={{0,3},{1,0},{2,1},{3,2},{4,7},{5,4},{6,5},{7,6},{8,11},{9,8},{10,9... | collective-permute-start | bytes 393224 | tf_op jit(solution)/shard_map/ppermute | solution.py:265
  38.6 0.0 copy-done.1
  38.6 0.5 shard_map.78.spread_ref
  39.1 0.0 collective-permute-done.7.one_ref
  39.1 2.2 %collective-permute-done.8.two_ref = f32[8,32,128]{2,1,0:T(8,128)S(1)} collective-permute-done((f32[8,32,128]{2,1,0:T(8,128)S(1)}, f32[8,32,128]{2,1,0:T(8,128)S(1)}, u32[]{:S(2)}, u32[]{:S(2)}) %collective-permute-start.8) | collective-permute-done | bytes 131104 | tf_op jit(solution)/shard_map/ppermute | solution.py:265
  41.3 0.3 collective-permute-done.9.three_ref
  41.6 0.0 copy-done.2
  41.6 0.9 %shard_map.79 = (f32[64,128]{1,0:T(8,128)S(1)}, f32[4,8,32,128]{3,2,1,0:T(8,128)S(1)}) custom-call(f32[8,32,128]{2,1,0:T(8,128)S(1)} %fusion.3.mine_ref, f32[8,32,128]{2,1,0:T(8,128)S(1)} %collective-permute-done.7.one_ref, f32[8,32,128]{2,1,0:T(8,128)S(1)} %collective-permute-done.8.two_ref, f32[8,32,128]{2,1,0:T(8,128)S(1)} %collective-permute-done.9.three_ref, ...), custom_call_target="tpu_custom_call" | custom-call | tf_op jit(solution)/shard_map/pallas_call | solution.py:267
  42.5 4.1 %collective-permute-start.10 = (f32[64,128]{1,0:T(8,128)S(1)}, f32[64,128]{1,0:T(8,128)S(1)}, u32[]{:S(2)}, u32[]{:S(2)}) collective-permute-start(f32[64,128]{1,0:T(8,128)S(1)} %get-tuple-element.17), channel_id=1, source_target_pairs={{0,4},{4,0},{1,5},{5,1},{2,6},{6,2},{3,7},{7,3},{8,12},{12,8},{9,1... | collective-permute-start | bytes 98312 | tf_op jit(solution)/shard_map/ppermute | solution.py:274
  46.6 0.9 %collective-permute-done.10 = f32[64,128]{1,0:T(8,128)S(1)} collective-permute-done((f32[64,128]{1,0:T(8,128)S(1)}, f32[64,128]{1,0:T(8,128)S(1)}, u32[]{:S(2)}, u32[]{:S(2)}) %collective-permute-start.10) | collective-permute-done | bytes 32800 | tf_op jit(solution)/shard_map/ppermute | solution.py:274
  47.4 1.7 %collective-permute-start.11 = (f32[64,128]{1,0:T(8,128)S(1)}, f32[64,128]{1,0:T(8,128)S(1)}, u32[]{:S(2)}, u32[]{:S(2)}) collective-permute-start(f32[64,128]{1,0:T(8,128)S(1)} %add.45), channel_id=1, source_target_pairs={{0,16},{8,24},{16,0},{24,8},{1,17},{9,25},{17,1},{25,9},{2,18},{10... | collective-permute-start | bytes 98312 | tf_op jit(solution)/shard_map/ppermute | solution.py:30
  49.2 1.2 %collective-permute-start.12 = (f32[64,128]{1,0:T(8,128)S(1)}, f32[64,128]{1,0:T(8,128)S(1)}, u32[]{:S(2)}, u32[]{:S(2)}) collective-permute-start(f32[64,128]{1,0:T(8,128)S(1)} %add.45), channel_id=1, source_target_pairs={{0,8},{8,16},{16,24},{24,0},{1,9},{9,17},{17,25},{25,1},{2,10},{10... | collective-permute-start | bytes 98312 | tf_op jit(solution)/shard_map/ppermute | solution.py:30
  50.4 1.5 %collective-permute-start.13 = (f32[64,128]{1,0:T(8,128)S(1)}, f32[64,128]{1,0:T(8,128)S(1)}, u32[]{:S(2)}, u32[]{:S(2)}) collective-permute-start(f32[64,128]{1,0:T(8,128)S(1)} %add.45), channel_id=1, source_target_pairs={{0,24},{8,0},{16,8},{24,16},{1,25},{9,1},{17,9},{25,17},{2,26},{10... | collective-permute-start | bytes 98312 | tf_op jit(solution)/shard_map/ppermute | solution.py:30
  51.9 0.0 collective-permute-done.11
  51.9 1.3 %collective-permute-done.12 = f32[64,128]{1,0:T(8,128)S(1)} collective-permute-done((f32[64,128]{1,0:T(8,128)S(1)}, f32[64,128]{1,0:T(8,128)S(1)}, u32[]{:S(2)}, u32[]{:S(2)}) %collective-permute-start.12) | collective-permute-done | bytes 32800 | tf_op jit(solution)/shard_map/ppermute | solution.py:30
  53.2 0.0 collective-permute-done.13
  53.2 1.6 %collective-permute-start.14 = (f32[64,128]{1,0:T(8,128)S(1)}, f32[64,128]{1,0:T(8,128)S(1)}, u32[]{:S(2)}, u32[]{:S(2)}) collective-permute-start(f32[64,128]{1,0:T(8,128)S(1)} %add_add_fusion.1), channel_id=1, source_target_pairs={{0,64},{32,96},{64,0},{96,32},{1,65},{33,97},{65,1},{97,33},{2,66}... | collective-permute-start | bytes 98312 | tf_op jit(solution)/shard_map/ppermute | solution.py:30
  54.8 2.0 %collective-permute-start.15 = (f32[64,128]{1,0:T(8,128)S(1)}, f32[64,128]{1,0:T(8,128)S(1)}, u32[]{:S(2)}, u32[]{:S(2)}) collective-permute-start(f32[64,128]{1,0:T(8,128)S(1)} %add_add_fusion.1), channel_id=1, source_target_pairs={{0,32},{32,64},{64,96},{96,0},{1,33},{33,65},{65,97},{97,1},{2,34}... | collective-permute-start | bytes 98312 | tf_op jit(solution)/shard_map/ppermute | solution.py:30
  56.8 0.7 collective-permute-start.16
  57.4 0.1 collective-permute-done.14
  57.5 1.2 %collective-permute-done.15 = f32[64,128]{1,0:T(8,128)S(1)} collective-permute-done((f32[64,128]{1,0:T(8,128)S(1)}, f32[64,128]{1,0:T(8,128)S(1)}, u32[]{:S(2)}, u32[]{:S(2)}) %collective-permute-start.15) | collective-permute-done | bytes 32800 | tf_op jit(solution)/shard_map/ppermute | solution.py:30
  58.7 1.1 %collective-permute-done.16 = f32[64,128]{1,0:T(8,128)S(1)} collective-permute-done((f32[64,128]{1,0:T(8,128)S(1)}, f32[64,128]{1,0:T(8,128)S(1)}, u32[]{:S(2)}, u32[]{:S(2)}) %collective-permute-start.16) | collective-permute-done | bytes 32800 | tf_op jit(solution)/shard_map/ppermute | solution.py:30
  59.9 2.7 %shard_map.80 = (f32[128,128]{1,0:T(8,128)}, f32[32,8,128]{2,1,0:T(8,128)S(1)}) custom-call(f32[64,128]{1,0:T(8,128)S(1)} %add_add_fusion.rows_ref, f32[4,8,32,128]{3,2,1,0:T(8,128)S(1)} %get-tuple-element.18.block_ref), custom_call_target="tpu_custom_call" | custom-call | tf_op jit(solution)/shard_map/pallas_call | solution.py:276
  62.6 16.5 %all_to_all.5.grams_ref = f32[32,8,128]{2,1,0:T(8,128)S(1)} all-to-all(f32[32,8,128]{2,1,0:T(8,128)S(1)} %get-tuple-element.20), channel_id=1, replica_groups=mesh['z'=4,'y'=4,'c'=2,'x'=4] {'z','y','c'}, dimensions={0} | all-to-all | bytes 262144 | tf_op jit(solution)/shard_map/all_to_all | solution.py:283
  79.1 1.5 %shard_map.81 = (f32[32,32]{1,0:T(8,128)}, f32[1,1]{1,0:T(1,128)}) custom-call(f32[32,8,128]{2,1,0:T(8,128)S(1)} %all_to_all.5.grams_ref, f32[16,32]{1,0:T(8,128)S(1)} %bitcast.29), custom_call_target="tpu_custom_call" | custom-call | tf_op jit(solution)/shard_map/pallas_call | solution.py:284
  (5 shorter events, 0.1 us)
Async XLA Ops:
  0.6 7.1 %copy-start = (f32[32,64]{1,0:T(8,128)S(1)}, f32[32,64]{1,0:T(8,128)}, u32[]{:S(2)}) copy-start(f32[32,64]{1,0:T(8,128)} %mine_ref.1) | copy-start | bytes 24580
  3.9 3.8 %collective-permute-start = (f32[65,32,128]{2,1,0:T(8,128)S(1)}, f32[65,32,128]{2,1,0:T(8,128)S(1)}, u32[]{:S(2)}, u32[]{:S(2)}) collective-permute-start(f32[65,32,128]{2,1,0:T(8,128)S(1)} %get-tuple-element.15), channel_id=1, source_target_pairs={{0,4},{4,0},{1,5},{5,1},{2,6},{6,2},{3,7},{7,3},{8,12},{12,8},{9,1... | collective-permute-start | bytes 3194888 | tf_op jit(solution)/shard_map/ppermute | solution.py:247
  8.7 30.0 %copy-start.1 = (f32[32,16]{0,1:T(8,128)S(1)}, f32[32,16]{0,1:T(8,128)}, u32[]{:S(2)}) copy-start(f32[32,16]{0,1:T(8,128)} %param.9) | copy-start | bytes 6148
  8.7 10.7 %collective-permute-start.1 = (f32[4,8,32,128]{3,2,1,0:T(8,128)S(1)}, f32[4,8,32,128]{3,2,1,0:T(8,128)S(1)}, u32[]{:S(2)}, u32[]{:S(2)}) collective-permute-start(f32[4,8,32,128]{3,2,1,0:T(8,128)S(1)} %get-tuple-element.25), channel_id=1, source_target_pairs={{0,16},{4,68},{8,24},{12,76},{16,0},{20,84},{24,8},{28,92},{32,48}... | collective-permute-start | bytes 1572872 | tf_op jit(solution)/shard_map/ppermute | solution.py:24
  12.5 12.5 %collective-permute-start.2 = (f32[4,8,32,128]{3,2,1,0:T(8,128)S(1)}, f32[4,8,32,128]{3,2,1,0:T(8,128)S(1)}, u32[]{:S(2)}, u32[]{:S(2)}) collective-permute-start(f32[4,8,32,128]{3,2,1,0:T(8,128)S(1)} %get-tuple-element.24), channel_id=1, source_target_pairs={{0,8},{4,36},{8,16},{12,44},{16,24},{20,52},{24,0},{28,60},{32,40}... | collective-permute-start | bytes 1572872 | tf_op jit(solution)/shard_map/ppermute | solution.py:24
  13.2 28.4 %copy-start.2 = (f32[128,64]{0,1:T(8,128)S(1)}, f32[128,64]{0,1:T(8,128)}, u32[]{:S(2)}) copy-start(f32[128,64]{0,1:T(8,128)} %param.8) | copy-start | bytes 98308
  13.2 12.3 %collective-permute-start.3 = (f32[4,8,32,128]{3,2,1,0:T(8,128)S(1)}, f32[4,8,32,128]{3,2,1,0:T(8,128)S(1)}, u32[]{:S(2)}, u32[]{:S(2)}) collective-permute-start(f32[4,8,32,128]{3,2,1,0:T(8,128)S(1)} %get-tuple-element.23), channel_id=1, source_target_pairs={{0,24},{4,100},{8,0},{12,108},{16,8},{20,116},{24,16},{28,124},{32... | collective-permute-start | bytes 1572872 | tf_op jit(solution)/shard_map/ppermute | solution.py:24
  25.8 5.7 %collective-permute-start.4 = (f32[8,32,128]{2,1,0:T(8,128)S(1)}, f32[8,32,128]{2,1,0:T(8,128)S(1)}, u32[]{:S(2)}, u32[]{:S(2)}) collective-permute-start(f32[8,32,128]{2,1,0:T(8,128)S(1)} %get-tuple-element.28), channel_id=1, source_target_pairs={{0,64},{4,20},{8,72},{12,28},{16,80},{20,4},{24,88},{28,12},{32,96... | collective-permute-start | bytes 393224 | tf_op jit(solution)/shard_map/ppermute | solution.py:24
  28.7 5.0 %collective-permute-start.5 = (f32[8,32,128]{2,1,0:T(8,128)S(1)}, f32[8,32,128]{2,1,0:T(8,128)S(1)}, u32[]{:S(2)}, u32[]{:S(2)}) collective-permute-start(f32[8,32,128]{2,1,0:T(8,128)S(1)} %get-tuple-element.27), channel_id=1, source_target_pairs={{0,32},{4,12},{8,40},{12,20},{16,48},{20,28},{24,56},{28,4},{32,64... | collective-permute-start | bytes 393224 | tf_op jit(solution)/shard_map/ppermute | solution.py:24
  29.1 4.6 %collective-permute-start.6 = (f32[8,32,128]{2,1,0:T(8,128)S(1)}, f32[8,32,128]{2,1,0:T(8,128)S(1)}, u32[]{:S(2)}, u32[]{:S(2)}) collective-permute-start(f32[8,32,128]{2,1,0:T(8,128)S(1)} %get-tuple-element.26), channel_id=1, source_target_pairs={{0,96},{4,28},{8,104},{12,4},{16,112},{20,12},{24,120},{28,20},{32... | collective-permute-start | bytes 393224 | tf_op jit(solution)/shard_map/ppermute | solution.py:24
  33.7 5.4 %collective-permute-start.7 = (f32[8,32,128]{2,1,0:T(8,128)S(1)}, f32[8,32,128]{2,1,0:T(8,128)S(1)}, u32[]{:S(2)}, u32[]{:S(2)}) collective-permute-start(f32[8,32,128]{2,1,0:T(8,128)S(1)} %fusion.3.mine_ref), channel_id=1, source_target_pairs={{0,1},{1,2},{2,3},{3,0},{4,5},{5,6},{6,7},{7,4},{8,9},{9,10},{10,1... | collective-permute-start | bytes 393224 | tf_op jit(solution)/shard_map/ppermute | solution.py:265
  35.0 6.3 %collective-permute-start.8 = (f32[8,32,128]{2,1,0:T(8,128)S(1)}, f32[8,32,128]{2,1,0:T(8,128)S(1)}, u32[]{:S(2)}, u32[]{:S(2)}) collective-permute-start(f32[8,32,128]{2,1,0:T(8,128)S(1)} %fusion.3.mine_ref), channel_id=1, source_target_pairs={{0,2},{1,3},{2,0},{3,1},{4,6},{5,7},{6,4},{7,5},{8,10},{9,11},{10,... | collective-permute-start | bytes 393224 | tf_op jit(solution)/shard_map/ppermute | solution.py:265
  37.5 4.1 %collective-permute-start.9 = (f32[8,32,128]{2,1,0:T(8,128)S(1)}, f32[8,32,128]{2,1,0:T(8,128)S(1)}, u32[]{:S(2)}, u32[]{:S(2)}) collective-permute-start(f32[8,32,128]{2,1,0:T(8,128)S(1)} %fusion.3.mine_ref), channel_id=1, source_target_pairs={{0,3},{1,0},{2,1},{3,2},{4,7},{5,4},{6,5},{7,6},{8,11},{9,8},{10,9... | collective-permute-start | bytes 393224 | tf_op jit(solution)/shard_map/ppermute | solution.py:265
  42.5 5.0 %collective-permute-start.10 = (f32[64,128]{1,0:T(8,128)S(1)}, f32[64,128]{1,0:T(8,128)S(1)}, u32[]{:S(2)}, u32[]{:S(2)}) collective-permute-start(f32[64,128]{1,0:T(8,128)S(1)} %get-tuple-element.17), channel_id=1, source_target_pairs={{0,4},{4,0},{1,5},{5,1},{2,6},{6,2},{3,7},{7,3},{8,12},{12,8},{9,1... | collective-permute-start | bytes 98312 | tf_op jit(solution)/shard_map/ppermute | solution.py:274
  47.4 4.4 %collective-permute-start.11 = (f32[64,128]{1,0:T(8,128)S(1)}, f32[64,128]{1,0:T(8,128)S(1)}, u32[]{:S(2)}, u32[]{:S(2)}) collective-permute-start(f32[64,128]{1,0:T(8,128)S(1)} %add.45), channel_id=1, source_target_pairs={{0,16},{8,24},{16,0},{24,8},{1,17},{9,25},{17,1},{25,9},{2,18},{10... | collective-permute-start | bytes 98312 | tf_op jit(solution)/shard_map/ppermute | solution.py:30
  49.2 4.0 %collective-permute-start.12 = (f32[64,128]{1,0:T(8,128)S(1)}, f32[64,128]{1,0:T(8,128)S(1)}, u32[]{:S(2)}, u32[]{:S(2)}) collective-permute-start(f32[64,128]{1,0:T(8,128)S(1)} %add.45), channel_id=1, source_target_pairs={{0,8},{8,16},{16,24},{24,0},{1,9},{9,17},{17,25},{25,1},{2,10},{10... | collective-permute-start | bytes 98312 | tf_op jit(solution)/shard_map/ppermute | solution.py:30
  50.4 2.8 %collective-permute-start.13 = (f32[64,128]{1,0:T(8,128)S(1)}, f32[64,128]{1,0:T(8,128)S(1)}, u32[]{:S(2)}, u32[]{:S(2)}) collective-permute-start(f32[64,128]{1,0:T(8,128)S(1)} %add.45), channel_id=1, source_target_pairs={{0,24},{8,0},{16,8},{24,16},{1,25},{9,1},{17,9},{25,17},{2,26},{10... | collective-permute-start | bytes 98312 | tf_op jit(solution)/shard_map/ppermute | solution.py:30
  53.2 4.3 %collective-permute-start.14 = (f32[64,128]{1,0:T(8,128)S(1)}, f32[64,128]{1,0:T(8,128)S(1)}, u32[]{:S(2)}, u32[]{:S(2)}) collective-permute-start(f32[64,128]{1,0:T(8,128)S(1)} %add_add_fusion.1), channel_id=1, source_target_pairs={{0,64},{32,96},{64,0},{96,32},{1,65},{33,97},{65,1},{97,33},{2,66}... | collective-permute-start | bytes 98312 | tf_op jit(solution)/shard_map/ppermute | solution.py:30
  54.8 4.0 %collective-permute-start.15 = (f32[64,128]{1,0:T(8,128)S(1)}, f32[64,128]{1,0:T(8,128)S(1)}, u32[]{:S(2)}, u32[]{:S(2)}) collective-permute-start(f32[64,128]{1,0:T(8,128)S(1)} %add_add_fusion.1), channel_id=1, source_target_pairs={{0,32},{32,64},{64,96},{96,0},{1,33},{33,65},{65,97},{97,1},{2,34}... | collective-permute-start | bytes 98312 | tf_op jit(solution)/shard_map/ppermute | solution.py:30
  56.8 3.1 %collective-permute-start.16 = (f32[64,128]{1,0:T(8,128)S(1)}, f32[64,128]{1,0:T(8,128)S(1)}, u32[]{:S(2)}, u32[]{:S(2)}) collective-permute-start(f32[64,128]{1,0:T(8,128)S(1)} %add_add_fusion.1), channel_id=1, source_target_pairs={{0,96},{32,0},{64,32},{96,64},{1,97},{33,1},{65,33},{97,65},{2,98}... | collective-permute-start | bytes 98312 | tf_op jit(solution)/shard_map/ppermute | solution.py:30

commit v9 on v8

--- a/solution.py
+++ b/solution.py
@@ -74,8 +74,8 @@
 
 def x_kernel(factor_ref, factor_y_ref, field_ref, keep_ref, send_ref, held, held_x, held_y, arrived, small):
     copies = [
-        pltpu.make_async_copy(field_ref.at[4 * i:4 * i + 4], held.at[4 * i:4 * i + 4], arrived.at[i])
-        for i in range(2)
+        pltpu.make_async_copy(field_ref.at[low:high], held.at[low:high], arrived.at[i])
+        for i, (low, high) in enumerate(((0, 3), (3, 8)))
     ]
     copy_x = pltpu.make_async_copy(factor_ref, held_x, small.at[0])
     copy_y = pltpu.make_async_copy(factor_y_ref, held_y, small.at[1])
@@ -88,8 +88,8 @@
     send_ref[64, :, 0:64] = held_y[...]
     send_ref[64, :, 64:128] = held_y[...]
     for v in range(8):
-        if v % 4 == 0:
-            copies[v // 4].wait()
+        if v in (0, 3):
+            copies[v // 3].wait()
         tile = jnp.concatenate(
             [held[v, :, 8 * t:8 * t + 8, :].reshape(256, 128) for t in range(4)], axis=1
         )

time: 80.8 us -> 80.6 us (level)
  no operation moved by 1% of the time
where the time goes in v9:
time: 80.6 us; the launch traced here: 80.5 us
  starting transfers between devices  31.2 us (39%)
  waiting for transfers between devices  22.1 us (27%)
  blocking collectives  16.5 us (20%)
  Pallas kernels  9.51 us (12%)
    all_to_all x1, blocking collectives, per_device(): grams = lax.all_to_all(grams, ('z', 'y', 'c'), 0, 0, tiled=True)  16.5 us
    ppermute x6, waiting for transfers between devices, gather_sum(): lax.ppermute(slots[k], ('z', 'y', 'c'), hops(k, first))  12.7 us
    ppermute x6, starting transfers between devices, gather_sum(): lax.ppermute(slots[k], ('z', 'y', 'c'), hops(k, first))  12 us
    ppermute x6, starting transfers between devices, sum_all(): lax.ppermute(value, axis, [(i, (i + k) % 4) for i in range(4)])  8.69 us
    ppermute x3, starting transfers between devices, per_device(): lax.ppermute(mine, 'x', [(i, (i + k) % 4) for i in range(4)])  4.89 us
    ppermute x1, starting transfers between devices, per_device(): raw = raw + lax.ppermute(raw, 'c', swap)  4.11 us
    ppermute x6, waiting for transfers between devices, sum_all(): lax.ppermute(value, axis, [(i, (i + k) % 4) for i in range(4)])  3.71 us
    pallas_call x1, Pallas kernels, per_device(): pl.pallas_call(x_kernel, in_specs=[pl.BlockSpec(memory_space=pltpu.HBM)]...  3.1 us
  transfers between devices with their start and end apart: 17, of which 13 were waited for; matrix products, arithmetic and copies ran while one was open for 0% of the time, Pallas kernels for 1%

profile of v9, /device:TPU:1, one launch (start us, length us, event | category | flops | bytes accessed | tf_op | source)
XLA Modules:
  0.0 80.5 jit_solution(13462193214466423787)
XLA Ops:
  0.6 0.0 copy-start
  0.6 3.1 %shard_map.76 = (f32[8,8,32,128]{3,2,1,0:T(8,128)S(1)}, f32[65,32,128]{2,1,0:T(8,128)S(1)}) custom-call(f32[16,32]{1,0:T(8,128)} %bitcast.31, f32[32,64]{1,0:T(8,128)} %mine_ref.1, f32[8,32,32,128]{3,2,1,0:T(8,128)} %field_ref.1), custom_call_target="tpu_custom_call" | custom-call | tf_op jit(solution)/shard_map/pallas_call | solution.py:233
  3.7 1.5 %collective-permute-start = (f32[65,32,128]{2,1,0:T(8,128)S(1)}, f32[65,32,128]{2,1,0:T(8,128)S(1)}, u32[]{:S(2)}, u32[]{:S(2)}) collective-permute-start(f32[65,32,128]{2,1,0:T(8,128)S(1)} %get-tuple-element.15), channel_id=1, source_target_pairs={{0,4},{4,0},{1,5},{5,1},{2,6},{6,2},{3,7},{7,3},{8,12},{12,8},{9,1... | collective-permute-start | bytes 3194888 | tf_op jit(solution)/shard_map/ppermute | solution.py:247
  5.2 2.3 %collective-permute-done.got_ref = f32[65,32,128]{2,1,0:T(8,128)S(1)} collective-permute-done((f32[65,32,128]{2,1,0:T(8,128)S(1)}, f32[65,32,128]{2,1,0:T(8,128)S(1)}, u32[]{:S(2)}, u32[]{:S(2)}) %collective-permute-start) | collective-permute-done | bytes 1064992 | tf_op jit(solution)/shard_map/ppermute | solution.py:247
  7.6 0.0 copy-done
  7.6 0.8 %shard_map.77 = f32[4,4,8,32,128]{4,3,2,1,0:T(8,128)S(1)} custom-call(f32[32,64]{1,0:T(8,128)S(1)} %copy-done, f32[8,8,32,128]{3,2,1,0:T(8,128)S(1)} %get-tuple-element.14.keep_ref, f32[65,32,128]{2,1,0:T(8,128)S(1)} %collective-permute-done.got_ref), custom_call_target="tpu_custom_call" | custom-call | tf_op jit(solution)/shard_map/pallas_call | solution.py:256
  8.4 0.1 slice_bitcast_fusion
  8.5 0.0 copy-start.1
  8.5 3.8 %collective-permute-start.1 = (f32[4,8,32,128]{3,2,1,0:T(8,128)S(1)}, f32[4,8,32,128]{3,2,1,0:T(8,128)S(1)}, u32[]{:S(2)}, u32[]{:S(2)}) collective-permute-start(f32[4,8,32,128]{3,2,1,0:T(8,128)S(1)} %get-tuple-element.25), channel_id=1, source_target_pairs={{0,16},{4,68},{8,24},{12,76},{16,0},{20,84},{24,8},{28,92},{32,48}... | collective-permute-start | bytes 1572872 | tf_op jit(solution)/shard_map/ppermute | solution.py:24
  12.3 0.7 collective-permute-start.2
  13.0 0.0 copy-start.2
  13.0 1.9 %collective-permute-start.3 = (f32[4,8,32,128]{3,2,1,0:T(8,128)S(1)}, f32[4,8,32,128]{3,2,1,0:T(8,128)S(1)}, u32[]{:S(2)}, u32[]{:S(2)}) collective-permute-start(f32[4,8,32,128]{3,2,1,0:T(8,128)S(1)} %get-tuple-element.23), channel_id=1, source_target_pairs={{0,24},{4,100},{8,0},{12,108},{16,8},{20,116},{24,16},{28,124},{32... | collective-permute-start | bytes 1572872 | tf_op jit(solution)/shard_map/ppermute | solution.py:24
  15.0 4.2 %collective-permute-done.1 = f32[4,8,32,128]{3,2,1,0:T(8,128)S(1)} collective-permute-done((f32[4,8,32,128]{3,2,1,0:T(8,128)S(1)}, f32[4,8,32,128]{3,2,1,0:T(8,128)S(1)}, u32[]{:S(2)}, u32[]{:S(2)}) %collective-permute-start.1) | collective-permute-done | bytes 524320 | tf_op jit(solution)/shard_map/ppermute | solution.py:24
  19.2 5.6 %collective-permute-done.2 = f32[4,8,32,128]{3,2,1,0:T(8,128)S(1)} collective-permute-done((f32[4,8,32,128]{3,2,1,0:T(8,128)S(1)}, f32[4,8,32,128]{3,2,1,0:T(8,128)S(1)}, u32[]{:S(2)}, u32[]{:S(2)}) %collective-permute-start.2) | collective-permute-done | bytes 524320 | tf_op jit(solution)/shard_map/ppermute | solution.py:24
  24.8 0.6 collective-permute-done.3
  25.4 0.2 fusion.1
  25.6 2.9 %collective-permute-start.4 = (f32[8,32,128]{2,1,0:T(8,128)S(1)}, f32[8,32,128]{2,1,0:T(8,128)S(1)}, u32[]{:S(2)}, u32[]{:S(2)}) collective-permute-start(f32[8,32,128]{2,1,0:T(8,128)S(1)} %get-tuple-element.28), channel_id=1, source_target_pairs={{0,64},{4,20},{8,72},{12,28},{16,80},{20,4},{24,88},{28,12},{32,96... | collective-permute-start | bytes 393224 | tf_op jit(solution)/shard_map/ppermute | solution.py:24
  28.5 0.4 collective-permute-start.5
  28.9 2.3 %collective-permute-start.6 = (f32[8,32,128]{2,1,0:T(8,128)S(1)}, f32[8,32,128]{2,1,0:T(8,128)S(1)}, u32[]{:S(2)}, u32[]{:S(2)}) collective-permute-start(f32[8,32,128]{2,1,0:T(8,128)S(1)} %get-tuple-element.26), channel_id=1, source_target_pairs={{0,96},{4,28},{8,104},{12,4},{16,112},{20,12},{24,120},{28,20},{32... | collective-permute-start | bytes 393224 | tf_op jit(solution)/shard_map/ppermute | solution.py:24
  31.2 0.1 collective-permute-done.4
  31.3 2.2 %collective-permute-done.5 = f32[8,32,128]{2,1,0:T(8,128)S(1)} collective-permute-done((f32[8,32,128]{2,1,0:T(8,128)S(1)}, f32[8,32,128]{2,1,0:T(8,128)S(1)}, u32[]{:S(2)}, u32[]{:S(2)}) %collective-permute-start.5) | collective-permute-done | bytes 131104 | tf_op jit(solution)/shard_map/ppermute | solution.py:24
  33.5 0.0 collective-permute-done.6
  33.6 1.3 %collective-permute-start.7 = (f32[8,32,128]{2,1,0:T(8,128)S(1)}, f32[8,32,128]{2,1,0:T(8,128)S(1)}, u32[]{:S(2)}, u32[]{:S(2)}) collective-permute-start(f32[8,32,128]{2,1,0:T(8,128)S(1)} %fusion.3.mine_ref), channel_id=1, source_target_pairs={{0,1},{1,2},{2,3},{3,0},{4,5},{5,6},{6,7},{7,4},{8,9},{9,10},{10,1... | collective-permute-start | bytes 393224 | tf_op jit(solution)/shard_map/ppermute | solution.py:265
  34.9 2.5 %collective-permute-start.8 = (f32[8,32,128]{2,1,0:T(8,128)S(1)}, f32[8,32,128]{2,1,0:T(8,128)S(1)}, u32[]{:S(2)}, u32[]{:S(2)}) collective-permute-start(f32[8,32,128]{2,1,0:T(8,128)S(1)} %fusion.3.mine_ref), channel_id=1, source_target_pairs={{0,2},{1,3},{2,0},{3,1},{4,6},{5,7},{6,4},{7,5},{8,10},{9,11},{10,... | collective-permute-start | bytes 393224 | tf_op jit(solution)/shard_map/ppermute | solution.py:265
  37.3 1.2 %collective-permute-start.9 = (f32[8,32,128]{2,1,0:T(8,128)S(1)}, f32[8,32,128]{2,1,0:T(8,128)S(1)}, u32[]{:S(2)}, u32[]{:S(2)}) collective-permute-start(f32[8,32,128]{2,1,0:T(8,128)S(1)} %fusion.3.mine_ref), channel_id=1, source_target_pairs={{0,3},{1,0},{2,1},{3,2},{4,7},{5,4},{6,5},{7,6},{8,11},{9,8},{10,9... | collective-permute-start | bytes 393224 | tf_op jit(solution)/shard_map/ppermute | solution.py:265
  38.5 0.0 copy-done.1
  38.5 0.5 shard_map.78.spread_ref
  39.0 0.0 collective-permute-done.7.one_ref
  39.0 2.2 %collective-permute-done.8.two_ref = f32[8,32,128]{2,1,0:T(8,128)S(1)} collective-permute-done((f32[8,32,128]{2,1,0:T(8,128)S(1)}, f32[8,32,128]{2,1,0:T(8,128)S(1)}, u32[]{:S(2)}, u32[]{:S(2)}) %collective-permute-start.8) | collective-permute-done | bytes 131104 | tf_op jit(solution)/shard_map/ppermute | solution.py:265
  41.2 0.3 collective-permute-done.9.three_ref
  41.4 0.0 copy-done.2
  41.4 0.9 %shard_map.79 = (f32[64,128]{1,0:T(8,128)S(1)}, f32[4,8,32,128]{3,2,1,0:T(8,128)S(1)}) custom-call(f32[8,32,128]{2,1,0:T(8,128)S(1)} %fusion.3.mine_ref, f32[8,32,128]{2,1,0:T(8,128)S(1)} %collective-permute-done.7.one_ref, f32[8,32,128]{2,1,0:T(8,128)S(1)} %collective-permute-done.8.two_ref, f32[8,32,128]{2,1,0:T(8,128)S(1)} %collective-permute-done.9.three_ref, ...), custom_call_target="tpu_custom_call" | custom-call | tf_op jit(solution)/shard_map/pallas_call | solution.py:267
  42.3 4.1 %collective-permute-start.10 = (f32[64,128]{1,0:T(8,128)S(1)}, f32[64,128]{1,0:T(8,128)S(1)}, u32[]{:S(2)}, u32[]{:S(2)}) collective-permute-start(f32[64,128]{1,0:T(8,128)S(1)} %get-tuple-element.17), channel_id=1, source_target_pairs={{0,4},{4,0},{1,5},{5,1},{2,6},{6,2},{3,7},{7,3},{8,12},{12,8},{9,1... | collective-permute-start | bytes 98312 | tf_op jit(solution)/shard_map/ppermute | solution.py:274
  46.4 0.9 %collective-permute-done.10 = f32[64,128]{1,0:T(8,128)S(1)} collective-permute-done((f32[64,128]{1,0:T(8,128)S(1)}, f32[64,128]{1,0:T(8,128)S(1)}, u32[]{:S(2)}, u32[]{:S(2)}) %collective-permute-start.10) | collective-permute-done | bytes 32800 | tf_op jit(solution)/shard_map/ppermute | solution.py:274
  47.3 1.8 %collective-permute-start.11 = (f32[64,128]{1,0:T(8,128)S(1)}, f32[64,128]{1,0:T(8,128)S(1)}, u32[]{:S(2)}, u32[]{:S(2)}) collective-permute-start(f32[64,128]{1,0:T(8,128)S(1)} %add.45), channel_id=1, source_target_pairs={{0,16},{8,24},{16,0},{24,8},{1,17},{9,25},{17,1},{25,9},{2,18},{10... | collective-permute-start | bytes 98312 | tf_op jit(solution)/shard_map/ppermute | solution.py:30
  49.0 1.2 %collective-permute-start.12 = (f32[64,128]{1,0:T(8,128)S(1)}, f32[64,128]{1,0:T(8,128)S(1)}, u32[]{:S(2)}, u32[]{:S(2)}) collective-permute-start(f32[64,128]{1,0:T(8,128)S(1)} %add.45), channel_id=1, source_target_pairs={{0,8},{8,16},{16,24},{24,0},{1,9},{9,17},{17,25},{25,1},{2,10},{10... | collective-permute-start | bytes 98312 | tf_op jit(solution)/shard_map/ppermute | solution.py:30
  50.2 1.5 %collective-permute-start.13 = (f32[64,128]{1,0:T(8,128)S(1)}, f32[64,128]{1,0:T(8,128)S(1)}, u32[]{:S(2)}, u32[]{:S(2)}) collective-permute-start(f32[64,128]{1,0:T(8,128)S(1)} %add.45), channel_id=1, source_target_pairs={{0,24},{8,0},{16,8},{24,16},{1,25},{9,1},{17,9},{25,17},{2,26},{10... | collective-permute-start | bytes 98312 | tf_op jit(solution)/shard_map/ppermute | solution.py:30
  51.7 0.0 collective-permute-done.11
  51.7 1.3 %collective-permute-done.12 = f32[64,128]{1,0:T(8,128)S(1)} collective-permute-done((f32[64,128]{1,0:T(8,128)S(1)}, f32[64,128]{1,0:T(8,128)S(1)}, u32[]{:S(2)}, u32[]{:S(2)}) %collective-permute-start.12) | collective-permute-done | bytes 32800 | tf_op jit(solution)/shard_map/ppermute | solution.py:30
  53.0 0.0 collective-permute-done.13
  53.0 1.6 %collective-permute-start.14 = (f32[64,128]{1,0:T(8,128)S(1)}, f32[64,128]{1,0:T(8,128)S(1)}, u32[]{:S(2)}, u32[]{:S(2)}) collective-permute-start(f32[64,128]{1,0:T(8,128)S(1)} %add_add_fusion.1), channel_id=1, source_target_pairs={{0,64},{32,96},{64,0},{96,32},{1,65},{33,97},{65,1},{97,33},{2,66}... | collective-permute-start | bytes 98312 | tf_op jit(solution)/shard_map/ppermute | solution.py:30
  54.6 2.0 %collective-permute-start.15 = (f32[64,128]{1,0:T(8,128)S(1)}, f32[64,128]{1,0:T(8,128)S(1)}, u32[]{:S(2)}, u32[]{:S(2)}) collective-permute-start(f32[64,128]{1,0:T(8,128)S(1)} %add_add_fusion.1), channel_id=1, source_target_pairs={{0,32},{32,64},{64,96},{96,0},{1,33},{33,65},{65,97},{97,1},{2,34}... | collective-permute-start | bytes 98312 | tf_op jit(solution)/shard_map/ppermute | solution.py:30
  56.6 0.7 collective-permute-start.16
  57.3 0.1 collective-permute-done.14
  57.4 1.2 %collective-permute-done.15 = f32[64,128]{1,0:T(8,128)S(1)} collective-permute-done((f32[64,128]{1,0:T(8,128)S(1)}, f32[64,128]{1,0:T(8,128)S(1)}, u32[]{:S(2)}, u32[]{:S(2)}) %collective-permute-start.15) | collective-permute-done | bytes 32800 | tf_op jit(solution)/shard_map/ppermute | solution.py:30
  58.6 1.1 %collective-permute-done.16 = f32[64,128]{1,0:T(8,128)S(1)} collective-permute-done((f32[64,128]{1,0:T(8,128)S(1)}, f32[64,128]{1,0:T(8,128)S(1)}, u32[]{:S(2)}, u32[]{:S(2)}) %collective-permute-start.16) | collective-permute-done | bytes 32800 | tf_op jit(solution)/shard_map/ppermute | solution.py:30
  59.7 2.7 %shard_map.80 = (f32[128,128]{1,0:T(8,128)}, f32[32,8,128]{2,1,0:T(8,128)S(1)}) custom-call(f32[64,128]{1,0:T(8,128)S(1)} %add_add_fusion.rows_ref, f32[4,8,32,128]{3,2,1,0:T(8,128)S(1)} %get-tuple-element.18.block_ref), custom_call_target="tpu_custom_call" | custom-call | tf_op jit(solution)/shard_map/pallas_call | solution.py:276
  62.5 16.5 %all_to_all.5.grams_ref = f32[32,8,128]{2,1,0:T(8,128)S(1)} all-to-all(f32[32,8,128]{2,1,0:T(8,128)S(1)} %get-tuple-element.20), channel_id=1, replica_groups=mesh['z'=4,'y'=4,'c'=2,'x'=4] {'z','y','c'}, dimensions={0} | all-to-all | bytes 262144 | tf_op jit(solution)/shard_map/all_to_all | solution.py:283
  79.0 1.5 %shard_map.81 = (f32[32,32]{1,0:T(8,128)}, f32[1,1]{1,0:T(1,128)}) custom-call(f32[32,8,128]{2,1,0:T(8,128)S(1)} %all_to_all.5.grams_ref, f32[16,32]{1,0:T(8,128)S(1)} %bitcast.29), custom_call_target="tpu_custom_call" | custom-call | tf_op jit(solution)/shard_map/pallas_call | solution.py:284
  (5 shorter events, 0.1 us)
Async XLA Ops:
  0.6 6.9 %copy-start = (f32[32,64]{1,0:T(8,128)S(1)}, f32[32,64]{1,0:T(8,128)}, u32[]{:S(2)}) copy-start(f32[32,64]{1,0:T(8,128)} %mine_ref.1) | copy-start | bytes 24580
  3.7 3.8 %collective-permute-start = (f32[65,32,128]{2,1,0:T(8,128)S(1)}, f32[65,32,128]{2,1,0:T(8,128)S(1)}, u32[]{:S(2)}, u32[]{:S(2)}) collective-permute-start(f32[65,32,128]{2,1,0:T(8,128)S(1)} %get-tuple-element.15), channel_id=1, source_target_pairs={{0,4},{4,0},{1,5},{5,1},{2,6},{6,2},{3,7},{7,3},{8,12},{12,8},{9,1... | collective-permute-start | bytes 3194888 | tf_op jit(solution)/shard_map/ppermute | solution.py:247
  8.5 30.0 %copy-start.1 = (f32[32,16]{0,1:T(8,128)S(1)}, f32[32,16]{0,1:T(8,128)}, u32[]{:S(2)}) copy-start(f32[32,16]{0,1:T(8,128)} %param.9) | copy-start | bytes 6148
  8.5 10.7 %collective-permute-start.1 = (f32[4,8,32,128]{3,2,1,0:T(8,128)S(1)}, f32[4,8,32,128]{3,2,1,0:T(8,128)S(1)}, u32[]{:S(2)}, u32[]{:S(2)}) collective-permute-start(f32[4,8,32,128]{3,2,1,0:T(8,128)S(1)} %get-tuple-element.25), channel_id=1, source_target_pairs={{0,16},{4,68},{8,24},{12,76},{16,0},{20,84},{24,8},{28,92},{32,48}... | collective-permute-start | bytes 1572872 | tf_op jit(solution)/shard_map/ppermute | solution.py:24
  12.3 12.5 %collective-permute-start.2 = (f32[4,8,32,128]{3,2,1,0:T(8,128)S(1)}, f32[4,8,32,128]{3,2,1,0:T(8,128)S(1)}, u32[]{:S(2)}, u32[]{:S(2)}) collective-permute-start(f32[4,8,32,128]{3,2,1,0:T(8,128)S(1)} %get-tuple-element.24), channel_id=1, source_target_pairs={{0,8},{4,36},{8,16},{12,44},{16,24},{20,52},{24,0},{28,60},{32,40}... | collective-permute-start | bytes 1572872 | tf_op jit(solution)/shard_map/ppermute | solution.py:24
  13.0 28.4 %copy-start.2 = (f32[128,64]{0,1:T(8,128)S(1)}, f32[128,64]{0,1:T(8,128)}, u32[]{:S(2)}) copy-start(f32[128,64]{0,1:T(8,128)} %param.8) | copy-start | bytes 98308
  13.0 12.3 %collective-permute-start.3 = (f32[4,8,32,128]{3,2,1,0:T(8,128)S(1)}, f32[4,8,32,128]{3,2,1,0:T(8,128)S(1)}, u32[]{:S(2)}, u32[]{:S(2)}) collective-permute-start(f32[4,8,32,128]{3,2,1,0:T(8,128)S(1)} %get-tuple-element.23), channel_id=1, source_target_pairs={{0,24},{4,100},{8,0},{12,108},{16,8},{20,116},{24,16},{28,124},{32... | collective-permute-start | bytes 1572872 | tf_op jit(solution)/shard_map/ppermute | solution.py:24
  25.6 5.7 %collective-permute-start.4 = (f32[8,32,128]{2,1,0:T(8,128)S(1)}, f32[8,32,128]{2,1,0:T(8,128)S(1)}, u32[]{:S(2)}, u32[]{:S(2)}) collective-permute-start(f32[8,32,128]{2,1,0:T(8,128)S(1)} %get-tuple-element.28), channel_id=1, source_target_pairs={{0,64},{4,20},{8,72},{12,28},{16,80},{20,4},{24,88},{28,12},{32,96... | collective-permute-start | bytes 393224 | tf_op jit(solution)/shard_map/ppermute | solution.py:24
  28.5 5.0 %collective-permute-start.5 = (f32[8,32,128]{2,1,0:T(8,128)S(1)}, f32[8,32,128]{2,1,0:T(8,128)S(1)}, u32[]{:S(2)}, u32[]{:S(2)}) collective-permute-start(f32[8,32,128]{2,1,0:T(8,128)S(1)} %get-tuple-element.27), channel_id=1, source_target_pairs={{0,32},{4,12},{8,40},{12,20},{16,48},{20,28},{24,56},{28,4},{32,64... | collective-permute-start | bytes 393224 | tf_op jit(solution)/shard_map/ppermute | solution.py:24
  28.9 4.6 %collective-permute-start.6 = (f32[8,32,128]{2,1,0:T(8,128)S(1)}, f32[8,32,128]{2,1,0:T(8,128)S(1)}, u32[]{:S(2)}, u32[]{:S(2)}) collective-permute-start(f32[8,32,128]{2,1,0:T(8,128)S(1)} %get-tuple-element.26), channel_id=1, source_target_pairs={{0,96},{4,28},{8,104},{12,4},{16,112},{20,12},{24,120},{28,20},{32... | collective-permute-start | bytes 393224 | tf_op jit(solution)/shard_map/ppermute | solution.py:24
  33.6 5.4 %collective-permute-start.7 = (f32[8,32,128]{2,1,0:T(8,128)S(1)}, f32[8,32,128]{2,1,0:T(8,128)S(1)}, u32[]{:S(2)}, u32[]{:S(2)}) collective-permute-start(f32[8,32,128]{2,1,0:T(8,128)S(1)} %fusion.3.mine_ref), channel_id=1, source_target_pairs={{0,1},{1,2},{2,3},{3,0},{4,5},{5,6},{6,7},{7,4},{8,9},{9,10},{10,1... | collective-permute-start | bytes 393224 | tf_op jit(solution)/shard_map/ppermute | solution.py:265
  34.9 6.3 %collective-permute-start.8 = (f32[8,32,128]{2,1,0:T(8,128)S(1)}, f32[8,32,128]{2,1,0:T(8,128)S(1)}, u32[]{:S(2)}, u32[]{:S(2)}) collective-permute-start(f32[8,32,128]{2,1,0:T(8,128)S(1)} %fusion.3.mine_ref), channel_id=1, source_target_pairs={{0,2},{1,3},{2,0},{3,1},{4,6},{5,7},{6,4},{7,5},{8,10},{9,11},{10,... | collective-permute-start | bytes 393224 | tf_op jit(solution)/shard_map/ppermute | solution.py:265
  37.3 4.1 %collective-permute-start.9 = (f32[8,32,128]{2,1,0:T(8,128)S(1)}, f32[8,32,128]{2,1,0:T(8,128)S(1)}, u32[]{:S(2)}, u32[]{:S(2)}) collective-permute-start(f32[8,32,128]{2,1,0:T(8,128)S(1)} %fusion.3.mine_ref), channel_id=1, source_target_pairs={{0,3},{1,0},{2,1},{3,2},{4,7},{5,4},{6,5},{7,6},{8,11},{9,8},{10,9... | collective-permute-start | bytes 393224 | tf_op jit(solution)/shard_map/ppermute | solution.py:265
  42.3 5.0 %collective-permute-start.10 = (f32[64,128]{1,0:T(8,128)S(1)}, f32[64,128]{1,0:T(8,128)S(1)}, u32[]{:S(2)}, u32[]{:S(2)}) collective-permute-start(f32[64,128]{1,0:T(8,128)S(1)} %get-tuple-element.17), channel_id=1, source_target_pairs={{0,4},{4,0},{1,5},{5,1},{2,6},{6,2},{3,7},{7,3},{8,12},{12,8},{9,1... | collective-permute-start | bytes 98312 | tf_op jit(solution)/shard_map/ppermute | solution.py:274
  47.3 4.4 %collective-permute-start.11 = (f32[64,128]{1,0:T(8,128)S(1)}, f32[64,128]{1,0:T(8,128)S(1)}, u32[]{:S(2)}, u32[]{:S(2)}) collective-permute-start(f32[64,128]{1,0:T(8,128)S(1)} %add.45), channel_id=1, source_target_pairs={{0,16},{8,24},{16,0},{24,8},{1,17},{9,25},{17,1},{25,9},{2,18},{10... | collective-permute-start | bytes 98312 | tf_op jit(solution)/shard_map/ppermute | solution.py:30
  49.0 4.0 %collective-permute-start.12 = (f32[64,128]{1,0:T(8,128)S(1)}, f32[64,128]{1,0:T(8,128)S(1)}, u32[]{:S(2)}, u32[]{:S(2)}) collective-permute-start(f32[64,128]{1,0:T(8,128)S(1)} %add.45), channel_id=1, source_target_pairs={{0,8},{8,16},{16,24},{24,0},{1,9},{9,17},{17,25},{25,1},{2,10},{10... | collective-permute-start | bytes 98312 | tf_op jit(solution)/shard_map/ppermute | solution.py:30
  50.2 2.8 %collective-permute-start.13 = (f32[64,128]{1,0:T(8,128)S(1)}, f32[64,128]{1,0:T(8,128)S(1)}, u32[]{:S(2)}, u32[]{:S(2)}) collective-permute-start(f32[64,128]{1,0:T(8,128)S(1)} %add.45), channel_id=1, source_target_pairs={{0,24},{8,0},{16,8},{24,16},{1,25},{9,1},{17,9},{25,17},{2,26},{10... | collective-permute-start | bytes 98312 | tf_op jit(solution)/shard_map/ppermute | solution.py:30
  53.0 4.3 %collective-permute-start.14 = (f32[64,128]{1,0:T(8,128)S(1)}, f32[64,128]{1,0:T(8,128)S(1)}, u32[]{:S(2)}, u32[]{:S(2)}) collective-permute-start(f32[64,128]{1,0:T(8,128)S(1)} %add_add_fusion.1), channel_id=1, source_target_pairs={{0,64},{32,96},{64,0},{96,32},{1,65},{33,97},{65,1},{97,33},{2,66}... | collective-permute-start | bytes 98312 | tf_op jit(solution)/shard_map/ppermute | solution.py:30
  54.6 4.0 %collective-permute-start.15 = (f32[64,128]{1,0:T(8,128)S(1)}, f32[64,128]{1,0:T(8,128)S(1)}, u32[]{:S(2)}, u32[]{:S(2)}) collective-permute-start(f32[64,128]{1,0:T(8,128)S(1)} %add_add_fusion.1), channel_id=1, source_target_pairs={{0,32},{32,64},{64,96},{96,0},{1,33},{33,65},{65,97},{97,1},{2,34}... | collective-permute-start | bytes 98312 | tf_op jit(solution)/shard_map/ppermute | solution.py:30
  56.6 3.1 %collective-permute-start.16 = (f32[64,128]{1,0:T(8,128)S(1)}, f32[64,128]{1,0:T(8,128)S(1)}, u32[]{:S(2)}, u32[]{:S(2)}) collective-permute-start(f32[64,128]{1,0:T(8,128)S(1)} %add_add_fusion.1), channel_id=1, source_target_pairs={{0,96},{32,0},{64,32},{96,64},{1,97},{33,1},{65,33},{97,65},{2,98}... | collective-permute-start | bytes 98312 | tf_op jit(solution)/shard_map/ppermute | solution.py:30
